TPU v7x, 256 devices: a whole 4x4x8 slice. The times are simulated.
256 devices in a mesh: inner: 4 (over x_hi, core), outer: 64 (over y, z, x_lo).
Axes of the slice: x: 4 (x_hi: 2, x_lo: 2; x = x_hi * 2 + x_lo), y: 4, z: 8, core: 2. Of those that a mesh axis runs over, the one named last changes fastest.
Arguments:
- q_nope: bfloat16 [16384, 1024], P(('inner', 'outer')), may hold values from -6 to 6
- q_rope: bfloat16 [16384, 512], P(('inner', 'outer')), may hold values from -48 to 48
- kv_compressed: bfloat16 [16384, 576], P(('inner', 'outer')), may hold values from -16 to 16
- token_pos: int32 [16384], P(('inner', 'outer')), may hold values from 0 to 16383, as said below
- kv_gain: float32 [512], replicated, may hold values from 0.25 to 1.75
- w_uk: bfloat16 [8, 128, 512], replicated, may hold values from -0.5 to 0.5
- w_uv: bfloat16 [8, 512, 128], replicated, may hold values from -0.25 to 0.25
Outputs:
- attn_out: bfloat16 [16384, 1024], P(('inner', 'outer'))
Inputs may be any that keep to these rules, and one draw needn't show every extreme that they name: `token_pos`: every position 0 to 16383 occurs once; each device's 64 rows are two runs of 32 consecutive increasing positions, span c and span 2 * 256 - 1 - c of the sequence's spans of 32 positions, c differing between devices.
All inputs are finite; a program needn't handle non-finite values.
Results may differ from a plain program's by a relative error of at most 0.012.
The roundings to bfloat16 on the way count: a program that leaves them out, or rounds other values in their place, can miss the bound.
Values may be sent and summed in bfloat16 or wider, within the bound.
No kernel may reach another device: no remote copies, remote signals or barrier semaphores. Data moves between devices by JAX's collectives and lax.ppermute only.
A program may use at most 192 MiB of HBM per device.

v0:
```python
import math

import jax
import jax.numpy as jnp
from jax import lax
from jax.sharding import Mesh
from jax.sharding import PartitionSpec as P

INNER_OUTER = ("inner_0", "inner_1", "outer_0", "outer_1", "outer_2")


NEGATIVE = -1e30


def piece_ends(length, count):
    hop = length // count
    if hop >= 8:
        hop -= hop % 8
    return [hop * k for k in range(1, count)]


def stacked_from(shard, axes, sequence):
    blocks = shard
    for k in sequence:
        blocks = lax.all_gather(blocks, axes[k])
    done = sequence[::-1]
    back = [done.index(k) for k in range(len(axes))]
    blocks = blocks.transpose(*back, *range(len(axes), blocks.ndim))
    return blocks.reshape(-1, *shard.shape)


def laid_out(blocks, dim):
    blocks = jnp.moveaxis(blocks, 0, dim)
    lengths = blocks.shape
    return blocks.reshape(*lengths[:dim], lengths[dim] * lengths[dim + 1], *lengths[dim + 2 :])


def spread_gather(shard, axes, dim):
    widest = max(range(max(1, shard.ndim - 1)), key=lambda d: shard.shape[d])
    count, finished = (len(axes), [])
    for first, section in enumerate(
        jnp.split(shard, piece_ends(shard.shape[widest], count), axis=widest)
    ):
        if section.size:
            sequence = [(first - k) % count for k in range(count)]
            finished.append(stacked_from(section, axes, sequence))
    return laid_out(jnp.concatenate(finished, axis=widest + 1), dim)


def rotate(values, positions):
    half = values.shape[-1] // 2
    freqs = 10000.0 ** (-jnp.arange(half, dtype=jnp.float32) / half)
    angle = positions.astype(jnp.float32)[:, None] * freqs[None, :]
    cosine = jnp.cos(angle)[:, None, :]
    sine = jnp.sin(angle)[:, None, :]
    first = values[..., :half]
    second = values[..., half:]
    return jnp.concatenate(
        [first * cosine - second * sine, second * cosine + first * sine], axis=-1
    )


def body(q_nope, q_rope, kv_compressed, token_pos, kv_gain, w_uk, w_uv):
    heads = w_uk.shape[0]
    d_latent = kv_gain.shape[0]
    d_nope = w_uk.shape[1]
    d_rope = kv_compressed.shape[1] - d_latent
    count = q_nope.shape[0]
    comp = kv_compressed.astype(jnp.float32)
    raw_latent = comp[:, :d_latent]
    mean_sq = jnp.mean(raw_latent * raw_latent, axis=1, keepdims=True)
    latent = (raw_latent * lax.rsqrt(mean_sq + 1e-06) * kv_gain[None, :]).astype(jnp.bfloat16)
    k_roped = rotate(comp[:, None, d_latent:], token_pos)[:, 0, :].astype(jnp.bfloat16)
    key_rows = jnp.concatenate([latent, k_roped], axis=1)
    q_roped = rotate(q_rope.astype(jnp.float32).reshape(count, heads, d_rope), token_pos).astype(
        jnp.bfloat16
    )
    q_absorbed = jnp.einsum(
        "thd,hde->the",
        q_nope.reshape(count, heads, d_nope),
        w_uk,
        preferred_element_type=jnp.float32,
    ).astype(jnp.bfloat16)
    queries = jnp.concatenate([q_absorbed, q_roped], axis=2)
    scale = 1.0 / math.sqrt(d_nope + d_rope)
    peak = jnp.full((heads, count), NEGATIVE, jnp.float32)
    keys = spread_gather(key_rows, INNER_OUTER, 0)
    key_pos = spread_gather(token_pos, INNER_OUTER, 0)
    score = jnp.einsum("thd,ud->htu", queries, keys, preferred_element_type=jnp.float32) * scale
    visible = (key_pos[None, :] <= token_pos[:, None])[None, :, :]
    piece_peak = jnp.max(jnp.where(visible, score, NEGATIVE), axis=2)
    new_peak = jnp.maximum(peak, piece_peak)
    expd = jnp.where(visible, jnp.exp(score - new_peak[:, :, None]), 0.0)
    total = jnp.sum(expd, axis=2)
    weight = expd.astype(jnp.bfloat16)
    added = jnp.einsum(
        "htu,ud->htd", weight, keys[:, :d_latent], preferred_element_type=jnp.float32
    )
    summed = added
    peak, total, summed = (new_peak, total, summed)
    o_latent = (summed / total[:, :, None]).astype(jnp.bfloat16)
    result = jnp.einsum("htd,hde->the", o_latent, w_uv, preferred_element_type=jnp.float32)
    return result.reshape(count, -1).astype(jnp.bfloat16)


def solution(mesh):
    finer = Mesh(
        mesh.devices.reshape(2, 2, 4, 8, 2), ("inner_0", "inner_1", "outer_0", "outer_1", "outer_2")
    )
    in_specs = (
        P(INNER_OUTER, None),
        P(INNER_OUTER, None),
        P(INNER_OUTER, None),
        P(INNER_OUTER),
        P(),
        P(),
        P(),
    )
    out_specs = P(INNER_OUTER, None)
    return jax.shard_map(body, mesh=finer, in_specs=in_specs, out_specs=out_specs, check_vma=False)
```

profile of v0, /device:TPU:1, one launch (start us, length us, event | category | flops | bytes accessed | tf_op | source)
XLA Modules:
  0.0 556.7 jit_solution(8283473964513010630)
XLA Ops:
  6.7 1.2 copy.143
  8.0 0.7 convert_element_type.39
  8.8 0.8 multiply_convert_fusion
  9.9 4.1 all-gather.45
  14.0 26.1 %all-gather.46 = bf16[16,32,576]{2,1,0:T(8,128)(2,1)} all-gather(bf16[2,32,576]{2,1,0:T(8,128)(2,1)S(1)} %bitcast.148), channel_id=48, replica_groups=mesh['inner_0'=2,'inner_1'=2,'outer_0'=4,'outer_1'=8,'outer_2'=2] {'oute..., dimensions={0}, use_global_device_ids=true | all-gather | bytes 663552 | tf_op jit(solution)/shard_map/all_gather | solution.py:25
  40.4 18.7 %all-gather.40 = bf16[64,576]{1,0:T(8,128)(2,1)S(1)} all-gather(bf16[8,576]{1,0:T(8,128)(2,1)S(1)} %copy.150), channel_id=42, replica_groups=mesh['inner_0'=2,'inner_1'=2,'outer_0'=4,'outer_1'=8,'outer_2'=2] {'oute..., dimensions={0}, use_global_device_ids=true | all-gather | bytes 82944 | tf_op jit(solution)/shard_map/all_gather | solution.py:25
  59.0 12.2 %all-gather.41 = bf16[32,8,576]{2,1,0:T(8,128)(2,1)S(1)} all-gather(bf16[8,8,576]{2,1,0:T(8,128)(2,1)S(1)} %bitcast.146), channel_id=43, replica_groups=mesh['inner_0'=2,'inner_1'=2,'outer_0'=4,'outer_1'=8,'outer_2'=2] {'oute..., dimensions={0}, use_global_device_ids=true | all-gather | bytes 368640 | tf_op jit(solution)/shard_map/all_gather | solution.py:25
  71.3 17.4 %all-gather.42 = bf16[8,8,8,576]{3,2,1,0:T(8,128)(2,1)} all-gather(bf16[4,8,8,576]{3,2,1,0:T(8,128)(2,1)S(1)} %bitcast.135), channel_id=44, replica_groups=mesh['inner_0'=2,'inner_1'=2,'outer_0'=4,'outer_1'=8,'outer_2'=2] {'inne..., dimensions={0}, use_global_device_ids=true | all-gather | bytes 884736 | tf_op jit(solution)/shard_map/all_gather | solution.py:25
  88.9 4.8 all-gather.25
  93.7 3.3 all-gather.26
  97.0 22.1 %all-gather.27 = bf16[16,2,8,576]{3,2,1,0:T(8,128)(2,1)} all-gather(bf16[2,2,8,576]{3,2,1,0:T(8,128)(2,1)S(1)} %bitcast.155), channel_id=29, replica_groups=mesh['inner_0'=2,'inner_1'=2,'outer_0'=4,'outer_1'=8,'outer_2'=2] {'oute..., dimensions={0}, use_global_device_ids=true | all-gather | bytes 331776 | tf_op jit(solution)/shard_map/all_gather | solution.py:25
  119.8 9.2 %all-gather.30 = bf16[16,576]{1,0:T(8,128)(2,1)S(1)} all-gather(bf16[8,576]{1,0:T(8,128)(2,1)S(1)} %copy.146), channel_id=32, replica_groups=mesh['inner_0'=2,'inner_1'=2,'outer_0'=4,'outer_1'=8,'outer_2'=2] {'inne..., dimensions={0}, use_global_device_ids=true | all-gather | bytes 27648 | tf_op jit(solution)/shard_map/all_gather | solution.py:25
  129.0 4.8 all-gather.31
  133.8 3.5 all-gather.32
  137.3 23.0 %all-gather.33 = bf16[16,2,2,8,576]{4,3,2,1,0:T(8,128)(2,1)} all-gather(bf16[2,2,2,8,576]{4,3,2,1,0:T(8,128)(2,1)S(1)} %bitcast.149), channel_id=35, replica_groups=mesh['inner_0'=2,'inner_1'=2,'outer_0'=4,'outer_1'=8,'outer_2'=2] {'oute..., dimensions={0}, use_global_device_ids=true | all-gather | bytes 663552 | tf_op jit(solution)/shard_map/all_gather | solution.py:25
  161.1 9.4 %all-gather.35 = bf16[32,576]{1,0:T(8,128)(2,1)S(1)} all-gather(bf16[8,576]{1,0:T(8,128)(2,1)S(1)} %copy.148), channel_id=37, replica_groups=mesh['inner_0'=2,'inner_1'=2,'outer_0'=4,'outer_1'=8,'outer_2'=2] {'oute..., dimensions={0}, use_global_device_ids=true | all-gather | bytes 46080 | tf_op jit(solution)/shard_map/all_gather | solution.py:25
  170.5 11.6 %all-gather.36 = bf16[8,8,576]{2,1,0:T(8,128)(2,1)S(1)} all-gather(bf16[4,8,576]{2,1,0:T(8,128)(2,1)S(1)} %bitcast.153), channel_id=38, replica_groups=mesh['inner_0'=2,'inner_1'=2,'outer_0'=4,'outer_1'=8,'outer_2'=2] {'inne..., dimensions={0}, use_global_device_ids=true | all-gather | bytes 110592 | tf_op jit(solution)/shard_map/all_gather | solution.py:25
  182.1 5.8 %all-gather.37 = bf16[4,4,8,576]{3,2,1,0:T(8,128)(2,1)S(1)} all-gather(bf16[2,4,8,576]{3,2,1,0:T(8,128)(2,1)S(1)} %bitcast.147), channel_id=39, replica_groups=mesh['inner_0'=2,'inner_1'=2,'outer_0'=4,'outer_1'=8,'outer_2'=2] {'inne..., dimensions={0}, use_global_device_ids=true | all-gather | bytes 221184 | tf_op jit(solution)/shard_map/all_gather | solution.py:25
  187.9 5.3 all-gather.38
  193.3 0.7 all-gather.66.cloned.1.call-update
  194.1 0.7 all-gather.80.cloned.1.call-update
  194.7 0.6 dynamic-slice.2
  195.4 0.6 dynamic-slice.3
  198.6 3.6 all-reduce.1
  203.6 4.7 all-reduce
  208.3 4.8 all-gather.51
  213.2 3.4 all-gather.50
  216.6 8.8 %all-reduce.3 = s32[64]{0:T(128)S(1)} all-reduce(s32[64]{0:T(128)S(1)} %get-tuple-element.17), channel_id=17, replica_groups=mesh['inner_0'=2,'inner_1'=2,'outer_0'=4,'outer_1'=8,'outer_2'=2] {'oute..., use_global_device_ids=true, to_apply=%add.3 | all-reduce | flops 64 | bytes 512
  225.4 9.2 %all-gather.16 = s32[32,8]{1,0:T(8,128)S(1)} all-gather(s32[8,8]{1,0:T(8,128)S(1)} %reshape.216), channel_id=18, replica_groups=mesh['inner_0'=2,'inner_1'=2,'outer_0'=4,'outer_1'=8,'outer_2'=2] {'oute..., dimensions={0}, use_global_device_ids=true | all-gather | bytes 1280 | tf_op jit(solution)/shard_map/all_gather | solution.py:25
  234.7 9.8 %all-gather.17 = s32[8,8,8]{2,1,0:T(8,128)S(1)} all-gather(s32[4,8,8]{2,1,0:T(8,128)S(1)} %bitcast.161), channel_id=19, replica_groups=mesh['inner_0'=2,'inner_1'=2,'outer_0'=4,'outer_1'=8,'outer_2'=2] {'inne..., dimensions={0}, use_global_device_ids=true | all-gather | bytes 3072 | tf_op jit(solution)/shard_map/all_gather | solution.py:25
  244.5 6.0 %all-gather.18 = s32[4,4,8,8]{3,2,1,0:T(8,128)S(1)} all-gather(s32[2,4,8,8]{3,2,1,0:T(8,128)S(1)} %bitcast.156), channel_id=20, replica_groups=mesh['inner_0'=2,'inner_1'=2,'outer_0'=4,'outer_1'=8,'outer_2'=2] {'inne..., dimensions={0}, use_global_device_ids=true | all-gather | bytes 6144 | tf_op jit(solution)/shard_map/all_gather | solution.py:25
  250.5 5.7 %all-gather.19 = s32[4,2,4,8,8]{4,3,2,1,0:T(8,128)S(1)} all-gather(s32[2,2,4,8,8]{4,3,2,1,0:T(8,128)S(1)} %bitcast.150), channel_id=21, replica_groups=mesh['inner_0'=2,'inner_1'=2,'outer_0'=4,'outer_1'=8,'outer_2'=2] {'oute..., dimensions={0}, use_global_device_ids=true | all-gather | bytes 12288 | tf_op jit(solution)/shard_map/all_gather | solution.py:25
  256.3 3.5 all-gather.7
  259.8 18.1 %all-gather.8 = s32[16,2,2,8]{3,2,1,0:T(2,128)S(1)} all-gather(s32[2,2,2,8]{3,2,1,0:T(2,128)S(1)} %bitcast.165), channel_id=10, replica_groups=mesh['inner_0'=2,'inner_1'=2,'outer_0'=4,'outer_1'=8,'outer_2'=2] {'oute..., dimensions={0}, use_global_device_ids=true | all-gather | bytes 2304 | tf_op jit(solution)/shard_map/all_gather | solution.py:25
  277.9 10.3 %all-gather.9 = s32[32,2,2,2,8]{4,3,2,1,0:T(2,128)S(1)} all-gather(s32[8,2,2,2,8]{4,3,2,1,0:T(2,128)S(1)} %bitcast.157), channel_id=11, replica_groups=mesh['inner_0'=2,'inner_1'=2,'outer_0'=4,'outer_1'=8,'outer_2'=2] {'oute..., dimensions={0}, use_global_device_ids=true | all-gather | bytes 10240 | tf_op jit(solution)/shard_map/all_gather | solution.py:25
  288.3 6.5 %all-reduce.2 = s32[32]{0:T(128)S(1)} all-reduce(s32[32]{0:T(128)S(1)} %get-tuple-element.18), channel_id=12, replica_groups=mesh['inner_0'=2,'inner_1'=2,'outer_0'=4,'outer_1'=8,'outer_2'=2] {'oute..., use_global_device_ids=true, to_apply=%add.2 | all-reduce | flops 32 | bytes 256
  294.8 13.4 %all-gather.52 = s32[2,4,8]{2,1,0:T(4,128)S(1)} all-gather(s32[1,4,8]{2,1,0:T(4,128)S(1)} %reshape.272), channel_id=13, replica_groups=mesh['inner_0'=2,'inner_1'=2,'outer_0'=4,'outer_1'=8,'outer_2'=2] {'inne..., dimensions={0}, use_global_device_ids=true | all-gather | bytes 384 | tf_op jit(solution)/shard_map/all_gather | solution.py:25
  308.3 4.7 all-gather.12
  313.0 3.2 all-gather.13
  316.2 18.2 %all-gather.14 = s32[16,2,2,4,8]{4,3,2,1,0:T(4,128)S(1)} all-gather(s32[2,2,2,4,8]{4,3,2,1,0:T(4,128)S(1)} %bitcast.162), channel_id=16, replica_groups=mesh['inner_0'=2,'inner_1'=2,'outer_0'=4,'outer_1'=8,'outer_2'=2] {'oute..., dimensions={0}, use_global_device_ids=true | all-gather | bytes 9216 | tf_op jit(solution)/shard_map/all_gather | solution.py:25
  334.4 15.9 %all-gather.2 = s32[16,2,8]{2,1,0:T(2,128)S(1)} all-gather(s32[2,2,8]{2,1,0:T(2,128)S(1)} %all-gather.50), channel_id=4, replica_groups=mesh['inner_0'=2,'inner_1'=2,'outer_0'=4,'outer_1'=8,'outer_2'=2] {'oute..., dimensions={0}, use_global_device_ids=true | all-gather | bytes 1152 | tf_op jit(solution)/shard_map/all_gather | solution.py:25
  350.3 10.2 %all-gather.3 = s32[32,2,2,8]{3,2,1,0:T(2,128)S(1)} all-gather(s32[8,2,2,8]{3,2,1,0:T(2,128)S(1)} %bitcast.163), channel_id=5, replica_groups=mesh['inner_0'=2,'inner_1'=2,'outer_0'=4,'outer_1'=8,'outer_2'=2] {'oute..., dimensions={0}, use_global_device_ids=true | all-gather | bytes 5120 | tf_op jit(solution)/shard_map/all_gather | solution.py:25
  360.5 18.0 %all-gather.4 = s32[8,8,2,2,8]{4,1,3,2,0:T(8,128)S(1)} all-gather(s32[4,8,2,2,8]{4,1,3,2,0:T(8,128)S(1)} %copy.136), channel_id=6, replica_groups=mesh['inner_0'=2,'inner_1'=2,'outer_0'=4,'outer_1'=8,'outer_2'=2] {'inne..., dimensions={0}, use_global_device_ids=true | all-gather | bytes 12288 | tf_op jit(solution)/shard_map/all_gather | solution.py:25
  378.6 0.6 dynamic-slice.4
  380.0 3.6 all-reduce.4
  383.6 12.1 %all-gather.53 = s32[8,2,32]{2,1,0:T(2,128)S(1)} all-gather(s32[1,2,32]{2,1,0:T(2,128)S(1)} %reshape.274), channel_id=23, replica_groups=mesh['inner_0'=2,'inner_1'=2,'outer_0'=4,'outer_1'=8,'outer_2'=2] {'oute..., dimensions={0}, use_global_device_ids=true | all-gather | bytes 2304 | tf_op jit(solution)/shard_map/all_gather | solution.py:25
  395.7 10.1 %all-gather.22 = s32[32,2,32]{2,1,0:T(2,128)S(1)} all-gather(s32[8,2,32]{2,1,0:T(2,128)S(1)} %all-gather.53), channel_id=24, replica_groups=mesh['inner_0'=2,'inner_1'=2,'outer_0'=4,'outer_1'=8,'outer_2'=2] {'oute..., dimensions={0}, use_global_device_ids=true | all-gather | bytes 10240 | tf_op jit(solution)/shard_map/all_gather | solution.py:25
  405.8 6.6 %all-gather.23 = s32[8,8,2,32]{3,1,2,0:T(8,128)S(1)} all-gather(s32[4,8,2,32]{3,1,2,0:T(8,128)S(1)} %copy.141), channel_id=25, replica_groups=mesh['inner_0'=2,'inner_1'=2,'outer_0'=4,'outer_1'=8,'outer_2'=2] {'inne..., dimensions={0}, use_global_device_ids=true | all-gather | bytes 24576 | tf_op jit(solution)/shard_map/all_gather | solution.py:25
  412.4 7.5 %all-gather.24 = s32[4,4,8,2,32]{4,2,3,1,0:T(8,128)S(1)} all-gather(s32[2,4,8,2,32]{4,2,3,1,0:T(8,128)S(1)} %bitcast.151), channel_id=26, replica_groups=mesh['inner_0'=2,'inner_1'=2,'outer_0'=4,'outer_1'=8,'outer_2'=2] {'inne..., dimensions={0}, use_global_device_ids=true | all-gather | bytes 49152 | tf_op jit(solution)/shard_map/all_gather | solution.py:25
  421.1 0.6 broadcast_compare_fusion
  421.8 3.6 copy.147
  425.3 3.5 copy.151
  428.9 3.6 copy.149
  432.5 2.3 copy.145
  434.8 1.8 constant_dynamic-update-slice_fusion.4
  436.6 3.5 constant_dynamic-update-slice_fusion.3
  440.1 3.6 constant_dynamic-update-slice_fusion.2
  443.7 1.8 constant_dynamic-update-slice_fusion.1
  445.5 21.3 %all-gather.80.cloned.1.call-done = bf16[4,4,8,2,32,576]{5,4,3,2,1,0:T(8,128)(2,1)} async-done(((bf16[2,4,8,2,32,576]{5,4,3,2,1,0:T(8,128)(2,1)}), bf16[4,4,8,2,32,576]{5,4,3,2,1,0:T(8,128)(2,1)}) %all-gather.80.cloned.1.call-update) | async-done | bytes 9437200 | tf_op jit(solution)/shard_map/all_gather | solution.py:25
  466.8 8.8 %constant_dynamic-update-slice_fusion = bf16[256,64,576]{2,1,0:T(8,128)(2,1)} fusion(bf16[256,64,576]{2,1,0:T(8,128)(2,1)} %constant_dynamic-update-slice_fusion.1, bf16[256,32,576]{2,1,0:T(8,128)(2,1)} %bitcast.117), kind=kLoop, calls=%fused_computation.55 | loop fusion | bytes 20971520 | tf_op jit(solution)/shard_map/concatenate | solution.py:47
  475.6 38.7 %fusion = (f32[8,64]{1,0:T(8,128)S(1)}, f32[16384,64,8]{0,1,2:T(8,128)}) fusion(pred[64,16384]{1,0:T(8,128)(4,1)S(1)} %broadcast_compare_fusion, bf16[16384,576,1]{1,0,2:T(8,128)(2,1)} %bitcast.65, bf16[64,8,32]{2,0,1:T(8,128)(2,1)S(1)} %get-tuple-element.6, bf16[64,8,32]{2,0,1:T(8,128)(2,1)S(1)} %get-tuple-element.5, bf16[64,8,512]{2,0,1:T(8,128)(2,1)S(1)} %fusion.11), kind=kOutput, calls=%fused_computation.2 | convolution fusion | flops 9690611712 | bytes 54069248 | tf_op jit(solution)/shard_map/thd,ud->htu/dot_general | solution.py:89
  514.3 15.4 %fusion.3 = f32[8,64]{1,0:T(8,128)S(1)} fusion(f32[16384,64,8]{0,1,2:T(8,128)} %get-tuple-element.21, f32[8,64]{1,0:T(8,128)S(1)} %broadcast_maximum_fusion, pred[64,16384]{1,0:T(8,128)(4,1)S(1)} %broadcast_compare_fusion), kind=kLoop, calls=%fused_computation.5 | loop fusion | flops 33553920 | bytes 34607104 | tf_op jit(solution)/shard_map/reduce_sum | solution.py:94
  529.7 19.4 %divide_convert_fusion = bf16[8,64,512]{2,1,0:T(8,128)(2,1)S(1)} fusion(bf16[16384,576]{1,0:T(8,128)(2,1)} %bitcast.64, f32[16384,64,8]{0,1,2:T(8,128)} %get-tuple-element.21, f32[8,64]{1,0:T(8,128)S(1)} %broadcast_maximum_fusion, pred[64,16384]{1,0:T(8,128)(4,1)S(1)} %broadcast_compare_fusion, f32[8,64]{1,0:T(8,128)S(1)} %fusion.3), kind=kOutput, calls=%fused_computation.18 | convolution fusion | flops 8624013312 | bytes 51908608 | tf_op jit(solution)/shard_map/htu,ud->htd/dot_general | solution.py:96
  549.5 0.7 copy.173
  (93 shorter events, 6.6 us)
Async XLA Ops:
  6.5 414.3 %copy-start = (bf16[8,128,512]{2,1,0:T(8,128)(2,1)S(1)}, bf16[8,128,512]{2,1,0:T(8,128)(2,1)}, u32[]{:S(2)}) copy-start(bf16[8,128,512]{2,1,0:T(8,128)(2,1)} %param.12) | copy-start | bytes 3145732
  6.5 188.2 %copy-start.11 = (u32[256]{0:T(256)S(1)}, u32[256]{0:T(256)}, u32[]{:S(2)}) copy-start(u32[256]{0:T(256)} %constant.35) | copy-start | bytes 3076
  6.5 188.8 %copy-start.10 = (u32[256]{0:T(256)S(1)}, u32[256]{0:T(256)}, u32[]{:S(2)}) copy-start(u32[256]{0:T(256)} %constant.40) | copy-start | bytes 3076
  6.5 190.7 %copy-start.9 = (u32[256]{0:T(256)S(1)}, u32[256]{0:T(256)}, u32[]{:S(2)}) copy-start(u32[256]{0:T(256)} %constant.30) | copy-start | bytes 3076
  6.5 195.7 %copy-start.8 = (u32[256]{0:T(256)S(1)}, u32[256]{0:T(256)}, u32[]{:S(2)}) copy-start(u32[256]{0:T(256)} %constant.25) | copy-start | bytes 3076
  6.6 372.0 %copy-start.7 = (u32[256]{0:T(256)S(1)}, u32[256]{0:T(256)}, u32[]{:S(2)}) copy-start(u32[256]{0:T(256)} %constant.45) | copy-start | bytes 3076
  6.6 191.8 %copy-start.6 = (s32[64]{0:T(128)S(1)}, s32[64]{0:T(128)}, u32[]{:S(2)}) copy-start(s32[64]{0:T(128)} %param.10) | copy-start | bytes 772
  6.6 413.7 %copy-start.5 = (bf16[64,512]{1,0:T(8,128)(2,1)S(1)}, bf16[64,512]{1,0:T(8,128)(2,1)}, u32[]{:S(2)}) copy-start(bf16[64,512]{1,0:T(8,128)(2,1)} %param.8) | copy-start | bytes 196612
  6.6 414.2 %copy-start.4 = (bf16[64,1024]{1,0:T(8,128)(2,1)S(1)}, bf16[64,1024]{1,0:T(8,128)(2,1)}, u32[]{:S(2)}) copy-start(bf16[64,1024]{1,0:T(8,128)(2,1)} %param.7) | copy-start | bytes 393220
  6.6 112.5 %all-gather.76.cloned.1.call-start = ((), (), s32[]{:S(2)}) async-start(), calls=%async_computation.6 | async-start | bytes 3276800 | tf_op jit(solution)/shard_map/all_gather | solution.py:25
  40.1 120.4 %all-gather.72.cloned.1.call-start = ((), (), s32[]{:S(2)}) async-start(), calls=%async_computation.4 | async-start | bytes 1966080 | tf_op jit(solution)/shard_map/all_gather | solution.py:25
  88.8 104.5 %all-gather.64.cloned.1.call-start = ((), (), s32[]{:S(2)}) async-start(), calls=%async_computation | async-start | bytes 1638400 | tf_op jit(solution)/shard_map/all_gather | solution.py:25
  119.0 75.0 %all-gather.78.cloned.1.call-start = ((), (), s32[]{:S(2)}) async-start(), calls=%async_computation.7 | async-start | bytes 7864320 | tf_op jit(solution)/shard_map/all_gather | solution.py:25
  119.6 302.1 %all-gather.68.cloned.1.call-start = ((), (), s32[]{:S(2)}) async-start(), calls=%async_computation.2 | async-start | bytes 3276800 | tf_op jit(solution)/shard_map/all_gather | solution.py:25
  160.3 265.0 %all-gather.74.cloned.1.call-start = ((), (), s32[]{:S(2)}) async-start(), calls=%async_computation.5 | async-start | bytes 3932160 | tf_op jit(solution)/shard_map/all_gather | solution.py:25
  160.9 268.0 %all-gather.70.cloned.1.call-start = ((), (), s32[]{:S(2)}) async-start(), calls=%async_computation.3 | async-start | bytes 2949120 | tf_op jit(solution)/shard_map/all_gather | solution.py:25
  193.2 239.3 %all-gather.66.cloned.1.call-start = ((), (), s32[]{:S(2)}) async-start(), calls=%async_computation.1 | async-start | bytes 3932160 | tf_op jit(solution)/shard_map/all_gather | solution.py:25
  194.0 272.8 %all-gather.80.cloned.1.call-start = ((), (), s32[]{:S(2)}) async-start(), calls=%async_computation.8 | async-start | bytes 15728640 | tf_op jit(solution)/shard_map/all_gather | solution.py:25
  432.5 11.2 %copy-start.2 = (bf16[2,2,4,8,2,8,576]{6,5,4,3,2,1,0:T(8,128)(2,1)S(1)}, bf16[2,2,4,8,2,8,576]{6,5,4,3,2,1,0:T(8,128)(2,1)}, u32[]{:S(2)}) copy-start(bf16[2,2,4,8,2,8,576]{6,5,4,3,2,1,0:T(8,128)(2,1)} %copy.151) | copy-start | bytes 7077892
  529.7 19.4 %copy-start.3 = (bf16[8,512,128]{2,1,0:T(8,128)(2,1)S(1)}, bf16[8,512,128]{2,1,0:T(8,128)(2,1)}, u32[]{:S(2)}) copy-start(bf16[8,512,128]{2,1,0:T(8,128)(2,1)} %param.13) | copy-start | bytes 3145732
  529.7 20.4 %copy-start.1 = (bf16[8,128,512]{2,1,0:T(8,128)(2,1)S(1)}, bf16[8,128,512]{2,1,0:T(8,128)(2,1)}, u32[]{:S(2)}) copy-start(bf16[8,128,512]{2,1,0:T(8,128)(2,1)} %param.12) | copy-start | bytes 3145732
Sparse Core Ops, SparseCore 0:
  40.2 46.5 all-gather.75
  88.9 30.1 all-gather.71
  120.9 30.0 all-gather.63
  152.6 23.0 all-gather.77
  177.3 38.3 all-gather.67
  217.4 46.3 all-gather.73
  265.5 40.4 all-gather.69
  307.8 18.9 all-gather.65
  328.6 138.1 all-gather.79
where the time goes:
time: 558 us; the launch traced here: 557 us
  blocking collectives  399 us (72%)
  matrix products  58.7 us (11%)
  local copies, waits for them, and re-layouts  39.7 us (7%)
  waiting for transfers between devices  23.8 us (4%)
  other arithmetic  18.4 us (3%)
  between operations  16.7 us (3%)
    all_gather x36, blocking collectives, stacked_from(): blocks = lax.all_gather(blocks, axes[k])  372 us
    dot_general x1, matrix products, body(): jnp.einsum('thd,ud->htu', queries, keys, preferred_element_type=jnp.float32)  38.7 us
    unnamed x5, blocking collectives  27.1 us
    all_gather x9, waiting for transfers between devices, stacked_from(): blocks = lax.all_gather(blocks, axes[k])  21.4 us
    dot_general x1, matrix products, body(): jnp.einsum('htu,ud->htd', weight, keys[:, :d_latent], preferred_element_t...  19.4 us
    unnamed x46, local copies, waits for them, and re-layouts  15.7 us
    reduce_sum x1, other arithmetic, body(): total = jnp.sum(expd, axis=2)  15.4 us
    transpose x5, local copies, waits for them, and re-layouts, stacked_from(): blocks = blocks.transpose(*back, *range(len(axes), blocks.ndim))  13.1 us
  transfers between devices with their start and end apart: 9, of which 1 were waited for; matrix products, arithmetic and copies ran while one was open for 5% of the time, Pallas kernels for 0%

commit v1 on v0

v1 whole, which is shorter than its diff:
```python
import functools
import math

import jax
import jax.numpy as jnp
import numpy as np
from jax import lax
from jax.experimental import pallas as pl
from jax.experimental.pallas import tpu as pltpu
from jax.sharding import Mesh
from jax.sharding import PartitionSpec as P

ALL_AXES = ("x_hi", "core", "y", "z", "x_lo")
ACROSS = ("x_hi", "x_lo")
X_SIZE, Y_SIZE, Z_SIZE = 4, 4, 8

RUN = 32
TOK = 2 * RUN
D_LAT = 512
HEADS = 8
D_NOPE = 128
D_VAL = 128
ROW = D_LAT + 128
Q_ROW = HEADS * D_NOPE + 512 + 128
OUT_ROW = HEADS * D_VAL + 128
Q_TILE = 2 * X_SIZE * RUN
SPANS = 512

NEGATIVE = -1e30
FLOOR = -1e28
LOG2E = 1.4426950408889634

VMEM = pl.BlockSpec(memory_space=pltpu.VMEM)
SMEM = pl.BlockSpec(memory_space=pltpu.SMEM)


def lanes(rows):
    return lax.broadcasted_iota(jnp.int32, (rows, 128), 1)


def turned(values, cosine, sine, first):
    partner = jnp.where(first, pltpu.roll(values, 96, 1), pltpu.roll(values, 32, 1))
    return values * cosine + partner * jnp.where(first, -sine, sine)


def rows_kernel(pos_ref, low_ref, high_ref, step_ref, qn_ref, qr_ref, kv_ref, gain_ref, key_ref, q_ref):
    lane = lanes(RUN)
    first = lane % 64 < 32
    slot = lax.axis_index("y") * Z_SIZE + lax.axis_index("z")
    turn = jnp.where(pos_ref[0] < pos_ref[RUN], 0, RUN)
    span = (jnp.minimum(pos_ref[0], pos_ref[RUN]) // RUN + 1).astype(jnp.float32)
    step_cos, step_sin = step_ref[0], step_ref[1]
    for half, base_ref in enumerate((low_ref, high_ref)):
        src = pl.ds(pl.multiple_of(turn if half == 0 else RUN - turn, RUN), RUN)
        dst = slice(half * RUN, (half + 1) * RUN)
        base_cos, base_sin = base_ref[0, 0:1], base_ref[0, 1:2]
        cosine = base_cos * step_cos - base_sin * step_sin
        sine = base_sin * step_cos + base_cos * step_sin

        raw = kv_ref[src, :D_LAT].astype(jnp.float32)
        mean_sq = jnp.mean(raw * raw, axis=1, keepdims=True)
        latent = raw * lax.rsqrt(mean_sq + 1e-06) * gain_ref[...]
        key_ref[dst, :D_LAT] = latent.astype(jnp.bfloat16)
        rope = kv_ref[src, D_LAT:].astype(jnp.float32)
        rope = turned(jnp.concatenate([rope, jnp.zeros_like(rope)], axis=1), cosine, sine, first)
        tail = jnp.where(lane == 64 + slot, span, 0.0)
        key_ref[dst, D_LAT:] = jnp.where(lane < 64, rope, tail).astype(jnp.bfloat16)

        q_ref[dst, : HEADS * D_NOPE] = qn_ref[src, :]
        for pair in range(HEADS // 2):
            part = qr_ref[src, pair * 128 : (pair + 1) * 128].astype(jnp.float32)
            at = HEADS * D_NOPE + pair * 128
            q_ref[dst, at : at + 128] = turned(part, cosine, sine, first).astype(jnp.bfloat16)
        q_ref[dst, Q_ROW - 128 :] = jnp.full((RUN, 128), span, jnp.float32).astype(jnp.bfloat16)


def rotations():
    freqs = np.tile(10000.0 ** (-np.arange(32) / 32.0), 4)
    table = lambda p: np.stack([np.cos(p[:, None] * freqs), np.sin(p[:, None] * freqs)], axis=1)
    spans = table(np.arange(SPANS) * float(RUN)).astype(np.float32)
    steps = table(np.arange(RUN) * 1.0).astype(np.float32).transpose(1, 0, 2)
    return spans, steps


def over_lanes(a, b):
    return lax.dot_general(a, b, (((1,), (1,)), ((), ())), preferred_element_type=jnp.float32)


def expand_kernel(n_keys, *refs):
    key_refs, (uk_ref, uv_ref, k_ref, v_ref, tail_ref) = refs[:n_keys], refs[n_keys:]
    for half in range(2):
        run = slice(half * RUN, (half + 1) * RUN)
        rows = [ref[:, run, :].reshape(-1, ROW) for ref in key_refs]
        rows = jnp.concatenate(rows, axis=0) if n_keys > 1 else rows[0]
        latent = rows[:, :D_LAT]
        tail_ref[half] = rows[:, D_LAT:]
        for pair in range(HEADS // 2):
            cols = slice(pair * 256, (pair + 1) * 256)
            k_ref[half, :, cols] = over_lanes(latent, uk_ref[cols, :]).astype(jnp.bfloat16)
            w = jnp.concatenate([uv_ref[2 * pair], uv_ref[2 * pair + 1]], axis=1)
            v_ref[half, :, cols] = jnp.dot(latent, w, preferred_element_type=jnp.float32).astype(jnp.bfloat16)


def expand(blocks, w_uk, w_uv):
    n = sum(b.shape[0] for b in blocks) * RUN
    out = lambda width: jax.ShapeDtypeStruct((2, n, width), jnp.bfloat16)
    return pl.pallas_call(
        functools.partial(expand_kernel, len(blocks)),
        in_specs=[VMEM] * (len(blocks) + 2),
        out_specs=[VMEM] * 3,
        out_shape=[out(HEADS * D_NOPE), out(HEADS * D_VAL), out(128)],
        compiler_params=pltpu.CompilerParams(vmem_limit_bytes=24 << 20),
        cost_estimate=pl.CostEstimate(
            flops=4 * n * D_LAT * 2048, bytes_accessed=n * 12000 + (2 << 20), transcendentals=0
        ),
        name="expand",
    )(*blocks, w_uk.reshape(HEADS * D_NOPE, D_LAT), w_uv)


def packed(stats):
    top = stats.astype(jnp.bfloat16)
    rest = stats - top.astype(jnp.float32)
    mid = rest.astype(jnp.bfloat16)
    rest = rest - mid.astype(jnp.float32)
    pieces = top.astype(jnp.float32) + pltpu.roll(mid.astype(jnp.float32), 8, 1)
    return (pieces + pltpu.roll(rest, 16, 1)).astype(jnp.bfloat16)


def unpacked(pieces):
    pieces = pieces.astype(jnp.float32)
    return pieces + pltpu.roll(pieces, 120, 1) + pltpu.roll(pieces, 112, 1)


def attend_kernel(n_chunks, scale, *refs):
    near_ref, far_ref = refs[:2]
    k_refs, v_refs, tail_refs = (refs[2 + i * n_chunks : 2 + (i + 1) * n_chunks] for i in range(3))
    outs, lse_scr = refs[2 + 3 * n_chunks : -1], refs[-1]
    step = pl.program_id(0)
    lane = lanes(RUN)
    q_refs = [(ref, i) for ref in (near_ref, far_ref) for i in range(X_SIZE)]
    q_at = pl.multiple_of(step * 256, 256)
    rope_at = pl.multiple_of(HEADS * D_NOPE + step * 128, 128)
    tails = [jnp.concatenate([ref[half] for ref in tail_refs], axis=0) for half in range(2)]
    spans = jnp.max(tails[0].astype(jnp.float32), axis=0, keepdims=True)
    first_keys = tail_refs[0].shape[1]
    shape = (Q_TILE, first_keys)
    row, col = (lax.broadcasted_iota(jnp.int32, shape, d) for d in (0, 1))
    later = (row < RUN) & (col < RUN) & (col > row)

    @pl.when(step == 0)
    def _():
        lse_scr[...] = jnp.zeros_like(lse_scr)

    for half in range(2):
        run = slice(half * RUN, (half + 1) * RUN)
        nope = jnp.concatenate([ref[i, run, pl.ds(q_at, 256)] for ref, i in q_refs], axis=0)
        ropes = [ref[i, run, pl.ds(rope_at, 128)].astype(jnp.float32) for ref, i in q_refs]
        biases = []
        for ref, i in q_refs:
            mine = ref[i, 0:16, Q_ROW - 128 :].astype(jnp.float32)[0:1]
            seen = (spans >= mine) if half else (spans <= mine)
            biases.append(jnp.where(seen, 0.0, NEGATIVE))
        for inner in range(2):
            cols = slice(inner * 128, (inner + 1) * 128)
            turned_by = [pltpu.roll(r, 64, 1) if inner else r for r in ropes]
            ends = lambda fill: jnp.concatenate(
                [jnp.where(lane < 64, r, f) for r, f in zip(turned_by, fill)], axis=0
            ).astype(jnp.bfloat16)
            masked = jnp.concatenate([nope[:, cols], ends(biases)], axis=1)
            keys = lambda run: jnp.concatenate(
                [jnp.concatenate([ref[run, :, cols] for ref in k_refs], axis=0), tails[run]], axis=1
            )
            values = lambda run: jnp.concatenate([ref[run, :, cols] for ref in v_refs], axis=0)
            score = over_lanes(masked, keys(half)) * scale
            head = jnp.where(later, NEGATIVE, score[:, :first_keys])
            parts = [(jnp.concatenate([head, score[:, first_keys:]], axis=1), half)]
            if half:
                plain = jnp.concatenate([nope[:, cols], ends([0.0] * len(q_refs))], axis=1)
                parts.append((over_lanes(plain, keys(0)) * scale, 0))
            peak = functools.reduce(jnp.maximum, [jnp.max(s, axis=1, keepdims=True) for s, _ in parts])
            peak = jnp.maximum(peak, FLOOR)
            total, added = None, None
            for s, run_of in parts:
                expd = jnp.exp2(s - peak)
                t = jnp.sum(expd, axis=1, keepdims=True)
                a = jnp.dot(expd.astype(jnp.bfloat16), values(run_of), preferred_element_type=jnp.float32)
                total = t if total is None else total + t
                added = a if added is None else added + a
            some = total > 0.0
            total = jnp.where(some, total, 1.0)
            result = (added / total).astype(jnp.bfloat16)
            lse = jnp.where(some, peak + jnp.log2(total), NEGATIVE)
            head_at = pl.multiple_of(step * 256 + inner * 128, 128)
            for i in range(2 * X_SIZE):
                rows = slice(i * RUN, (i + 1) * RUN)
                outs[i // X_SIZE][i % X_SIZE, run, pl.ds(head_at, 128)] = result[rows]
                lse_scr[i, run, :] = jnp.where(lane == 2 * step + inner, lse[rows], lse_scr[i, run, :])

    @pl.when(step == HEADS // 2 - 1)
    def _():
        for i in range(2 * X_SIZE):
            outs[i // X_SIZE][i % X_SIZE, :, HEADS * D_VAL :] = packed(lse_scr[i])


def attend(near, far, chunks, scale):
    whole = lambda shape: pl.BlockSpec(shape, lambda i: (0,) * len(shape))
    by_head = lambda a: pl.BlockSpec((2, a.shape[1], 256), lambda i: (0, 0, i))
    ks, vs, tails = zip(*chunks)
    out = jax.ShapeDtypeStruct((X_SIZE, TOK, OUT_ROW), jnp.bfloat16)
    return pl.pallas_call(
        functools.partial(attend_kernel, len(chunks), scale),
        grid=(HEADS // 2,),
        in_specs=[whole(near.shape), whole(far.shape)]
        + [by_head(a) for a in ks + vs]
        + [whole(a.shape) for a in tails],
        out_specs=[whole(out.shape)] * 2,
        out_shape=[out, out],
        scratch_shapes=[pltpu.VMEM((2 * X_SIZE, TOK, 128), jnp.float32)],
        compiler_params=pltpu.CompilerParams(vmem_limit_bytes=48 << 20),
        cost_estimate=pl.CostEstimate(flops=10**10, bytes_accessed=12 << 20, transcendentals=6 * 10**6),
        name="attend",
    )(near, far, *ks, *vs, *tails)


def mix(parts, shares, run, h):
    cols = slice(h * D_VAL, (h + 1) * D_VAL)
    terms = [p[run, cols].astype(jnp.float32) * s[run, h : h + 1] for p, s in zip(parts, shares)]
    return functools.reduce(jnp.add, terms)


def merge_kernel(near_ref, far_ref, *out_refs):
    for i, out_ref in enumerate(out_refs, 1):
        parts = [near_ref.at[i], far_ref.at[i]]
        stats = [unpacked(p[:, HEADS * D_VAL :]) for p in parts]
        best = functools.reduce(jnp.maximum, stats)
        shares = [jnp.exp2(s - best) for s in stats]
        whole = functools.reduce(jnp.add, shares)
        used = lanes(TOK) < HEADS
        out_ref[:, HEADS * D_VAL :] = packed(jnp.where(used, best + jnp.log2(whole), 0.0))
        shares = [s / whole for s in shares]
        for h in range(HEADS):
            out_ref[:, h * D_VAL : (h + 1) * D_VAL] = mix(parts, shares, slice(0, TOK), h).astype(jnp.bfloat16)


def combine_kernel(pos_ref, near_ref, far_ref, *refs):
    parts, out_ref = [near_ref.at[0], far_ref.at[0], *refs[:-1]], refs[-1]
    stats = [unpacked(p[:, HEADS * D_VAL :]) for p in parts]
    best = functools.reduce(jnp.maximum, stats)
    shares = [jnp.exp2(s - best) for s in stats]
    whole = functools.reduce(jnp.add, shares)
    shares = [s / whole for s in shares]
    turn = jnp.where(pos_ref[0] < pos_ref[RUN], 0, RUN)
    for half in range(2):
        dst = pl.ds(pl.multiple_of(turn if half == 0 else RUN - turn, RUN), RUN)
        run = slice(half * RUN, (half + 1) * RUN)
        for h in range(HEADS):
            out_ref[dst, h * D_VAL : (h + 1) * D_VAL] = mix(parts, shares, run, h).astype(jnp.bfloat16)


def shift(size, by):
    return [(i, (i + by) % size) for i in range(size)]


def body(q_nope, q_rope, kv_compressed, token_pos, kv_gain, w_uk, w_uv):
    scale = LOG2E / math.sqrt(D_NOPE + 64)
    spans, steps = rotations()
    low_span = lambda i, pos: (jnp.minimum(pos[0], pos[RUN]) // RUN, 0, 0)
    high_span = lambda i, pos: (jnp.maximum(pos[0], pos[RUN]) // RUN, 0, 0)
    whole = lambda shape: pl.BlockSpec(shape, lambda i, pos: (0,) * len(shape))
    key_rows, q_rows = pl.pallas_call(
        rows_kernel,
        grid_spec=pltpu.PrefetchScalarGridSpec(
            num_scalar_prefetch=1,
            grid=(1,),
            in_specs=[
                pl.BlockSpec((1, 2, 128), low_span),
                pl.BlockSpec((1, 2, 128), high_span),
                whole((2, RUN, 128)),
                whole(q_nope.shape),
                whole(q_rope.shape),
                whole(kv_compressed.shape),
                whole((1, D_LAT)),
            ],
            out_specs=[whole((TOK, ROW)), whole((TOK, Q_ROW))],
        ),
        out_shape=[
            jax.ShapeDtypeStruct((TOK, ROW), jnp.bfloat16),
            jax.ShapeDtypeStruct((TOK, Q_ROW), jnp.bfloat16),
        ],
        name="rows",
    )(token_pos, spans, spans, steps, q_nope, q_rope, kv_compressed, kv_gain[None, :])

    swap = lambda block: lax.ppermute(block, "core", [(0, 1), (1, 0)])
    across = lambda block, by: lax.ppermute(block, ACROSS, shift(X_SIZE, by))
    along = lambda block, by: lax.ppermute(block, "z", shift(Z_SIZE, by))

    along_y = [key_rows] + [lax.ppermute(key_rows, "y", shift(Y_SIZE, by)) for by in (1, -1, 2)]
    mine = jnp.stack(along_y)
    mine, q_rows = lax.optimization_barrier((mine, q_rows))

    up, down = along(mine, 1), along(mine, -1)
    near = jnp.stack([q_rows] + [across(q_rows, by) for by in (1, -1, 2)])
    far = swap(near)
    chunks = [expand([mine], w_uk, w_uv)]
    up, down, near, chunks = lax.optimization_barrier((up, down, near, chunks))
    for hop in range(2, Z_SIZE // 2 + 1):
        blocks = [up, down]
        if hop == Z_SIZE // 2:
            up, down = up[: Y_SIZE // 2], down[Y_SIZE // 2 :]
        up, down = along(up, 1), along(down, -1)
        chunks.append(expand(blocks, w_uk, w_uv))
        up, down, chunks = lax.optimization_barrier((up, down, chunks))
    chunks.append(expand([up, down], w_uk, w_uv))

    near, far = attend(near, far, chunks, scale)
    far = swap(far)
    part = jax.ShapeDtypeStruct((TOK, OUT_ROW), jnp.bfloat16)
    merged = pl.pallas_call(
        merge_kernel,
        in_specs=[VMEM] * 2,
        out_specs=[VMEM] * 3,
        out_shape=[part] * 3,
        name="merge",
    )(near, far)
    back = [across(m, by) for m, by in zip(merged, (-1, 1, 2))]
    return pl.pallas_call(
        combine_kernel,
        in_specs=[SMEM] + [VMEM] * 5,
        out_specs=VMEM,
        out_shape=jax.ShapeDtypeStruct((TOK, HEADS * D_VAL), jnp.bfloat16),
        name="combine",
    )(token_pos, near, far, *back)


def solution(mesh):
    finer = Mesh(mesh.devices.reshape(2, 2, Y_SIZE, Z_SIZE, 2), ALL_AXES)
    rows = P(ALL_AXES, None)
    in_specs = (rows, rows, rows, P(ALL_AXES), P(), P(), P())
    return jax.shard_map(body, mesh=finer, in_specs=in_specs, out_specs=rows, check_vma=False)
```

time: 558 us -> 100 us (0.18)
  blocking collectives: 399 us -> 0 us
  matrix products: 58.7 us -> 0 us
  starting transfers between devices: 0.36 us -> 35.5 us
  local copies, waits for them, and re-layouts: 39.7 us -> 6.24 us
  Pallas kernels: 0 us -> 29.1 us
  other arithmetic: 18.4 us -> 1.11 us
  between operations: 16.7 us -> 0.21 us
    all_gather x36 -> x0, blocking collectives: 372 us -> none  [stacked_from(): blocks = lax.all_gather(blocks, axes[k])]
    dot_general x4 -> x0, matrix products: 58.7 us -> none  [the longest x1 38.7 us: body(): jnp.einsum('thd,ud->htu', queries, keys, preferred_element_type=jnp.float32)]
    ppermute x0 -> x19, starting transfers between devices: none -> 35.5 us  [the longest x8 13.4 us: body(): along = lambda block, by: lax.ppermute(block, 'z', shift(Z_SIZE, by))]
    pallas_call x0 -> x9, Pallas kernels: none -> 29.1 us  [the longest x1 14.9 us: attend(): pl.pallas_call(functools.partial(attend_kernel, len(chunks), scale), grid...]
    ppermute x0 -> x19, waiting for transfers between devices: none -> 27.9 us  [the longest x8 13.1 us: body(): along = lambda block, by: lax.ppermute(block, 'z', shift(Z_SIZE, by))]
    unnamed x5 -> x0, blocking collectives: 27.1 us -> none
    all_gather x9 -> x0, waiting for transfers between devices: 21.4 us -> none  [stacked_from(): blocks = lax.all_gather(blocks, axes[k])]
    reduce_sum x2 -> x0, other arithmetic: 15.5 us -> none  [the longest x1 15.4 us: body(): total = jnp.sum(expd, axis=2)]
  transfers between devices with their start and end apart: 9 -> 19, of which waited for: 1 -> 12; matrix products, arithmetic and copies ran while one was open for 5% -> 0% of each run, Pallas kernels for 0% -> 6%
where the time goes in v1:
time: 100 us
  starting transfers between devices  35.5 us (36%)
  Pallas kernels  29.1 us (29%)
  waiting for transfers between devices  27.9 us (28%)
  local copies, waits for them, and re-layouts  6.24 us (6%)
  other arithmetic  1.11 us (1%)
    pallas_call x1, Pallas kernels, attend(): pl.pallas_call(functools.partial(attend_kernel, len(chunks), scale), grid...  14.9 us
    ppermute x8, starting transfers between devices, body(): along = lambda block, by: lax.ppermute(block, 'z', shift(Z_SIZE, by))  13.4 us
    ppermute x8, waiting for transfers between devices, body(): along = lambda block, by: lax.ppermute(block, 'z', shift(Z_SIZE, by))  13.1 us
    ppermute x2, starting transfers between devices, body(): swap = lambda block: lax.ppermute(block, 'core', [(0, 1), (1, 0)])  9.9 us
    ppermute x6, waiting for transfers between devices, body(): across = lambda block, by: lax.ppermute(block, ACROSS, shift(X_SIZE, by))  8.55 us
    ppermute x6, starting transfers between devices, body(): across = lambda block, by: lax.ppermute(block, ACROSS, shift(X_SIZE, by))  7.03 us
    unnamed x28, local copies, waits for them, and re-layouts  6.21 us
    pallas_call x5, Pallas kernels, expand(): pl.pallas_call(functools.partial(expand_kernel, len(blocks)), in_specs=[V...  5.91 us
  transfers between devices with their start and end apart: 19, of which 12 were waited for; matrix products, arithmetic and copies ran while one was open for 0% of the time, Pallas kernels for 6%

profile of v1, /device:TPU:1, one launch (start us, length us, event | category | flops | bytes accessed | tf_op | source)
XLA Modules:
  0.0 100.0 jit_solution(18342423810663975706)
XLA Ops:
  0.0 2.7 %rows.1 = (bf16[64,640]{1,0:T(8,128)(2,1)}, bf16[64,1664]{1,0:T(8,128)(2,1)}) custom-call(s32[64]{0:T(128)} %pos_ref.3, f32[512,2,128]{2,1,0:T(2,128)} %constant.4.clone.low_ref.high_ref, f32[512,2,128]{2,1,0:T(2,128)} %constant.4.clone.low_ref.high_ref, f32[2,32,128]{2,1,0:T(8,128)} %constant.5.clone.step_ref, bf16[64,1024]{1,0:T(8,128)(2,1)} %qn_ref.1, ...), custom_call_target="tpu_custom_call" | custom-call | tf_op jit(solution)/shard_map/rows/pallas_call | solution.py:270
  2.7 3.7 %collective-permute-start.2 = (bf16[64,640]{1,0:T(8,128)(2,1)}, bf16[64,640]{1,0:T(8,128)(2,1)S(1)}, u32[]{:S(2)}, u32[]{:S(2)}) collective-permute-start(bf16[64,640]{1,0:T(8,128)(2,1)} %get-tuple-element.68), channel_id=1, source_target_pairs={{0,32},{16,48},{32,0},{48,16},{1,33},{17,49},{33,1},{49,17},{2,34}... | collective-permute-start | bytes 245768 | tf_op jit(solution)/shard_map/ppermute | solution.py:297
  6.4 0.8 collective-permute-start.1
  7.2 0.7 collective-permute-start
  7.9 0.6 collective-permute-done.2
  8.4 2.6 %collective-permute-done.1 = bf16[64,640]{1,0:T(8,128)(2,1)S(1)} collective-permute-done((bf16[64,640]{1,0:T(8,128)(2,1)}, bf16[64,640]{1,0:T(8,128)(2,1)S(1)}, u32[]{:S(2)}, u32[]{:S(2)}) %collective-permute-start.1) | collective-permute-done | bytes 81952 | tf_op jit(solution)/shard_map/ppermute | solution.py:297
  11.0 1.4 %collective-permute-done = bf16[64,640]{1,0:T(8,128)(2,1)S(1)} collective-permute-done((bf16[64,640]{1,0:T(8,128)(2,1)}, bf16[64,640]{1,0:T(8,128)(2,1)S(1)}, u32[]{:S(2)}, u32[]{:S(2)}) %collective-permute-start) | collective-permute-done | bytes 81952 | tf_op jit(solution)/shard_map/ppermute | solution.py:297
  12.4 1.0 pad_maximum_fusion.1.refs_0_
  13.4 0.0 copy-done.10
  13.4 2.3 %collective-permute-start.7 = (bf16[64,1664]{1,0:T(8,128)(2,1)S(1)}, bf16[64,1664]{1,0:T(8,128)(2,1)S(1)}, u32[]{:S(2)}, u32[]{:S(2)}) collective-permute-start(bf16[64,1664]{1,0:T(8,128)(2,1)S(1)} %copy-done.10), channel_id=1, source_target_pairs={{0,128},{1,129},{128,0},{129,1},{2,130},{3,131},{130,2},{131,3},{4... | collective-permute-start | bytes 638984 | tf_op jit(solution)/shard_map/ppermute | solution.py:294
  15.7 0.9 collective-permute-start.6
  16.6 0.6 collective-permute-start.5
  17.2 5.6 %collective-permute-start.4 = (bf16[4,64,640]{2,1,0:T(8,128)(2,1)S(1)}, bf16[4,64,640]{2,1,0:T(8,128)(2,1)S(1)}, u32[]{:S(2)}, u32[]{:S(2)}) collective-permute-start(bf16[4,64,640]{2,1,0:T(8,128)(2,1)S(1)} %pad_maximum_fusion.1.refs_0_), channel_id=1, source_target_pairs={{0,14},{2,0},{4,2},{6,4},{8,6},{10,8},{12,10},{14,12},{1,15},{3,1}... | collective-permute-start | bytes 983048 | tf_op jit(solution)/shard_map/ppermute | solution.py:295
  22.8 0.0 collective-permute-start.3
  22.8 0.0 copy-done
  22.8 1.2 %copy-done.1 = bf16[8,512,128]{2,1,0:T(8,128)(2,1)S(1)} copy-done((bf16[8,512,128]{2,1,0:T(8,128)(2,1)S(1)}, bf16[8,512,128]{2,1,0:T(8,128)(2,1)}, u32[]{:S(2)}) %copy-start.1) | copy-done | bytes 1048600
  24.0 1.1 %expand.5 = (bf16[2,128,1024]{2,1,0:T(8,128)(2,1)S(1)}, bf16[2,128,1024]{2,1,0:T(8,128)(2,1)S(1)}, bf16[2,128,128]{2,1,0:T(8,128)(2,1)S(1)}) custom-call(bf16[4,64,640]{2,1,0:T(8,128)(2,1)S(1)} %pad_maximum_fusion.1.refs_0_, bf16[1024,512]{1,0:T(8,128)(2,1)S(1)} %bitcast.10, bf16[8,512,128]{2,1,0:T(8,128)(2,1)S(1)} %copy-done.1), custom_call_target="tpu_custom_call" | custom-call | flops 536870912 | bytes 3633152 | tf_op jit(solution)/shard_map/expand/pallas_call | solution.py:107
  25.1 0.0 collective-permute-done.7
  25.1 0.0 collective-permute-done.6
  25.1 0.3 collective-permute-done.5
  25.4 0.1 pad_maximum_fusion.refs_0_
  25.5 1.3 %collective-permute-done.4.refs_1_ = bf16[4,64,640]{2,1,0:T(8,128)(2,1)S(1)} collective-permute-done((bf16[4,64,640]{2,1,0:T(8,128)(2,1)S(1)}, bf16[4,64,640]{2,1,0:T(8,128)(2,1)S(1)}, u32[]{:S(2)}, u32[]{:S(2)}) %collective-permute-start.4) | collective-permute-done | bytes 327712 | tf_op jit(solution)/shard_map/ppermute | solution.py:295
  26.8 3.1 %collective-permute-done.3.refs_0_ = bf16[4,64,640]{2,1,0:T(8,128)(2,1)S(1)} collective-permute-done((bf16[4,64,640]{2,1,0:T(8,128)(2,1)S(1)}, bf16[4,64,640]{2,1,0:T(8,128)(2,1)S(1)}, u32[]{:S(2)}, u32[]{:S(2)}) %collective-permute-start.3) | collective-permute-done | bytes 327712 | tf_op jit(solution)/shard_map/ppermute | solution.py:295
  29.9 0.0 collective-permute-start.9
  29.9 2.7 %collective-permute-start.10 = (bf16[4,64,640]{2,1,0:T(8,128)(2,1)S(1)}, bf16[4,64,640]{2,1,0:T(8,128)(2,1)S(1)}, u32[]{:S(2)}, u32[]{:S(2)}) collective-permute-start(bf16[4,64,640]{2,1,0:T(8,128)(2,1)S(1)} %collective-permute-done.4.refs_1_), channel_id=1, source_target_pairs={{0,14},{2,0},{4,2},{6,4},{8,6},{10,8},{12,10},{14,12},{1,15},{3,1}... | collective-permute-start | bytes 983048 | tf_op jit(solution)/shard_map/ppermute | solution.py:295
  32.6 5.5 %collective-permute-start.8 = (bf16[4,64,1664]{2,1,0:T(8,128)(2,1)S(1)}, bf16[4,64,1664]{2,1,0:T(8,128)(2,1)S(1)}, u32[]{:S(2)}, u32[]{:S(2)}) collective-permute-start(bf16[4,64,1664]{2,1,0:T(8,128)(2,1)S(1)} %pad_maximum_fusion.refs_0_), channel_id=1, source_target_pairs={{0,64},{64,0},{1,65},{65,1},{2,66},{66,2},{3,67},{67,3},{4,68},{68... | collective-permute-start | bytes 2555912 | tf_op jit(solution)/shard_map/ppermute | solution.py:293
  38.1 1.3 %expand.6 = (bf16[2,256,1024]{2,1,0:T(8,128)(2,1)S(1)}, bf16[2,256,1024]{2,1,0:T(8,128)(2,1)S(1)}, bf16[2,256,128]{2,1,0:T(8,128)(2,1)S(1)}) custom-call(bf16[4,64,640]{2,1,0:T(8,128)(2,1)S(1)} %collective-permute-done.3.refs_0_, bf16[4,64,640]{2,1,0:T(8,128)(2,1)S(1)} %collective-permute-done.4.refs_1_, bf16[1024,512]{1,0:T(8,128)(2,1)S(1)} %bitcast.11, ...), custom_call_target="tpu_custom_call" | custom-call | flops 1073741824 | bytes 5169152 | tf_op jit(solution)/shard_map/expand/pallas_call | solution.py:107
  39.3 0.0 copy-start.3
  39.3 1.0 copy-done.3
  40.3 1.0 %copy-done.4 = bf16[2,256,1024]{2,1,0:T(8,128)(2,1)} copy-done((bf16[2,256,1024]{2,1,0:T(8,128)(2,1)}, bf16[2,256,1024]{2,1,0:T(8,128)(2,1)S(1)}, u32[]{:S(2)}) %copy-start.4) | copy-done | bytes 1048600
  41.3 0.0 collective-permute-done.9.refs_0_
  41.3 0.0 collective-permute-done.10.refs_1_
  41.3 0.0 collective-permute-start.11
  41.3 2.7 %collective-permute-start.12 = (bf16[4,64,640]{2,1,0:T(8,128)(2,1)S(1)}, bf16[4,64,640]{2,1,0:T(8,128)(2,1)S(1)}, u32[]{:S(2)}, u32[]{:S(2)}) collective-permute-start(bf16[4,64,640]{2,1,0:T(8,128)(2,1)S(1)} %collective-permute-done.10.refs_1_), channel_id=1, source_target_pairs={{0,14},{2,0},{4,2},{6,4},{8,6},{10,8},{12,10},{14,12},{1,15},{3,1}... | collective-permute-start | bytes 983048 | tf_op jit(solution)/shard_map/ppermute | solution.py:295
  44.0 1.3 %expand.7 = (bf16[2,256,1024]{2,1,0:T(8,128)(2,1)S(1)}, bf16[2,256,1024]{2,1,0:T(8,128)(2,1)S(1)}, bf16[2,256,128]{2,1,0:T(8,128)(2,1)S(1)}) custom-call(bf16[4,64,640]{2,1,0:T(8,128)(2,1)S(1)} %collective-permute-done.9.refs_0_, bf16[4,64,640]{2,1,0:T(8,128)(2,1)S(1)} %collective-permute-done.10.refs_1_, bf16[1024,512]{1,0:T(8,128)(2,1)S(1)} %bitcast.12, ...), custom_call_target="tpu_custom_call" | custom-call | flops 1073741824 | bytes 5169152 | tf_op jit(solution)/shard_map/expand/pallas_call | solution.py:107
  45.3 0.0 copy-start.5
  45.3 0.0 copy-start.6
  45.3 4.7 %collective-permute-done.11.refs_0_ = bf16[4,64,640]{2,1,0:T(8,128)(2,1)S(1)} collective-permute-done((bf16[4,64,640]{2,1,0:T(8,128)(2,1)S(1)}, bf16[4,64,640]{2,1,0:T(8,128)(2,1)S(1)}, u32[]{:S(2)}, u32[]{:S(2)}) %collective-permute-start.11) | collective-permute-done | bytes 327712 | tf_op jit(solution)/shard_map/ppermute | solution.py:295
  49.9 0.0 collective-permute-done.12.refs_1_
  50.0 2.5 %collective-permute-start.14 = (bf16[2,64,640]{2,1,0:T(8,128)(2,1)S(1)}, bf16[2,64,640]{2,1,0:T(8,128)(2,1)S(1)}, u32[]{:S(2)}, u32[]{:S(2)}) collective-permute-start(bf16[2,64,640]{2,1,0:T(8,128)(2,1)S(1)} %slice.7), channel_id=1, source_target_pairs={{0,14},{2,0},{4,2},{6,4},{8,6},{10,8},{12,10},{14,12},{1,15},{3,1}... | collective-permute-start | bytes 491528 | tf_op jit(solution)/shard_map/ppermute | solution.py:295
  52.4 0.0 collective-permute-start.13
  52.5 1.3 %expand.8 = (bf16[2,256,1024]{2,1,0:T(8,128)(2,1)S(1)}, bf16[2,256,1024]{2,1,0:T(8,128)(2,1)S(1)}, bf16[2,256,128]{2,1,0:T(8,128)(2,1)S(1)}) custom-call(bf16[4,64,640]{2,1,0:T(8,128)(2,1)S(1)} %collective-permute-done.11.refs_0_, bf16[4,64,640]{2,1,0:T(8,128)(2,1)S(1)} %collective-permute-done.12.refs_1_, bf16[1024,512]{1,0:T(8,128)(2,1)S(1)} %bitcast.13, ...), custom_call_target="tpu_custom_call" | custom-call | flops 1073741824 | bytes 5169152 | tf_op jit(solution)/shard_map/expand/pallas_call | solution.py:107
  53.7 0.0 copy-done.5
  53.7 0.0 copy-done.6
  53.7 0.0 copy-start.7
  53.8 1.0 collective-permute-done.14.refs_1_
  54.7 3.1 %collective-permute-done.13.refs_0_ = bf16[2,64,640]{2,1,0:T(8,128)(2,1)S(1)} collective-permute-done((bf16[2,64,640]{2,1,0:T(8,128)(2,1)S(1)}, bf16[2,64,640]{2,1,0:T(8,128)(2,1)S(1)}, u32[]{:S(2)}, u32[]{:S(2)}) %collective-permute-start.13) | collective-permute-done | bytes 163872 | tf_op jit(solution)/shard_map/ppermute | solution.py:295
  57.8 1.1 %expand.9 = (bf16[2,128,1024]{2,1,0:T(8,128)(2,1)S(1)}, bf16[2,128,1024]{2,1,0:T(8,128)(2,1)S(1)}, bf16[2,128,128]{2,1,0:T(8,128)(2,1)S(1)}) custom-call(bf16[2,64,640]{2,1,0:T(8,128)(2,1)S(1)} %collective-permute-done.13.refs_0_, bf16[2,64,640]{2,1,0:T(8,128)(2,1)S(1)} %collective-permute-done.14.refs_1_, bf16[1024,512]{1,0:T(8,128)(2,1)S(1)} %bitcast.14, ...), custom_call_target="tpu_custom_call" | custom-call | flops 536870912 | bytes 3633152 | tf_op jit(solution)/shard_map/expand/pallas_call | solution.py:107
  58.9 0.0 collective-permute-done.8.refs_1_
  58.9 14.9 %attend.1 = (bf16[4,64,1152]{2,1,0:T(8,128)(2,1)S(1)}, bf16[4,64,1152]{2,1,0:T(8,128)(2,1)S(1)}) custom-call(bf16[4,64,1664]{2,1,0:T(8,128)(2,1)S(1)} %pad_maximum_fusion.refs_0_, bf16[4,64,1664]{2,1,0:T(8,128)(2,1)S(1)} %collective-permute-done.8.refs_1_, bf16[2,128,1024]{2,1,0:T(8,128)(2,1)S(1)} %get-tuple-element.109.refs_2_, ...), custom_call_target="tpu_custom_call" | custom-call | flops 10000000000 | bytes 12582912 | tf_op jit(solution)/shard_map/attend/pallas_call | solution.py:210
  73.8 0.8 copy-done.2
  74.7 4.4 %collective-permute-start.15 = (bf16[4,64,1152]{2,1,0:T(8,128)(2,1)S(1)}, bf16[4,64,1152]{2,1,0:T(8,128)(2,1)S(1)}, u32[]{:S(2)}, u32[]{:S(2)}) collective-permute-start(bf16[4,64,1152]{2,1,0:T(8,128)(2,1)S(1)} %get-tuple-element.127), channel_id=1, source_target_pairs={{0,64},{64,0},{1,65},{65,1},{2,66},{66,2},{3,67},{67,3},{4,68},{68... | collective-permute-start | bytes 1769480 | tf_op jit(solution)/shard_map/ppermute | solution.py:293
  79.1 1.6 %collective-permute-done.15.far_ref = bf16[4,64,1152]{2,1,0:T(8,128)(2,1)S(1)} collective-permute-done((bf16[4,64,1152]{2,1,0:T(8,128)(2,1)S(1)}, bf16[4,64,1152]{2,1,0:T(8,128)(2,1)S(1)}, u32[]{:S(2)}, u32[]{:S(2)}) %collective-permute-start.15) | collective-permute-done | bytes 589856 | tf_op jit(solution)/shard_map/ppermute | solution.py:293
  80.7 0.8 copy-done.9
  81.6 3.0 %merge.1 = (bf16[64,1152]{1,0:T(8,128)(2,1)}, bf16[64,1152]{1,0:T(8,128)(2,1)}, bf16[64,1152]{1,0:T(8,128)(2,1)}) custom-call(bf16[4,64,1152]{2,1,0:T(8,128)(2,1)} %copy-done.2, bf16[4,64,1152]{2,1,0:T(8,128)(2,1)} %copy-done.9), custom_call_target="tpu_custom_call" | custom-call | tf_op jit(solution)/shard_map/merge/pallas_call | solution.py:318
  84.6 2.1 %collective-permute-start.16 = (bf16[64,1152]{1,0:T(8,128)(2,1)}, bf16[64,1152]{1,0:T(8,128)(2,1)S(1)}, u32[]{:S(2)}, u32[]{:S(2)}) collective-permute-start(bf16[64,1152]{1,0:T(8,128)(2,1)} %get-tuple-element.128), channel_id=1, source_target_pairs={{0,129},{1,0},{128,1},{129,128},{2,131},{3,2},{130,3},{131,130},{4... | collective-permute-start | bytes 442376 | tf_op jit(solution)/shard_map/ppermute | solution.py:294
  86.7 0.0 collective-permute-start.17
  86.7 1.2 %collective-permute-start.18 = (bf16[64,1152]{1,0:T(8,128)(2,1)}, bf16[64,1152]{1,0:T(8,128)(2,1)S(1)}, u32[]{:S(2)}, u32[]{:S(2)}) collective-permute-start(bf16[64,1152]{1,0:T(8,128)(2,1)} %get-tuple-element.130), channel_id=1, source_target_pairs={{0,128},{1,129},{128,0},{129,1},{2,130},{3,131},{130,2},{131,3},{4... | collective-permute-start | bytes 442376 | tf_op jit(solution)/shard_map/ppermute | solution.py:294
  87.9 2.0 %collective-permute-done.16.refs_0_ = bf16[64,1152]{1,0:T(8,128)(2,1)S(1)} collective-permute-done((bf16[64,1152]{1,0:T(8,128)(2,1)}, bf16[64,1152]{1,0:T(8,128)(2,1)S(1)}, u32[]{:S(2)}, u32[]{:S(2)}) %collective-permute-start.16) | collective-permute-done | bytes 147488 | tf_op jit(solution)/shard_map/ppermute | solution.py:294
  89.9 6.2 %collective-permute-done.17.refs_1_ = bf16[64,1152]{1,0:T(8,128)(2,1)S(1)} collective-permute-done((bf16[64,1152]{1,0:T(8,128)(2,1)}, bf16[64,1152]{1,0:T(8,128)(2,1)S(1)}, u32[]{:S(2)}, u32[]{:S(2)}) %collective-permute-start.17) | collective-permute-done | bytes 147488 | tf_op jit(solution)/shard_map/ppermute | solution.py:294
  96.1 0.0 collective-permute-done.18.refs_2_
  96.1 0.6 copy-done.12
  96.8 0.7 copy-done.13
  97.4 2.6 %combine.1 = bf16[64,1024]{1,0:T(8,128)(2,1)} custom-call(s32[64]{0:T(128)} %pos_ref.3, bf16[4,64,1152]{2,1,0:T(8,128)(2,1)} %copy-done.2, bf16[4,64,1152]{2,1,0:T(8,128)(2,1)} %copy-done.9, bf16[64,1152]{1,0:T(8,128)(2,1)} %copy-done.11, bf16[64,1152]{1,0:T(8,128)(2,1)} %copy-done.12, bf16[64,1152]{1,0:T(8,128)(2,1)} %copy-done.13), custom_call_target="tpu_custom_call" | custom-call | tf_op jit(solution)/shard_map/combine/pallas_call | solution.py:326
  (15 shorter events, 0.1 us)
Async XLA Ops:
  0.0 22.8 %copy-start = (bf16[8,128,512]{2,1,0:T(8,128)(2,1)S(1)}, bf16[8,128,512]{2,1,0:T(8,128)(2,1)}, u32[]{:S(2)}) copy-start(bf16[8,128,512]{2,1,0:T(8,128)(2,1)} %param.14) | copy-start | bytes 3145732
  2.7 5.8 %collective-permute-start.2 = (bf16[64,640]{1,0:T(8,128)(2,1)}, bf16[64,640]{1,0:T(8,128)(2,1)S(1)}, u32[]{:S(2)}, u32[]{:S(2)}) collective-permute-start(bf16[64,640]{1,0:T(8,128)(2,1)} %get-tuple-element.68), channel_id=1, source_target_pairs={{0,32},{16,48},{32,0},{48,16},{1,33},{17,49},{33,1},{49,17},{2,34}... | collective-permute-start | bytes 245768 | tf_op jit(solution)/shard_map/ppermute | solution.py:297
  6.4 4.6 %collective-permute-start.1 = (bf16[64,640]{1,0:T(8,128)(2,1)}, bf16[64,640]{1,0:T(8,128)(2,1)S(1)}, u32[]{:S(2)}, u32[]{:S(2)}) collective-permute-start(bf16[64,640]{1,0:T(8,128)(2,1)} %get-tuple-element.68), channel_id=1, source_target_pairs={{0,48},{16,0},{32,16},{48,32},{1,49},{17,1},{33,17},{49,33},{2,50}... | collective-permute-start | bytes 245768 | tf_op jit(solution)/shard_map/ppermute | solution.py:297
  7.2 5.2 %collective-permute-start = (bf16[64,640]{1,0:T(8,128)(2,1)}, bf16[64,640]{1,0:T(8,128)(2,1)S(1)}, u32[]{:S(2)}, u32[]{:S(2)}) collective-permute-start(bf16[64,640]{1,0:T(8,128)(2,1)} %get-tuple-element.68), channel_id=1, source_target_pairs={{0,16},{16,32},{32,48},{48,0},{1,17},{17,33},{33,49},{49,1},{2,18}... | collective-permute-start | bytes 245768 | tf_op jit(solution)/shard_map/ppermute | solution.py:297
  12.4 1.0 copy-start.10
  13.4 11.7 %collective-permute-start.7 = (bf16[64,1664]{1,0:T(8,128)(2,1)S(1)}, bf16[64,1664]{1,0:T(8,128)(2,1)S(1)}, u32[]{:S(2)}, u32[]{:S(2)}) collective-permute-start(bf16[64,1664]{1,0:T(8,128)(2,1)S(1)} %copy-done.10), channel_id=1, source_target_pairs={{0,128},{1,129},{128,0},{129,1},{2,130},{3,131},{130,2},{131,3},{4... | collective-permute-start | bytes 638984 | tf_op jit(solution)/shard_map/ppermute | solution.py:294
  15.7 9.4 %collective-permute-start.6 = (bf16[64,1664]{1,0:T(8,128)(2,1)S(1)}, bf16[64,1664]{1,0:T(8,128)(2,1)S(1)}, u32[]{:S(2)}, u32[]{:S(2)}) collective-permute-start(bf16[64,1664]{1,0:T(8,128)(2,1)S(1)} %copy-done.10), channel_id=1, source_target_pairs={{0,129},{1,0},{128,1},{129,128},{2,131},{3,2},{130,3},{131,130},{4... | collective-permute-start | bytes 638984 | tf_op jit(solution)/shard_map/ppermute | solution.py:294
  16.6 8.8 %collective-permute-start.5 = (bf16[64,1664]{1,0:T(8,128)(2,1)S(1)}, bf16[64,1664]{1,0:T(8,128)(2,1)S(1)}, u32[]{:S(2)}, u32[]{:S(2)}) collective-permute-start(bf16[64,1664]{1,0:T(8,128)(2,1)S(1)} %copy-done.10), channel_id=1, source_target_pairs={{0,1},{1,128},{128,129},{129,0},{2,3},{3,130},{130,131},{131,2},{4... | collective-permute-start | bytes 638984 | tf_op jit(solution)/shard_map/ppermute | solution.py:294
  17.2 9.6 %collective-permute-start.4 = (bf16[4,64,640]{2,1,0:T(8,128)(2,1)S(1)}, bf16[4,64,640]{2,1,0:T(8,128)(2,1)S(1)}, u32[]{:S(2)}, u32[]{:S(2)}) collective-permute-start(bf16[4,64,640]{2,1,0:T(8,128)(2,1)S(1)} %pad_maximum_fusion.1.refs_0_), channel_id=1, source_target_pairs={{0,14},{2,0},{4,2},{6,4},{8,6},{10,8},{12,10},{14,12},{1,15},{3,1}... | collective-permute-start | bytes 983048 | tf_op jit(solution)/shard_map/ppermute | solution.py:295
  22.8 7.1 %collective-permute-start.3 = (bf16[4,64,640]{2,1,0:T(8,128)(2,1)S(1)}, bf16[4,64,640]{2,1,0:T(8,128)(2,1)S(1)}, u32[]{:S(2)}, u32[]{:S(2)}) collective-permute-start(bf16[4,64,640]{2,1,0:T(8,128)(2,1)S(1)} %pad_maximum_fusion.1.refs_0_), channel_id=1, source_target_pairs={{0,2},{2,4},{4,6},{6,8},{8,10},{10,12},{12,14},{14,0},{1,3},{3,5},... | collective-permute-start | bytes 983048 | tf_op jit(solution)/shard_map/ppermute | solution.py:295
  22.8 1.2 %copy-start.1 = (bf16[8,512,128]{2,1,0:T(8,128)(2,1)S(1)}, bf16[8,512,128]{2,1,0:T(8,128)(2,1)}, u32[]{:S(2)}) copy-start(bf16[8,512,128]{2,1,0:T(8,128)(2,1)} %refs_3_.7) | copy-start | bytes 3145732
  29.9 11.4 %collective-permute-start.9 = (bf16[4,64,640]{2,1,0:T(8,128)(2,1)S(1)}, bf16[4,64,640]{2,1,0:T(8,128)(2,1)S(1)}, u32[]{:S(2)}, u32[]{:S(2)}) collective-permute-start(bf16[4,64,640]{2,1,0:T(8,128)(2,1)S(1)} %collective-permute-done.3.refs_0_), channel_id=1, source_target_pairs={{0,2},{2,4},{4,6},{6,8},{8,10},{10,12},{12,14},{14,0},{1,3},{3,5},... | collective-permute-start | bytes 983048 | tf_op jit(solution)/shard_map/ppermute | solution.py:295
  29.9 11.4 %collective-permute-start.10 = (bf16[4,64,640]{2,1,0:T(8,128)(2,1)S(1)}, bf16[4,64,640]{2,1,0:T(8,128)(2,1)S(1)}, u32[]{:S(2)}, u32[]{:S(2)}) collective-permute-start(bf16[4,64,640]{2,1,0:T(8,128)(2,1)S(1)} %collective-permute-done.4.refs_1_), channel_id=1, source_target_pairs={{0,14},{2,0},{4,2},{6,4},{8,6},{10,8},{12,10},{14,12},{1,15},{3,1}... | collective-permute-start | bytes 983048 | tf_op jit(solution)/shard_map/ppermute | solution.py:295
  32.6 26.4 %collective-permute-start.8 = (bf16[4,64,1664]{2,1,0:T(8,128)(2,1)S(1)}, bf16[4,64,1664]{2,1,0:T(8,128)(2,1)S(1)}, u32[]{:S(2)}, u32[]{:S(2)}) collective-permute-start(bf16[4,64,1664]{2,1,0:T(8,128)(2,1)S(1)} %pad_maximum_fusion.refs_0_), channel_id=1, source_target_pairs={{0,64},{64,0},{1,65},{65,1},{2,66},{66,2},{3,67},{67,3},{4,68},{68... | collective-permute-start | bytes 2555912 | tf_op jit(solution)/shard_map/ppermute | solution.py:293
  39.3 1.0 copy-start.3
  40.3 1.0 %copy-start.4 = (bf16[2,256,1024]{2,1,0:T(8,128)(2,1)}, bf16[2,256,1024]{2,1,0:T(8,128)(2,1)S(1)}, u32[]{:S(2)}) copy-start(bf16[2,256,1024]{2,1,0:T(8,128)(2,1)S(1)} %get-tuple-element.117.refs_8_) | copy-start | bytes 3145732
  41.3 8.6 %collective-permute-start.11 = (bf16[4,64,640]{2,1,0:T(8,128)(2,1)S(1)}, bf16[4,64,640]{2,1,0:T(8,128)(2,1)S(1)}, u32[]{:S(2)}, u32[]{:S(2)}) collective-permute-start(bf16[4,64,640]{2,1,0:T(8,128)(2,1)S(1)} %collective-permute-done.9.refs_0_), channel_id=1, source_target_pairs={{0,2},{2,4},{4,6},{6,8},{8,10},{10,12},{12,14},{14,0},{1,3},{3,5},... | collective-permute-start | bytes 983048 | tf_op jit(solution)/shard_map/ppermute | solution.py:295
  41.3 8.6 %collective-permute-start.12 = (bf16[4,64,640]{2,1,0:T(8,128)(2,1)S(1)}, bf16[4,64,640]{2,1,0:T(8,128)(2,1)S(1)}, u32[]{:S(2)}, u32[]{:S(2)}) collective-permute-start(bf16[4,64,640]{2,1,0:T(8,128)(2,1)S(1)} %collective-permute-done.10.refs_1_), channel_id=1, source_target_pairs={{0,14},{2,0},{4,2},{6,4},{8,6},{10,8},{12,10},{14,12},{1,15},{3,1}... | collective-permute-start | bytes 983048 | tf_op jit(solution)/shard_map/ppermute | solution.py:295
  45.3 8.5 %copy-start.5 = (bf16[2,256,1024]{2,1,0:T(8,128)(2,1)}, bf16[2,256,1024]{2,1,0:T(8,128)(2,1)S(1)}, u32[]{:S(2)}) copy-start(bf16[2,256,1024]{2,1,0:T(8,128)(2,1)S(1)} %get-tuple-element.111.refs_4_) | copy-start | bytes 3145732
  45.3 8.5 %copy-start.6 = (bf16[2,256,1024]{2,1,0:T(8,128)(2,1)}, bf16[2,256,1024]{2,1,0:T(8,128)(2,1)S(1)}, u32[]{:S(2)}) copy-start(bf16[2,256,1024]{2,1,0:T(8,128)(2,1)S(1)} %get-tuple-element.118.refs_9_) | copy-start | bytes 3145732
  50.0 4.7 %collective-permute-start.14 = (bf16[2,64,640]{2,1,0:T(8,128)(2,1)S(1)}, bf16[2,64,640]{2,1,0:T(8,128)(2,1)S(1)}, u32[]{:S(2)}, u32[]{:S(2)}) collective-permute-start(bf16[2,64,640]{2,1,0:T(8,128)(2,1)S(1)} %slice.7), channel_id=1, source_target_pairs={{0,14},{2,0},{4,2},{6,4},{8,6},{10,8},{12,10},{14,12},{1,15},{3,1}... | collective-permute-start | bytes 491528 | tf_op jit(solution)/shard_map/ppermute | solution.py:295
  52.4 5.4 %collective-permute-start.13 = (bf16[2,64,640]{2,1,0:T(8,128)(2,1)S(1)}, bf16[2,64,640]{2,1,0:T(8,128)(2,1)S(1)}, u32[]{:S(2)}, u32[]{:S(2)}) collective-permute-start(bf16[2,64,640]{2,1,0:T(8,128)(2,1)S(1)} %slice.6), channel_id=1, source_target_pairs={{0,2},{2,4},{4,6},{6,8},{8,10},{10,12},{12,14},{14,0},{1,3},{3,5},... | collective-permute-start | bytes 491528 | tf_op jit(solution)/shard_map/ppermute | solution.py:295
  53.7 5.2 %copy-start.7 = (bf16[2,256,1024]{2,1,0:T(8,128)(2,1)}, bf16[2,256,1024]{2,1,0:T(8,128)(2,1)S(1)}, u32[]{:S(2)}) copy-start(bf16[2,256,1024]{2,1,0:T(8,128)(2,1)S(1)} %get-tuple-element.112.refs_5_) | copy-start | bytes 3145732
  53.7 5.2 %copy-start.8 = (bf16[2,256,1024]{2,1,0:T(8,128)(2,1)}, bf16[2,256,1024]{2,1,0:T(8,128)(2,1)S(1)}, u32[]{:S(2)}) copy-start(bf16[2,256,1024]{2,1,0:T(8,128)(2,1)S(1)} %get-tuple-element.119.refs_10_) | copy-start | bytes 3145732
  73.8 0.8 copy-start.2
  74.7 6.0 %collective-permute-start.15 = (bf16[4,64,1152]{2,1,0:T(8,128)(2,1)S(1)}, bf16[4,64,1152]{2,1,0:T(8,128)(2,1)S(1)}, u32[]{:S(2)}, u32[]{:S(2)}) collective-permute-start(bf16[4,64,1152]{2,1,0:T(8,128)(2,1)S(1)} %get-tuple-element.127), channel_id=1, source_target_pairs={{0,64},{64,0},{1,65},{65,1},{2,66},{66,2},{3,67},{67,3},{4,68},{68... | collective-permute-start | bytes 1769480 | tf_op jit(solution)/shard_map/ppermute | solution.py:293
  80.7 0.8 copy-start.9
  84.6 5.3 %collective-permute-start.16 = (bf16[64,1152]{1,0:T(8,128)(2,1)}, bf16[64,1152]{1,0:T(8,128)(2,1)S(1)}, u32[]{:S(2)}, u32[]{:S(2)}) collective-permute-start(bf16[64,1152]{1,0:T(8,128)(2,1)} %get-tuple-element.128), channel_id=1, source_target_pairs={{0,129},{1,0},{128,1},{129,128},{2,131},{3,2},{130,3},{131,130},{4... | collective-permute-start | bytes 442376 | tf_op jit(solution)/shard_map/ppermute | solution.py:294
  86.7 9.4 %collective-permute-start.17 = (bf16[64,1152]{1,0:T(8,128)(2,1)}, bf16[64,1152]{1,0:T(8,128)(2,1)S(1)}, u32[]{:S(2)}, u32[]{:S(2)}) collective-permute-start(bf16[64,1152]{1,0:T(8,128)(2,1)} %get-tuple-element.129), channel_id=1, source_target_pairs={{0,1},{1,128},{128,129},{129,0},{2,3},{3,130},{130,131},{131,2},{4... | collective-permute-start | bytes 442376 | tf_op jit(solution)/shard_map/ppermute | solution.py:294
  86.7 9.4 %collective-permute-start.18 = (bf16[64,1152]{1,0:T(8,128)(2,1)}, bf16[64,1152]{1,0:T(8,128)(2,1)S(1)}, u32[]{:S(2)}, u32[]{:S(2)}) collective-permute-start(bf16[64,1152]{1,0:T(8,128)(2,1)} %get-tuple-element.130), channel_id=1, source_target_pairs={{0,128},{1,129},{128,0},{129,1},{2,130},{3,131},{130,2},{131,3},{4... | collective-permute-start | bytes 442376 | tf_op jit(solution)/shard_map/ppermute | solution.py:294
  89.9 6.3 %copy-start.11 = (bf16[64,1152]{1,0:T(8,128)(2,1)}, bf16[64,1152]{1,0:T(8,128)(2,1)S(1)}, u32[]{:S(2)}) copy-start(bf16[64,1152]{1,0:T(8,128)(2,1)S(1)} %collective-permute-done.16.refs_0_) | copy-start | bytes 442372
  96.1 0.6 copy-start.12
  96.8 0.7 copy-start.13

commit v2 on v1

--- a/solution.py
+++ b/solution.py
@@ -28,7 +28,7 @@
 
 NEGATIVE = -1e30
 FLOOR = -1e28
-LOG2E = 1.4426950408889634
+SCALE = 1.4426950408889634 / math.sqrt(D_NOPE + 64)
 
 VMEM = pl.BlockSpec(memory_space=pltpu.VMEM)
 SMEM = pl.BlockSpec(memory_space=pltpu.SMEM)
@@ -70,7 +70,7 @@
         for pair in range(HEADS // 2):
             part = qr_ref[src, pair * 128 : (pair + 1) * 128].astype(jnp.float32)
             at = HEADS * D_NOPE + pair * 128
-            q_ref[dst, at : at + 128] = turned(part, cosine, sine, first).astype(jnp.bfloat16)
+            q_ref[dst, at : at + 128] = (turned(part, cosine, sine, first) * SCALE).astype(jnp.bfloat16)
         q_ref[dst, Q_ROW - 128 :] = jnp.full((RUN, 128), span, jnp.float32).astype(jnp.bfloat16)
 
 
@@ -96,7 +96,7 @@
         tail_ref[half] = rows[:, D_LAT:]
         for pair in range(HEADS // 2):
             cols = slice(pair * 256, (pair + 1) * 256)
-            k_ref[half, :, cols] = over_lanes(latent, uk_ref[cols, :]).astype(jnp.bfloat16)
+            k_ref[half, :, cols] = (over_lanes(latent, uk_ref[cols, :]) * SCALE).astype(jnp.bfloat16)
             w = jnp.concatenate([uv_ref[2 * pair], uv_ref[2 * pair + 1]], axis=1)
             v_ref[half, :, cols] = jnp.dot(latent, w, preferred_element_type=jnp.float32).astype(jnp.bfloat16)
 
@@ -109,7 +109,7 @@
         in_specs=[VMEM] * (len(blocks) + 2),
         out_specs=[VMEM] * 3,
         out_shape=[out(HEADS * D_NOPE), out(HEADS * D_VAL), out(128)],
-        compiler_params=pltpu.CompilerParams(vmem_limit_bytes=24 << 20),
+        compiler_params=pltpu.CompilerParams(vmem_limit_bytes=14 << 20),
         cost_estimate=pl.CostEstimate(
             flops=4 * n * D_LAT * 2048, bytes_accessed=n * 12000 + (2 << 20), transcendentals=0
         ),
@@ -131,7 +131,7 @@
     return pieces + pltpu.roll(pieces, 120, 1) + pltpu.roll(pieces, 112, 1)
 
 
-def attend_kernel(n_chunks, scale, *refs):
+def attend_kernel(n_chunks, own, *refs):
     near_ref, far_ref = refs[:2]
     k_refs, v_refs, tail_refs = (refs[2 + i * n_chunks : 2 + (i + 1) * n_chunks] for i in range(3))
     outs, lse_scr = refs[2 + 3 * n_chunks : -1], refs[-1]
@@ -142,6 +142,7 @@
     rope_at = pl.multiple_of(HEADS * D_NOPE + step * 128, 128)
     tails = [jnp.concatenate([ref[half] for ref in tail_refs], axis=0) for half in range(2)]
     spans = jnp.max(tails[0].astype(jnp.float32), axis=0, keepdims=True)
+    ones = jnp.ones((tails[0].shape[0], 128), jnp.bfloat16)
     first_keys = tail_refs[0].shape[1]
     shape = (Q_TILE, first_keys)
     row, col = (lax.broadcasted_iota(jnp.int32, shape, d) for d in (0, 1))
@@ -170,25 +171,27 @@
             keys = lambda run: jnp.concatenate(
                 [jnp.concatenate([ref[run, :, cols] for ref in k_refs], axis=0), tails[run]], axis=1
             )
-            values = lambda run: jnp.concatenate([ref[run, :, cols] for ref in v_refs], axis=0)
-            score = over_lanes(masked, keys(half)) * scale
-            head = jnp.where(later, NEGATIVE, score[:, :first_keys])
-            parts = [(jnp.concatenate([head, score[:, first_keys:]], axis=1), half)]
+            values = lambda run: jnp.concatenate(
+                [jnp.concatenate([ref[run, :, cols] for ref in v_refs], axis=0), ones], axis=1
+            )
+            score = over_lanes(masked, keys(half))
+            if own:
+                head = jnp.where(later, NEGATIVE, score[:, :first_keys])
+                score = jnp.concatenate([head, score[:, first_keys:]], axis=1)
+            parts = [(score, half)]
             if half:
                 plain = jnp.concatenate([nope[:, cols], ends([0.0] * len(q_refs))], axis=1)
-                parts.append((over_lanes(plain, keys(0)) * scale, 0))
+                parts.append((over_lanes(plain, keys(0)), 0))
             peak = functools.reduce(jnp.maximum, [jnp.max(s, axis=1, keepdims=True) for s, _ in parts])
             peak = jnp.maximum(peak, FLOOR)
-            total, added = None, None
+            added = None
             for s, run_of in parts:
-                expd = jnp.exp2(s - peak)
-                t = jnp.sum(expd, axis=1, keepdims=True)
-                a = jnp.dot(expd.astype(jnp.bfloat16), values(run_of), preferred_element_type=jnp.float32)
-                total = t if total is None else total + t
+                weight = jnp.exp2(s - peak).astype(jnp.bfloat16)
+                a = jnp.dot(weight, values(run_of), preferred_element_type=jnp.float32)
                 added = a if added is None else added + a
-            some = total > 0.0
-            total = jnp.where(some, total, 1.0)
-            result = (added / total).astype(jnp.bfloat16)
+            some = added[:, D_VAL:] > 0.0
+            total = jnp.where(some, added[:, D_VAL:], 1.0)
+            result = (added[:, :D_VAL] / total).astype(jnp.bfloat16)
             lse = jnp.where(some, peak + jnp.log2(total), NEGATIVE)
             head_at = pl.multiple_of(step * 256 + inner * 128, 128)
             for i in range(2 * X_SIZE):
@@ -202,13 +205,13 @@
             outs[i // X_SIZE][i % X_SIZE, :, HEADS * D_VAL :] = packed(lse_scr[i])
 
 
-def attend(near, far, chunks, scale):
+def attend(near, far, chunks, own):
     whole = lambda shape: pl.BlockSpec(shape, lambda i: (0,) * len(shape))
     by_head = lambda a: pl.BlockSpec((2, a.shape[1], 256), lambda i: (0, 0, i))
     ks, vs, tails = zip(*chunks)
     out = jax.ShapeDtypeStruct((X_SIZE, TOK, OUT_ROW), jnp.bfloat16)
     return pl.pallas_call(
-        functools.partial(attend_kernel, len(chunks), scale),
+        functools.partial(attend_kernel, len(chunks), own),
         grid=(HEADS // 2,),
         in_specs=[whole(near.shape), whole(far.shape)]
         + [by_head(a) for a in ks + vs]
@@ -216,8 +219,10 @@
         out_specs=[whole(out.shape)] * 2,
         out_shape=[out, out],
         scratch_shapes=[pltpu.VMEM((2 * X_SIZE, TOK, 128), jnp.float32)],
-        compiler_params=pltpu.CompilerParams(vmem_limit_bytes=48 << 20),
-        cost_estimate=pl.CostEstimate(flops=10**10, bytes_accessed=12 << 20, transcendentals=6 * 10**6),
+        compiler_params=pltpu.CompilerParams(vmem_limit_bytes=22 << 20),
+        cost_estimate=pl.CostEstimate(
+            flops=10**7 * sum(a.shape[1] for a in ks), bytes_accessed=8 << 20, transcendentals=3 * 10**6
+        ),
         name="attend",
     )(near, far, *ks, *vs, *tails)
 
@@ -228,9 +233,9 @@
     return functools.reduce(jnp.add, terms)
 
 
-def merge_kernel(near_ref, far_ref, *out_refs):
-    for i, out_ref in enumerate(out_refs, 1):
-        parts = [near_ref.at[i], far_ref.at[i]]
+def merge_kernel(n_parts, *refs):
+    for i, out_ref in enumerate(refs[n_parts:], 1):
+        parts = [ref.at[i] for ref in refs[:n_parts]]
         stats = [unpacked(p[:, HEADS * D_VAL :]) for p in parts]
         best = functools.reduce(jnp.maximum, stats)
         shares = [jnp.exp2(s - best) for s in stats]
@@ -242,8 +247,8 @@
             out_ref[:, h * D_VAL : (h + 1) * D_VAL] = mix(parts, shares, slice(0, TOK), h).astype(jnp.bfloat16)
 
 
-def combine_kernel(pos_ref, near_ref, far_ref, *refs):
-    parts, out_ref = [near_ref.at[0], far_ref.at[0], *refs[:-1]], refs[-1]
+def combine_kernel(n_local, pos_ref, *refs):
+    parts, out_ref = [ref.at[0] for ref in refs[:n_local]] + list(refs[n_local:-1]), refs[-1]
     stats = [unpacked(p[:, HEADS * D_VAL :]) for p in parts]
     best = functools.reduce(jnp.maximum, stats)
     shares = [jnp.exp2(s - best) for s in stats]
@@ -262,7 +267,6 @@
 
 
 def body(q_nope, q_rope, kv_compressed, token_pos, kv_gain, w_uk, w_uv):
-    scale = LOG2E / math.sqrt(D_NOPE + 64)
     spans, steps = rotations()
     low_span = lambda i, pos: (jnp.minimum(pos[0], pos[RUN]) // RUN, 0, 0)
     high_span = lambda i, pos: (jnp.maximum(pos[0], pos[RUN]) // RUN, 0, 0)
@@ -294,42 +298,62 @@
     across = lambda block, by: lax.ppermute(block, ACROSS, shift(X_SIZE, by))
     along = lambda block, by: lax.ppermute(block, "z", shift(Z_SIZE, by))
 
-    along_y = [key_rows] + [lax.ppermute(key_rows, "y", shift(Y_SIZE, by)) for by in (1, -1, 2)]
-    mine = jnp.stack(along_y)
-    mine, q_rows = lax.optimization_barrier((mine, q_rows))
+    along_y = [lax.ppermute(key_rows, "y", shift(Y_SIZE, by)) for by in (1, -1, 2)]
+    mine = jnp.stack([key_rows] + along_y)
+    from_left = across(q_rows, 1)
+    mine, q_rows, from_left = lax.optimization_barrier((mine, q_rows, from_left))
 
     up, down = along(mine, 1), along(mine, -1)
-    near = jnp.stack([q_rows] + [across(q_rows, by) for by in (1, -1, 2)])
+    opposite = across(q_rows, 2)
+    first = [expand([mine], w_uk, w_uv)]
+    up, down, opposite, q_rows, first = lax.optimization_barrier((up, down, opposite, q_rows, first))
+
+    blocks = [up, down]
+    up, down = along(up, 1), along(down, -1)
+    from_right = across(q_rows, -1)
+    first.append(expand(blocks, w_uk, w_uv))
+    up, down, from_right, first = lax.optimization_barrier((up, down, from_right, first))
+
+    blocks = [up, down]
+    up, down = along(up, 1), along(down, -1)
+    near = jnp.stack([q_rows, from_left, from_right, opposite])
     far = swap(near)
-    chunks = [expand([mine], w_uk, w_uv)]
-    up, down, near, chunks = lax.optimization_barrier((up, down, near, chunks))
-    for hop in range(2, Z_SIZE // 2 + 1):
-        blocks = [up, down]
-        if hop == Z_SIZE // 2:
-            up, down = up[: Y_SIZE // 2], down[Y_SIZE // 2 :]
-        up, down = along(up, 1), along(down, -1)
-        chunks.append(expand(blocks, w_uk, w_uv))
-        up, down, chunks = lax.optimization_barrier((up, down, chunks))
-    chunks.append(expand([up, down], w_uk, w_uv))
-
-    near, far = attend(near, far, chunks, scale)
-    far = swap(far)
+    second = [expand(blocks, w_uk, w_uv)]
+    partials = [attend(near, far, first, True)]
+    up, down, second, partials = lax.optimization_barrier((up, down, second, partials))
+
+    blocks = [up, down]
+    half = Y_SIZE // 2
+    up, down = along(up[:half], 1), along(down[half:], -1)
+    crossed = [swap(partials[0][1])]
+    third = [expand(blocks, w_uk, w_uv)]
+    partials.append(attend(near, far, second, False))
+    up, down, third, partials, crossed = lax.optimization_barrier((up, down, third, partials, crossed))
+
+    third.append(expand([up, down], w_uk, w_uv))
+    crossed.append(swap(partials[1][1]))
+    partials.append(attend(near, far, third, False))
+    crossed.append(swap(partials[2][1]))
+
+    local = [p[0] for p in partials] + crossed
     part = jax.ShapeDtypeStruct((TOK, OUT_ROW), jnp.bfloat16)
     merged = pl.pallas_call(
-        merge_kernel,
-        in_specs=[VMEM] * 2,
+        functools.partial(merge_kernel, len(local)),
+        in_specs=[VMEM] * len(local),
         out_specs=[VMEM] * 3,
         out_shape=[part] * 3,
+        compiler_params=pltpu.CompilerParams(vmem_limit_bytes=8 << 20),
         name="merge",
-    )(near, far)
+    )(*local)
     back = [across(m, by) for m, by in zip(merged, (-1, 1, 2))]
     return pl.pallas_call(
-        combine_kernel,
-        in_specs=[SMEM] + [VMEM] * 5,
+        functools.partial(combine_kernel, len(local)),
+        in_specs=[SMEM] + [VMEM] * (len(local) + 3),
         out_specs=VMEM,
         out_shape=jax.ShapeDtypeStruct((TOK, HEADS * D_VAL), jnp.bfloat16),
+        compiler_params=pltpu.CompilerParams(vmem_limit_bytes=8 << 20),
         name="combine",
-    )(token_pos, near, far, *back)
+    )(token_pos, *local, *back)
 
 
 def solution(mesh):

time: 100 us -> 89.3 us (0.89)
  waiting for transfers between devices: 27.9 us -> 19.1 us
  local copies, waits for them, and re-layouts: 6.24 us -> 1.27 us
  Pallas kernels: 29.1 us -> 31.8 us
    ppermute x8, waiting for transfers between devices: 13.1 us -> 1.31 us  [body(): along = lambda block, by: lax.ppermute(block, 'z', shift(Z_SIZE, by))]
    unnamed x28 -> x10, local copies, waits for them, and re-layouts: 6.21 us -> 1.24 us
    ppermute x6, waiting for transfers between devices: 8.55 us -> 11.8 us  [body(): across = lambda block, by: lax.ppermute(block, ACROSS, shift(X_SIZE, by))]
    ppermute x6, starting transfers between devices: 7.03 us -> 9.99 us  [body(): across = lambda block, by: lax.ppermute(block, ACROSS, shift(X_SIZE, by))]
    pallas_call x3 -> x5, Pallas kernels: 20.5 us -> 23.2 us  [the longest x3 18.7 us: attend(): pl.pallas_call(functools.partial(attend_kernel, len(chunks), own), grid=(...]
    ppermute x2 -> x4, starting transfers between devices: 9.9 us -> 7.52 us  [body(): swap = lambda block: lax.ppermute(block, 'core', [(0, 1), (1, 0)])]
  transfers between devices with their start and end apart: 19 -> 21, of which waited for: 12 -> 9; matrix products, arithmetic and copies ran while one was open for 0% -> 1% of each run, Pallas kernels for 6% -> 28%
where the time goes in v2:
time: 89.3 us; the launch traced here: 89.1 us
  starting transfers between devices  35.6 us (40%)
  Pallas kernels  31.8 us (36%)
  waiting for transfers between devices  19.1 us (21%)
  local copies, waits for them, and re-layouts  1.27 us (1%)
  other arithmetic  1.11 us (1%)
    pallas_call x3, Pallas kernels, attend(): pl.pallas_call(functools.partial(attend_kernel, len(chunks), own), grid=(...  18.7 us
    ppermute x8, starting transfers between devices, body(): along = lambda block, by: lax.ppermute(block, 'z', shift(Z_SIZE, by))  13.8 us
    ppermute x6, waiting for transfers between devices, body(): across = lambda block, by: lax.ppermute(block, ACROSS, shift(X_SIZE, by))  11.8 us
    ppermute x6, starting transfers between devices, body(): across = lambda block, by: lax.ppermute(block, ACROSS, shift(X_SIZE, by))  9.99 us
    ppermute x4, starting transfers between devices, body(): swap = lambda block: lax.ppermute(block, 'core', [(0, 1), (1, 0)])  7.52 us
    pallas_call x5, Pallas kernels, expand(): pl.pallas_call(functools.partial(expand_kernel, len(blocks)), in_specs=[V...  5.92 us
    ppermute x3, starting transfers between devices, body(): lax.ppermute(key_rows, 'y', shift(Y_SIZE, by))  4.38 us
    ppermute x3, waiting for transfers between devices, body(): lax.ppermute(key_rows, 'y', shift(Y_SIZE, by))  4.02 us
  transfers between devices with their start and end apart: 21, of which 9 were waited for; matrix products, arithmetic and copies ran while one was open for 1% of the time, Pallas kernels for 28%

profile of v2, /device:TPU:1, one launch (start us, length us, event | category | flops | bytes accessed | tf_op | source)
XLA Modules:
  0.0 89.1 jit_solution(17904827585749462511)
XLA Ops:
  0.0 0.0 copy-start
  0.0 2.7 %rows.1 = (bf16[64,640]{1,0:T(8,128)(2,1)}, bf16[64,1664]{1,0:T(8,128)(2,1)}) custom-call(s32[64]{0:T(128)} %pos_ref.3, f32[512,2,128]{2,1,0:T(2,128)} %constant.4.clone.low_ref.high_ref, f32[512,2,128]{2,1,0:T(2,128)} %constant.4.clone.low_ref.high_ref, f32[2,32,128]{2,1,0:T(8,128)} %constant.5.clone.step_ref, bf16[64,1024]{1,0:T(8,128)(2,1)} %qn_ref.1, ...), custom_call_target="tpu_custom_call" | custom-call | tf_op jit(solution)/shard_map/rows/pallas_call | solution.py:274
  2.7 2.0 %collective-permute-start.3 = (bf16[64,1664]{1,0:T(8,128)(2,1)}, bf16[64,1664]{1,0:T(8,128)(2,1)S(1)}, u32[]{:S(2)}, u32[]{:S(2)}) collective-permute-start(bf16[64,1664]{1,0:T(8,128)(2,1)} %get-tuple-element.75), channel_id=1, source_target_pairs={{0,1},{1,128},{128,129},{129,0},{2,3},{3,130},{130,131},{131,2},{4... | collective-permute-start | bytes 638984 | tf_op jit(solution)/shard_map/ppermute | solution.py:298
  4.7 2.9 %collective-permute-start.2 = (bf16[64,640]{1,0:T(8,128)(2,1)}, bf16[64,640]{1,0:T(8,128)(2,1)S(1)}, u32[]{:S(2)}, u32[]{:S(2)}) collective-permute-start(bf16[64,640]{1,0:T(8,128)(2,1)} %get-tuple-element.66), channel_id=1, source_target_pairs={{0,32},{16,48},{32,0},{48,16},{1,33},{17,49},{33,1},{49,17},{2,34}... | collective-permute-start | bytes 245768 | tf_op jit(solution)/shard_map/ppermute | solution.py:301
  7.6 0.8 collective-permute-start.1
  8.4 0.7 collective-permute-start
  9.1 0.6 collective-permute-done.2
  9.7 2.3 %collective-permute-done.1 = bf16[64,640]{1,0:T(8,128)(2,1)S(1)} collective-permute-done((bf16[64,640]{1,0:T(8,128)(2,1)}, bf16[64,640]{1,0:T(8,128)(2,1)S(1)}, u32[]{:S(2)}, u32[]{:S(2)}) %collective-permute-start.1) | collective-permute-done | bytes 81952 | tf_op jit(solution)/shard_map/ppermute | solution.py:301
  12.0 1.1 %collective-permute-done = bf16[64,640]{1,0:T(8,128)(2,1)S(1)} collective-permute-done((bf16[64,640]{1,0:T(8,128)(2,1)}, bf16[64,640]{1,0:T(8,128)(2,1)S(1)}, u32[]{:S(2)}, u32[]{:S(2)}) %collective-permute-start) | collective-permute-done | bytes 81952 | tf_op jit(solution)/shard_map/ppermute | solution.py:301
  13.1 0.0 copy-start.4
  13.1 1.0 %pad_maximum_fusion.1.refs_0_ = bf16[4,64,640]{2,1,0:T(8,128)(2,1)S(1)} fusion(bf16[1,64,640]{2,1,0:T(8,128)(2,1)S(1)} %bitcast.20, bf16[1,64,640]{2,1,0:T(8,128)(2,1)S(1)} %bitcast.21, bf16[1,64,640]{2,1,0:T(8,128)(2,1)S(1)} %bitcast.22, bf16[1,64,640]{2,1,0:T(8,128)(2,1)} %bitcast.19), kind=kLoop, calls=%fused_computation.1 | loop fusion | flops 491520 | bytes 655360 | tf_op jit(solution)/shard_map/stack | solution.py:302
  14.1 0.0 collective-permute-done.3
  14.1 5.7 %collective-permute-start.5 = (bf16[4,64,640]{2,1,0:T(8,128)(2,1)S(1)}, bf16[4,64,640]{2,1,0:T(8,128)(2,1)S(1)}, u32[]{:S(2)}, u32[]{:S(2)}) collective-permute-start(bf16[4,64,640]{2,1,0:T(8,128)(2,1)S(1)} %pad_maximum_fusion.1.refs_0_), channel_id=1, source_target_pairs={{0,14},{2,0},{4,2},{6,4},{8,6},{10,8},{12,10},{14,12},{1,15},{3,1}... | collective-permute-start | bytes 983048 | tf_op jit(solution)/shard_map/ppermute | solution.py:299
  19.8 0.0 collective-permute-start.4
  19.8 0.0 copy-done.4
  19.8 2.5 %collective-permute-start.6 = (bf16[64,1664]{1,0:T(8,128)(2,1)S(1)}, bf16[64,1664]{1,0:T(8,128)(2,1)S(1)}, u32[]{:S(2)}, u32[]{:S(2)}) collective-permute-start(bf16[64,1664]{1,0:T(8,128)(2,1)S(1)} %copy-done.4), channel_id=1, source_target_pairs={{0,128},{1,129},{128,0},{129,1},{2,130},{3,131},{130,2},{131,3},{4... | collective-permute-start | bytes 638984 | tf_op jit(solution)/shard_map/ppermute | solution.py:298
  22.2 0.0 copy-done
  22.2 0.0 copy-start.1
  22.2 1.2 %copy-done.1 = bf16[8,512,128]{2,1,0:T(8,128)(2,1)S(1)} copy-done((bf16[8,512,128]{2,1,0:T(8,128)(2,1)S(1)}, bf16[8,512,128]{2,1,0:T(8,128)(2,1)}, u32[]{:S(2)}) %copy-start.1) | copy-done | bytes 1048600
  23.4 1.1 %expand.5 = (bf16[2,128,1024]{2,1,0:T(8,128)(2,1)S(1)}, bf16[2,128,1024]{2,1,0:T(8,128)(2,1)S(1)}, bf16[2,128,128]{2,1,0:T(8,128)(2,1)S(1)}) custom-call(bf16[4,64,640]{2,1,0:T(8,128)(2,1)S(1)} %pad_maximum_fusion.1.refs_0_, bf16[1024,512]{1,0:T(8,128)(2,1)S(1)} %bitcast.10, bf16[8,512,128]{2,1,0:T(8,128)(2,1)S(1)} %copy-done.1), custom_call_target="tpu_custom_call" | custom-call | flops 536870912 | bytes 3633152 | tf_op jit(solution)/shard_map/expand/pallas_call | solution.py:107
  24.5 1.4 %collective-permute-done.6 = bf16[64,1664]{1,0:T(8,128)(2,1)S(1)} collective-permute-done((bf16[64,1664]{1,0:T(8,128)(2,1)S(1)}, bf16[64,1664]{1,0:T(8,128)(2,1)S(1)}, u32[]{:S(2)}, u32[]{:S(2)}) %collective-permute-start.6) | collective-permute-done | bytes 213024 | tf_op jit(solution)/shard_map/ppermute | solution.py:298
  26.0 0.0 collective-permute-done.5.refs_1_
  26.0 1.3 %collective-permute-done.4.refs_0_ = bf16[4,64,640]{2,1,0:T(8,128)(2,1)S(1)} collective-permute-done((bf16[4,64,640]{2,1,0:T(8,128)(2,1)S(1)}, bf16[4,64,640]{2,1,0:T(8,128)(2,1)S(1)}, u32[]{:S(2)}, u32[]{:S(2)}) %collective-permute-start.4) | collective-permute-done | bytes 327712 | tf_op jit(solution)/shard_map/ppermute | solution.py:299
  27.2 0.0 collective-permute-start.7
  27.2 2.7 %collective-permute-start.8 = (bf16[4,64,640]{2,1,0:T(8,128)(2,1)S(1)}, bf16[4,64,640]{2,1,0:T(8,128)(2,1)S(1)}, u32[]{:S(2)}, u32[]{:S(2)}) collective-permute-start(bf16[4,64,640]{2,1,0:T(8,128)(2,1)S(1)} %collective-permute-done.5.refs_1_), channel_id=1, source_target_pairs={{0,14},{2,0},{4,2},{6,4},{8,6},{10,8},{12,10},{14,12},{1,15},{3,1}... | collective-permute-start | bytes 983048 | tf_op jit(solution)/shard_map/ppermute | solution.py:299
  29.9 1.5 %collective-permute-start.9 = (bf16[64,1664]{1,0:T(8,128)(2,1)S(1)}, bf16[64,1664]{1,0:T(8,128)(2,1)S(1)}, u32[]{:S(2)}, u32[]{:S(2)}) collective-permute-start(bf16[64,1664]{1,0:T(8,128)(2,1)S(1)} %copy-done.4), channel_id=1, source_target_pairs={{0,129},{1,0},{128,1},{129,128},{2,131},{3,2},{130,3},{131,130},{4... | collective-permute-start | bytes 638984 | tf_op jit(solution)/shard_map/ppermute | solution.py:298
  31.4 1.3 %expand.6 = (bf16[2,256,1024]{2,1,0:T(8,128)(2,1)S(1)}, bf16[2,256,1024]{2,1,0:T(8,128)(2,1)S(1)}, bf16[2,256,128]{2,1,0:T(8,128)(2,1)S(1)}) custom-call(bf16[4,64,640]{2,1,0:T(8,128)(2,1)S(1)} %collective-permute-done.4.refs_0_, bf16[4,64,640]{2,1,0:T(8,128)(2,1)S(1)} %collective-permute-done.5.refs_1_, bf16[1024,512]{1,0:T(8,128)(2,1)S(1)} %bitcast.11, ...), custom_call_target="tpu_custom_call" | custom-call | flops 1073741824 | bytes 5169152 | tf_op jit(solution)/shard_map/expand/pallas_call | solution.py:107
  32.6 0.0 copy-start.2
  32.7 2.2 %collective-permute-done.9 = bf16[64,1664]{1,0:T(8,128)(2,1)S(1)} collective-permute-done((bf16[64,1664]{1,0:T(8,128)(2,1)S(1)}, bf16[64,1664]{1,0:T(8,128)(2,1)S(1)}, u32[]{:S(2)}, u32[]{:S(2)}) %collective-permute-start.9) | collective-permute-done | bytes 213024 | tf_op jit(solution)/shard_map/ppermute | solution.py:298
  34.9 0.0 collective-permute-done.7.refs_0_
  34.9 0.0 collective-permute-done.8.refs_1_
  34.9 0.1 pad_maximum_fusion.refs_0_
  35.0 5.4 %collective-permute-start.12 = (bf16[4,64,1664]{2,1,0:T(8,128)(2,1)S(1)}, bf16[4,64,1664]{2,1,0:T(8,128)(2,1)S(1)}, u32[]{:S(2)}, u32[]{:S(2)}) collective-permute-start(bf16[4,64,1664]{2,1,0:T(8,128)(2,1)S(1)} %pad_maximum_fusion.refs_0_), channel_id=1, source_target_pairs={{0,64},{64,0},{1,65},{65,1},{2,66},{66,2},{3,67},{67,3},{4,68},{68... | collective-permute-start | bytes 2555912 | tf_op jit(solution)/shard_map/ppermute | solution.py:297
  40.4 0.0 collective-permute-start.10
  40.4 2.7 %collective-permute-start.11 = (bf16[4,64,640]{2,1,0:T(8,128)(2,1)S(1)}, bf16[4,64,640]{2,1,0:T(8,128)(2,1)S(1)}, u32[]{:S(2)}, u32[]{:S(2)}) collective-permute-start(bf16[4,64,640]{2,1,0:T(8,128)(2,1)S(1)} %collective-permute-done.8.refs_1_), channel_id=1, source_target_pairs={{0,14},{2,0},{4,2},{6,4},{8,6},{10,8},{12,10},{14,12},{1,15},{3,1}... | collective-permute-start | bytes 983048 | tf_op jit(solution)/shard_map/ppermute | solution.py:299
  43.1 0.0 copy-done.2
  43.1 1.3 %expand.7 = (bf16[2,256,1024]{2,1,0:T(8,128)(2,1)S(1)}, bf16[2,256,1024]{2,1,0:T(8,128)(2,1)S(1)}, bf16[2,256,128]{2,1,0:T(8,128)(2,1)S(1)}) custom-call(bf16[4,64,640]{2,1,0:T(8,128)(2,1)S(1)} %collective-permute-done.7.refs_0_, bf16[4,64,640]{2,1,0:T(8,128)(2,1)S(1)} %collective-permute-done.8.refs_1_, bf16[1024,512]{1,0:T(8,128)(2,1)S(1)} %bitcast.12, ...), custom_call_target="tpu_custom_call" | custom-call | flops 1073741824 | bytes 5169152 | tf_op jit(solution)/shard_map/expand/pallas_call | solution.py:107
  44.4 0.0 collective-permute-done.12.refs_1_
  44.4 6.7 %attend.3 = (bf16[4,64,1152]{2,1,0:T(8,128)(2,1)S(1)}, bf16[4,64,1152]{2,1,0:T(8,128)(2,1)S(1)}) custom-call(bf16[4,64,1664]{2,1,0:T(8,128)(2,1)S(1)} %pad_maximum_fusion.refs_0_, bf16[4,64,1664]{2,1,0:T(8,128)(2,1)S(1)} %collective-permute-done.12.refs_1_, bf16[2,128,1024]{2,1,0:T(8,128)(2,1)S(1)} %get-tuple-element.90.refs_2_, ...), custom_call_target="tpu_custom_call" | custom-call | flops 3840000000 | bytes 8388608 | tf_op jit(solution)/shard_map/attend/pallas_call | solution.py:213
  51.0 0.0 collective-permute-done.10.refs_0_
  51.1 0.0 collective-permute-done.11.refs_1_
  51.1 0.7 collective-permute-start.15
  51.8 2.7 %collective-permute-start.14 = (bf16[2,64,640]{2,1,0:T(8,128)(2,1)S(1)}, bf16[2,64,640]{2,1,0:T(8,128)(2,1)S(1)}, u32[]{:S(2)}, u32[]{:S(2)}) collective-permute-start(bf16[2,64,640]{2,1,0:T(8,128)(2,1)S(1)} %slice.7), channel_id=1, source_target_pairs={{0,14},{2,0},{4,2},{6,4},{8,6},{10,8},{12,10},{14,12},{1,15},{3,1}... | collective-permute-start | bytes 491528 | tf_op jit(solution)/shard_map/ppermute | solution.py:299
  54.6 0.0 collective-permute-start.13
  54.6 5.4 %attend.4 = (bf16[4,64,1152]{2,1,0:T(8,128)(2,1)S(1)}, bf16[4,64,1152]{2,1,0:T(8,128)(2,1)S(1)}) custom-call(bf16[4,64,1664]{2,1,0:T(8,128)(2,1)S(1)} %pad_maximum_fusion.refs_0_, bf16[4,64,1664]{2,1,0:T(8,128)(2,1)S(1)} %collective-permute-done.12.refs_1_, bf16[2,256,1024]{2,1,0:T(8,128)(2,1)S(1)} %get-tuple-element.105.refs_2_, ...), custom_call_target="tpu_custom_call" | custom-call | flops 2560000000 | bytes 8388608 | tf_op jit(solution)/shard_map/attend/pallas_call | solution.py:213
  60.0 1.3 %expand.8 = (bf16[2,256,1024]{2,1,0:T(8,128)(2,1)S(1)}, bf16[2,256,1024]{2,1,0:T(8,128)(2,1)S(1)}, bf16[2,256,128]{2,1,0:T(8,128)(2,1)S(1)}) custom-call(bf16[4,64,640]{2,1,0:T(8,128)(2,1)S(1)} %collective-permute-done.10.refs_0_, bf16[4,64,640]{2,1,0:T(8,128)(2,1)S(1)} %collective-permute-done.11.refs_1_, bf16[1024,512]{1,0:T(8,128)(2,1)S(1)} %bitcast.13, ...), custom_call_target="tpu_custom_call" | custom-call | flops 1073741824 | bytes 5169152 | tf_op jit(solution)/shard_map/expand/pallas_call | solution.py:107
  61.2 0.0 collective-permute-done.14.refs_1_
  61.2 0.0 collective-permute-done.13.refs_0_
  61.3 0.0 collective-permute-done.15.refs_3_
  61.3 1.1 %collective-permute-start.16 = (bf16[4,64,1152]{2,1,0:T(8,128)(2,1)S(1)}, bf16[4,64,1152]{2,1,0:T(8,128)(2,1)S(1)}, u32[]{:S(2)}, u32[]{:S(2)}) collective-permute-start(bf16[4,64,1152]{2,1,0:T(8,128)(2,1)S(1)} %get-tuple-element.122), channel_id=1, source_target_pairs={{0,64},{64,0},{1,65},{65,1},{2,66},{66,2},{3,67},{67,3},{4,68},{68... | collective-permute-start | bytes 1769480 | tf_op jit(solution)/shard_map/ppermute | solution.py:297
  62.4 1.1 %expand.9 = (bf16[2,128,1024]{2,1,0:T(8,128)(2,1)S(1)}, bf16[2,128,1024]{2,1,0:T(8,128)(2,1)S(1)}, bf16[2,128,128]{2,1,0:T(8,128)(2,1)S(1)}) custom-call(bf16[2,64,640]{2,1,0:T(8,128)(2,1)S(1)} %collective-permute-done.13.refs_0_, bf16[2,64,640]{2,1,0:T(8,128)(2,1)S(1)} %collective-permute-done.14.refs_1_, bf16[1024,512]{1,0:T(8,128)(2,1)S(1)} %bitcast.14, ...), custom_call_target="tpu_custom_call" | custom-call | flops 536870912 | bytes 3633152 | tf_op jit(solution)/shard_map/expand/pallas_call | solution.py:107
  63.5 6.6 %attend.5 = (bf16[4,64,1152]{2,1,0:T(8,128)(2,1)S(1)}, bf16[4,64,1152]{2,1,0:T(8,128)(2,1)S(1)}) custom-call(bf16[4,64,1664]{2,1,0:T(8,128)(2,1)S(1)} %pad_maximum_fusion.refs_0_, bf16[4,64,1664]{2,1,0:T(8,128)(2,1)S(1)} %collective-permute-done.12.refs_1_, bf16[2,256,1024]{2,1,0:T(8,128)(2,1)S(1)} %get-tuple-element.112.refs_2_, ...), custom_call_target="tpu_custom_call" | custom-call | flops 3840000000 | bytes 8388608 | tf_op jit(solution)/shard_map/attend/pallas_call | solution.py:213
  70.1 0.3 collective-permute-start.17
  70.4 0.0 collective-permute-done.16.refs_4_
  70.4 2.0 %collective-permute-done.17.refs_5_ = bf16[4,64,1152]{2,1,0:T(8,128)(2,1)S(1)} collective-permute-done((bf16[4,64,1152]{2,1,0:T(8,128)(2,1)S(1)}, bf16[4,64,1152]{2,1,0:T(8,128)(2,1)S(1)}, u32[]{:S(2)}, u32[]{:S(2)}) %collective-permute-start.17) | collective-permute-done | bytes 589856 | tf_op jit(solution)/shard_map/ppermute | solution.py:297
  72.4 2.5 %merge.1 = (bf16[64,1152]{1,0:T(8,128)(2,1)S(1)}, bf16[64,1152]{1,0:T(8,128)(2,1)S(1)}, bf16[64,1152]{1,0:T(8,128)(2,1)S(1)}) custom-call(bf16[4,64,1152]{2,1,0:T(8,128)(2,1)S(1)} %get-tuple-element.110.refs_0_, bf16[4,64,1152]{2,1,0:T(8,128)(2,1)S(1)} %get-tuple-element.111.refs_1_, bf16[4,64,1152]{2,1,0:T(8,128)(2,1)S(1)} %get-tuple-element.120.refs_2_, ...), custom_call_target="tpu_custom_call" | custom-call | tf_op jit(solution)/shard_map/merge/pallas_call | solution.py:340
  74.9 2.8 %collective-permute-start.18 = (bf16[64,1152]{1,0:T(8,128)(2,1)S(1)}, bf16[64,1152]{1,0:T(8,128)(2,1)S(1)}, u32[]{:S(2)}, u32[]{:S(2)}) collective-permute-start(bf16[64,1152]{1,0:T(8,128)(2,1)S(1)} %get-tuple-element.124), channel_id=1, source_target_pairs={{0,129},{1,0},{128,1},{129,128},{2,131},{3,2},{130,3},{131,130},{4... | collective-permute-start | bytes 442376 | tf_op jit(solution)/shard_map/ppermute | solution.py:298
  77.7 0.0 collective-permute-start.19
  77.7 1.3 %collective-permute-start.20 = (bf16[64,1152]{1,0:T(8,128)(2,1)S(1)}, bf16[64,1152]{1,0:T(8,128)(2,1)S(1)}, u32[]{:S(2)}, u32[]{:S(2)}) collective-permute-start(bf16[64,1152]{1,0:T(8,128)(2,1)S(1)} %get-tuple-element.126), channel_id=1, source_target_pairs={{0,128},{1,129},{128,0},{129,1},{2,130},{3,131},{130,2},{131,3},{4... | collective-permute-start | bytes 442376 | tf_op jit(solution)/shard_map/ppermute | solution.py:298
  78.9 1.8 %collective-permute-done.18.refs_6_ = bf16[64,1152]{1,0:T(8,128)(2,1)S(1)} collective-permute-done((bf16[64,1152]{1,0:T(8,128)(2,1)S(1)}, bf16[64,1152]{1,0:T(8,128)(2,1)S(1)}, u32[]{:S(2)}, u32[]{:S(2)}) %collective-permute-start.18) | collective-permute-done | bytes 147488 | tf_op jit(solution)/shard_map/ppermute | solution.py:298
  80.8 6.3 %collective-permute-done.19.refs_7_ = bf16[64,1152]{1,0:T(8,128)(2,1)S(1)} collective-permute-done((bf16[64,1152]{1,0:T(8,128)(2,1)S(1)}, bf16[64,1152]{1,0:T(8,128)(2,1)S(1)}, u32[]{:S(2)}, u32[]{:S(2)}) %collective-permute-start.19) | collective-permute-done | bytes 147488 | tf_op jit(solution)/shard_map/ppermute | solution.py:298
  87.0 0.0 collective-permute-done.20.refs_8_
  87.0 0.0 copy-done.3
  87.0 2.1 %combine.1 = bf16[64,1024]{1,0:T(8,128)(2,1)} custom-call(s32[64]{0:T(128)S(1)} %copy-done.3, bf16[4,64,1152]{2,1,0:T(8,128)(2,1)S(1)} %get-tuple-element.110.refs_0_, bf16[4,64,1152]{2,1,0:T(8,128)(2,1)S(1)} %get-tuple-element.111.refs_1_, bf16[4,64,1152]{2,1,0:T(8,128)(2,1)S(1)} %get-tuple-element.120.refs_2_, ...), custom_call_target="tpu_custom_call" | custom-call | tf_op jit(solution)/shard_map/combine/pallas_call | solution.py:349
  (3 shorter events, 0.0 us)
Async XLA Ops:
  0.0 22.2 %copy-start = (bf16[8,128,512]{2,1,0:T(8,128)(2,1)S(1)}, bf16[8,128,512]{2,1,0:T(8,128)(2,1)}, u32[]{:S(2)}) copy-start(bf16[8,128,512]{2,1,0:T(8,128)(2,1)} %param.14) | copy-start | bytes 3145732
  2.7 11.4 %collective-permute-start.3 = (bf16[64,1664]{1,0:T(8,128)(2,1)}, bf16[64,1664]{1,0:T(8,128)(2,1)S(1)}, u32[]{:S(2)}, u32[]{:S(2)}) collective-permute-start(bf16[64,1664]{1,0:T(8,128)(2,1)} %get-tuple-element.75), channel_id=1, source_target_pairs={{0,1},{1,128},{128,129},{129,0},{2,3},{3,130},{130,131},{131,2},{4... | collective-permute-start | bytes 638984 | tf_op jit(solution)/shard_map/ppermute | solution.py:298
  4.7 5.0 %collective-permute-start.2 = (bf16[64,640]{1,0:T(8,128)(2,1)}, bf16[64,640]{1,0:T(8,128)(2,1)S(1)}, u32[]{:S(2)}, u32[]{:S(2)}) collective-permute-start(bf16[64,640]{1,0:T(8,128)(2,1)} %get-tuple-element.66), channel_id=1, source_target_pairs={{0,32},{16,48},{32,0},{48,16},{1,33},{17,49},{33,1},{49,17},{2,34}... | collective-permute-start | bytes 245768 | tf_op jit(solution)/shard_map/ppermute | solution.py:301
  7.6 4.4 %collective-permute-start.1 = (bf16[64,640]{1,0:T(8,128)(2,1)}, bf16[64,640]{1,0:T(8,128)(2,1)S(1)}, u32[]{:S(2)}, u32[]{:S(2)}) collective-permute-start(bf16[64,640]{1,0:T(8,128)(2,1)} %get-tuple-element.66), channel_id=1, source_target_pairs={{0,48},{16,0},{32,16},{48,32},{1,49},{17,1},{33,17},{49,33},{2,50}... | collective-permute-start | bytes 245768 | tf_op jit(solution)/shard_map/ppermute | solution.py:301
  8.4 4.7 %collective-permute-start = (bf16[64,640]{1,0:T(8,128)(2,1)}, bf16[64,640]{1,0:T(8,128)(2,1)S(1)}, u32[]{:S(2)}, u32[]{:S(2)}) collective-permute-start(bf16[64,640]{1,0:T(8,128)(2,1)} %get-tuple-element.66), channel_id=1, source_target_pairs={{0,16},{16,32},{32,48},{48,0},{1,17},{17,33},{33,49},{49,1},{2,18}... | collective-permute-start | bytes 245768 | tf_op jit(solution)/shard_map/ppermute | solution.py:301
  13.1 6.7 %copy-start.4 = (bf16[64,1664]{1,0:T(8,128)(2,1)S(1)}, bf16[64,1664]{1,0:T(8,128)(2,1)}, u32[]{:S(2)}) copy-start(bf16[64,1664]{1,0:T(8,128)(2,1)} %get-tuple-element.75) | copy-start | bytes 638980
  14.1 11.9 %collective-permute-start.5 = (bf16[4,64,640]{2,1,0:T(8,128)(2,1)S(1)}, bf16[4,64,640]{2,1,0:T(8,128)(2,1)S(1)}, u32[]{:S(2)}, u32[]{:S(2)}) collective-permute-start(bf16[4,64,640]{2,1,0:T(8,128)(2,1)S(1)} %pad_maximum_fusion.1.refs_0_), channel_id=1, source_target_pairs={{0,14},{2,0},{4,2},{6,4},{8,6},{10,8},{12,10},{14,12},{1,15},{3,1}... | collective-permute-start | bytes 983048 | tf_op jit(solution)/shard_map/ppermute | solution.py:299
  19.8 7.5 %collective-permute-start.4 = (bf16[4,64,640]{2,1,0:T(8,128)(2,1)S(1)}, bf16[4,64,640]{2,1,0:T(8,128)(2,1)S(1)}, u32[]{:S(2)}, u32[]{:S(2)}) collective-permute-start(bf16[4,64,640]{2,1,0:T(8,128)(2,1)S(1)} %pad_maximum_fusion.1.refs_0_), channel_id=1, source_target_pairs={{0,2},{2,4},{4,6},{6,8},{8,10},{10,12},{12,14},{14,0},{1,3},{3,5},... | collective-permute-start | bytes 983048 | tf_op jit(solution)/shard_map/ppermute | solution.py:299
  19.8 6.2 %collective-permute-start.6 = (bf16[64,1664]{1,0:T(8,128)(2,1)S(1)}, bf16[64,1664]{1,0:T(8,128)(2,1)S(1)}, u32[]{:S(2)}, u32[]{:S(2)}) collective-permute-start(bf16[64,1664]{1,0:T(8,128)(2,1)S(1)} %copy-done.4), channel_id=1, source_target_pairs={{0,128},{1,129},{128,0},{129,1},{2,130},{3,131},{130,2},{131,3},{4... | collective-permute-start | bytes 638984 | tf_op jit(solution)/shard_map/ppermute | solution.py:298
  22.2 1.2 %copy-start.1 = (bf16[8,512,128]{2,1,0:T(8,128)(2,1)S(1)}, bf16[8,512,128]{2,1,0:T(8,128)(2,1)}, u32[]{:S(2)}) copy-start(bf16[8,512,128]{2,1,0:T(8,128)(2,1)} %refs_3_.7) | copy-start | bytes 3145732
  27.2 7.7 %collective-permute-start.7 = (bf16[4,64,640]{2,1,0:T(8,128)(2,1)S(1)}, bf16[4,64,640]{2,1,0:T(8,128)(2,1)S(1)}, u32[]{:S(2)}, u32[]{:S(2)}) collective-permute-start(bf16[4,64,640]{2,1,0:T(8,128)(2,1)S(1)} %collective-permute-done.4.refs_0_), channel_id=1, source_target_pairs={{0,2},{2,4},{4,6},{6,8},{8,10},{10,12},{12,14},{14,0},{1,3},{3,5},... | collective-permute-start | bytes 983048 | tf_op jit(solution)/shard_map/ppermute | solution.py:299
  27.2 7.7 %collective-permute-start.8 = (bf16[4,64,640]{2,1,0:T(8,128)(2,1)S(1)}, bf16[4,64,640]{2,1,0:T(8,128)(2,1)S(1)}, u32[]{:S(2)}, u32[]{:S(2)}) collective-permute-start(bf16[4,64,640]{2,1,0:T(8,128)(2,1)S(1)} %collective-permute-done.5.refs_1_), channel_id=1, source_target_pairs={{0,14},{2,0},{4,2},{6,4},{8,6},{10,8},{12,10},{14,12},{1,15},{3,1}... | collective-permute-start | bytes 983048 | tf_op jit(solution)/shard_map/ppermute | solution.py:299
  29.9 5.0 %collective-permute-start.9 = (bf16[64,1664]{1,0:T(8,128)(2,1)S(1)}, bf16[64,1664]{1,0:T(8,128)(2,1)S(1)}, u32[]{:S(2)}, u32[]{:S(2)}) collective-permute-start(bf16[64,1664]{1,0:T(8,128)(2,1)S(1)} %copy-done.4), channel_id=1, source_target_pairs={{0,129},{1,0},{128,1},{129,128},{2,131},{3,2},{130,3},{131,130},{4... | collective-permute-start | bytes 638984 | tf_op jit(solution)/shard_map/ppermute | solution.py:298
  32.6 10.5 %copy-start.2 = (bf16[8,512,128]{2,1,0:T(8,128)(2,1)S(1)}, bf16[8,512,128]{2,1,0:T(8,128)(2,1)}, u32[]{:S(2)}) copy-start(bf16[8,512,128]{2,1,0:T(8,128)(2,1)} %refs_3_.7) | copy-start | bytes 3145732
  35.0 9.3 %collective-permute-start.12 = (bf16[4,64,1664]{2,1,0:T(8,128)(2,1)S(1)}, bf16[4,64,1664]{2,1,0:T(8,128)(2,1)S(1)}, u32[]{:S(2)}, u32[]{:S(2)}) collective-permute-start(bf16[4,64,1664]{2,1,0:T(8,128)(2,1)S(1)} %pad_maximum_fusion.refs_0_), channel_id=1, source_target_pairs={{0,64},{64,0},{1,65},{65,1},{2,66},{66,2},{3,67},{67,3},{4,68},{68... | collective-permute-start | bytes 2555912 | tf_op jit(solution)/shard_map/ppermute | solution.py:297
  40.4 10.6 %collective-permute-start.10 = (bf16[4,64,640]{2,1,0:T(8,128)(2,1)S(1)}, bf16[4,64,640]{2,1,0:T(8,128)(2,1)S(1)}, u32[]{:S(2)}, u32[]{:S(2)}) collective-permute-start(bf16[4,64,640]{2,1,0:T(8,128)(2,1)S(1)} %collective-permute-done.7.refs_0_), channel_id=1, source_target_pairs={{0,2},{2,4},{4,6},{6,8},{8,10},{10,12},{12,14},{14,0},{1,3},{3,5},... | collective-permute-start | bytes 983048 | tf_op jit(solution)/shard_map/ppermute | solution.py:299
  40.4 10.6 %collective-permute-start.11 = (bf16[4,64,640]{2,1,0:T(8,128)(2,1)S(1)}, bf16[4,64,640]{2,1,0:T(8,128)(2,1)S(1)}, u32[]{:S(2)}, u32[]{:S(2)}) collective-permute-start(bf16[4,64,640]{2,1,0:T(8,128)(2,1)S(1)} %collective-permute-done.8.refs_1_), channel_id=1, source_target_pairs={{0,14},{2,0},{4,2},{6,4},{8,6},{10,8},{12,10},{14,12},{1,15},{3,1}... | collective-permute-start | bytes 983048 | tf_op jit(solution)/shard_map/ppermute | solution.py:299
  51.1 10.2 %collective-permute-start.15 = (bf16[4,64,1152]{2,1,0:T(8,128)(2,1)S(1)}, bf16[4,64,1152]{2,1,0:T(8,128)(2,1)S(1)}, u32[]{:S(2)}, u32[]{:S(2)}) collective-permute-start(bf16[4,64,1152]{2,1,0:T(8,128)(2,1)S(1)} %get-tuple-element.104), channel_id=1, source_target_pairs={{0,64},{64,0},{1,65},{65,1},{2,66},{66,2},{3,67},{67,3},{4,68},{68... | collective-permute-start | bytes 1769480 | tf_op jit(solution)/shard_map/ppermute | solution.py:297
  51.8 9.4 %collective-permute-start.14 = (bf16[2,64,640]{2,1,0:T(8,128)(2,1)S(1)}, bf16[2,64,640]{2,1,0:T(8,128)(2,1)S(1)}, u32[]{:S(2)}, u32[]{:S(2)}) collective-permute-start(bf16[2,64,640]{2,1,0:T(8,128)(2,1)S(1)} %slice.7), channel_id=1, source_target_pairs={{0,14},{2,0},{4,2},{6,4},{8,6},{10,8},{12,10},{14,12},{1,15},{3,1}... | collective-permute-start | bytes 491528 | tf_op jit(solution)/shard_map/ppermute | solution.py:299
  54.6 6.7 %collective-permute-start.13 = (bf16[2,64,640]{2,1,0:T(8,128)(2,1)S(1)}, bf16[2,64,640]{2,1,0:T(8,128)(2,1)S(1)}, u32[]{:S(2)}, u32[]{:S(2)}) collective-permute-start(bf16[2,64,640]{2,1,0:T(8,128)(2,1)S(1)} %slice.6), channel_id=1, source_target_pairs={{0,2},{2,4},{4,6},{6,8},{8,10},{10,12},{12,14},{14,0},{1,3},{3,5},... | collective-permute-start | bytes 491528 | tf_op jit(solution)/shard_map/ppermute | solution.py:299
  61.3 9.1 %collective-permute-start.16 = (bf16[4,64,1152]{2,1,0:T(8,128)(2,1)S(1)}, bf16[4,64,1152]{2,1,0:T(8,128)(2,1)S(1)}, u32[]{:S(2)}, u32[]{:S(2)}) collective-permute-start(bf16[4,64,1152]{2,1,0:T(8,128)(2,1)S(1)} %get-tuple-element.122), channel_id=1, source_target_pairs={{0,64},{64,0},{1,65},{65,1},{2,66},{66,2},{3,67},{67,3},{4,68},{68... | collective-permute-start | bytes 1769480 | tf_op jit(solution)/shard_map/ppermute | solution.py:297
  70.1 2.3 %collective-permute-start.17 = (bf16[4,64,1152]{2,1,0:T(8,128)(2,1)S(1)}, bf16[4,64,1152]{2,1,0:T(8,128)(2,1)S(1)}, u32[]{:S(2)}, u32[]{:S(2)}) collective-permute-start(bf16[4,64,1152]{2,1,0:T(8,128)(2,1)S(1)} %get-tuple-element.123), channel_id=1, source_target_pairs={{0,64},{64,0},{1,65},{65,1},{2,66},{66,2},{3,67},{67,3},{4,68},{68... | collective-permute-start | bytes 1769480 | tf_op jit(solution)/shard_map/ppermute | solution.py:297
  74.9 5.9 %collective-permute-start.18 = (bf16[64,1152]{1,0:T(8,128)(2,1)S(1)}, bf16[64,1152]{1,0:T(8,128)(2,1)S(1)}, u32[]{:S(2)}, u32[]{:S(2)}) collective-permute-start(bf16[64,1152]{1,0:T(8,128)(2,1)S(1)} %get-tuple-element.124), channel_id=1, source_target_pairs={{0,129},{1,0},{128,1},{129,128},{2,131},{3,2},{130,3},{131,130},{4... | collective-permute-start | bytes 442376 | tf_op jit(solution)/shard_map/ppermute | solution.py:298
  77.7 9.4 %copy-start.3 = (s32[64]{0:T(128)S(1)}, s32[64]{0:T(128)}, u32[]{:S(2)}) copy-start(s32[64]{0:T(128)} %pos_ref.3) | copy-start | bytes 772
  77.7 9.4 %collective-permute-start.19 = (bf16[64,1152]{1,0:T(8,128)(2,1)S(1)}, bf16[64,1152]{1,0:T(8,128)(2,1)S(1)}, u32[]{:S(2)}, u32[]{:S(2)}) collective-permute-start(bf16[64,1152]{1,0:T(8,128)(2,1)S(1)} %get-tuple-element.125), channel_id=1, source_target_pairs={{0,1},{1,128},{128,129},{129,0},{2,3},{3,130},{130,131},{131,2},{4... | collective-permute-start | bytes 442376 | tf_op jit(solution)/shard_map/ppermute | solution.py:298
  77.7 9.4 %collective-permute-start.20 = (bf16[64,1152]{1,0:T(8,128)(2,1)S(1)}, bf16[64,1152]{1,0:T(8,128)(2,1)S(1)}, u32[]{:S(2)}, u32[]{:S(2)}) collective-permute-start(bf16[64,1152]{1,0:T(8,128)(2,1)S(1)} %get-tuple-element.126), channel_id=1, source_target_pairs={{0,128},{1,129},{128,0},{129,1},{2,130},{3,131},{130,2},{131,3},{4... | collective-permute-start | bytes 442376 | tf_op jit(solution)/shard_map/ppermute | solution.py:298

commit v3 on v2

--- a/solution.py
+++ b/solution.py
@@ -135,88 +135,94 @@
     near_ref, far_ref = refs[:2]
     k_refs, v_refs, tail_refs = (refs[2 + i * n_chunks : 2 + (i + 1) * n_chunks] for i in range(3))
     outs, lse_scr = refs[2 + 3 * n_chunks : -1], refs[-1]
-    step = pl.program_id(0)
     lane = lanes(RUN)
     q_refs = [(ref, i) for ref in (near_ref, far_ref) for i in range(X_SIZE)]
-    q_at = pl.multiple_of(step * 256, 256)
-    rope_at = pl.multiple_of(HEADS * D_NOPE + step * 128, 128)
     tails = [jnp.concatenate([ref[half] for ref in tail_refs], axis=0) for half in range(2)]
     spans = jnp.max(tails[0].astype(jnp.float32), axis=0, keepdims=True)
     ones = jnp.ones((tails[0].shape[0], 128), jnp.bfloat16)
-    first_keys = tail_refs[0].shape[1]
-    shape = (Q_TILE, first_keys)
-    row, col = (lax.broadcasted_iota(jnp.int32, shape, d) for d in (0, 1))
+    row, col = (lax.broadcasted_iota(jnp.int32, (Q_TILE, 128), d) for d in (0, 1))
     later = (row < RUN) & (col < RUN) & (col > row)
-
-    @pl.when(step == 0)
-    def _():
-        lse_scr[...] = jnp.zeros_like(lse_scr)
-
+    runs = [slice(half * RUN, (half + 1) * RUN) for half in range(2)]
+    biases = []
     for half in range(2):
-        run = slice(half * RUN, (half + 1) * RUN)
-        nope = jnp.concatenate([ref[i, run, pl.ds(q_at, 256)] for ref, i in q_refs], axis=0)
-        ropes = [ref[i, run, pl.ds(rope_at, 128)].astype(jnp.float32) for ref, i in q_refs]
-        biases = []
+        biases.append([])
         for ref, i in q_refs:
             mine = ref[i, 0:16, Q_ROW - 128 :].astype(jnp.float32)[0:1]
             seen = (spans >= mine) if half else (spans <= mine)
-            biases.append(jnp.where(seen, 0.0, NEGATIVE))
+            biases[half].append(jnp.where(seen, 0.0, NEGATIVE))
+    lse_scr[...] = jnp.zeros_like(lse_scr)
+
+    def hide(score):
+        if not own:
+            return score
+        return jnp.concatenate([jnp.where(later, NEGATIVE, score[:, :128]), score[:, 128:]], axis=1)
+
+    def pair_of_heads(step, carry):
+        at = pl.multiple_of(step * 256, 256)
+        rope_at = pl.multiple_of(HEADS * D_NOPE + step * 128, 128)
+        nope = [jnp.concatenate([ref[i, run, pl.ds(at, 256)] for ref, i in q_refs], axis=0) for run in runs]
+        ropes = [[ref[i, run, pl.ds(rope_at, 128)].astype(jnp.float32) for ref, i in q_refs] for run in runs]
+        k_pair = [jnp.concatenate([ref[half, :, pl.ds(at, 256)] for ref in k_refs], axis=0) for half in range(2)]
+        v_pair = [jnp.concatenate([ref[half, :, pl.ds(at, 256)] for ref in v_refs], axis=0) for half in range(2)]
+        scores = []
         for inner in range(2):
             cols = slice(inner * 128, (inner + 1) * 128)
-            turned_by = [pltpu.roll(r, 64, 1) if inner else r for r in ropes]
-            ends = lambda fill: jnp.concatenate(
-                [jnp.where(lane < 64, r, f) for r, f in zip(turned_by, fill)], axis=0
-            ).astype(jnp.bfloat16)
-            masked = jnp.concatenate([nope[:, cols], ends(biases)], axis=1)
-            keys = lambda run: jnp.concatenate(
-                [jnp.concatenate([ref[run, :, cols] for ref in k_refs], axis=0), tails[run]], axis=1
-            )
-            values = lambda run: jnp.concatenate(
-                [jnp.concatenate([ref[run, :, cols] for ref in v_refs], axis=0), ones], axis=1
-            )
-            score = over_lanes(masked, keys(half))
-            if own:
-                head = jnp.where(later, NEGATIVE, score[:, :first_keys])
-                score = jnp.concatenate([head, score[:, first_keys:]], axis=1)
-            parts = [(score, half)]
-            if half:
-                plain = jnp.concatenate([nope[:, cols], ends([0.0] * len(q_refs))], axis=1)
-                parts.append((over_lanes(plain, keys(0)), 0))
-            peak = functools.reduce(jnp.maximum, [jnp.max(s, axis=1, keepdims=True) for s, _ in parts])
-            peak = jnp.maximum(peak, FLOOR)
-            added = None
-            for s, run_of in parts:
-                weight = jnp.exp2(s - peak).astype(jnp.bfloat16)
-                a = jnp.dot(weight, values(run_of), preferred_element_type=jnp.float32)
-                added = a if added is None else added + a
-            some = added[:, D_VAL:] > 0.0
-            total = jnp.where(some, added[:, D_VAL:], 1.0)
-            result = (added[:, :D_VAL] / total).astype(jnp.bfloat16)
-            lse = jnp.where(some, peak + jnp.log2(total), NEGATIVE)
+
+            def rows_of(half, fill):
+                ends = [
+                    jnp.where(lane < 64, pltpu.roll(r, 64, 1) if inner else r, f)
+                    for r, f in zip(ropes[half], fill)
+                ]
+                ends = jnp.concatenate(ends, axis=0).astype(jnp.bfloat16)
+                return jnp.concatenate([nope[half][:, cols], ends], axis=1)
+
+            keys = [jnp.concatenate([k[:, cols], tail], axis=1) for k, tail in zip(k_pair, tails)]
+            both = jnp.concatenate([rows_of(0, biases[0]), rows_of(1, [0.0] * len(q_refs))], axis=0)
+            on_low = over_lanes(both, keys[0])
+            on_high = over_lanes(rows_of(1, biases[1]), keys[1])
+            scores.append((hide(on_low[:Q_TILE]), on_low[Q_TILE:], hide(on_high)))
+        peaks = []
+        for low, middle, high in scores:
+            top = [jnp.max(s, axis=1, keepdims=True) for s in (low, middle, high)]
+            peaks.append((jnp.maximum(top[0], FLOOR), jnp.maximum(top[1], jnp.maximum(top[2], FLOOR))))
+        weights = []
+        for (low, middle, high), (p_low, p_high) in zip(scores, peaks):
+            on_low = [jnp.exp2(low - p_low).astype(jnp.bfloat16), jnp.exp2(middle - p_high).astype(jnp.bfloat16)]
+            weights.append((jnp.concatenate(on_low, axis=0), jnp.exp2(high - p_high).astype(jnp.bfloat16)))
+        sums = []
+        for inner, (on_low, on_high) in enumerate(weights):
+            cols = slice(inner * 128, (inner + 1) * 128)
+            values = [jnp.concatenate([v[:, cols], ones], axis=1) for v in v_pair]
+            a = jnp.dot(on_low, values[0], preferred_element_type=jnp.float32)
+            b = jnp.dot(on_high, values[1], preferred_element_type=jnp.float32)
+            sums.append((a[:Q_TILE], a[Q_TILE:] + b))
+        for inner in range(2):
             head_at = pl.multiple_of(step * 256 + inner * 128, 128)
-            for i in range(2 * X_SIZE):
-                rows = slice(i * RUN, (i + 1) * RUN)
-                outs[i // X_SIZE][i % X_SIZE, run, pl.ds(head_at, 128)] = result[rows]
-                lse_scr[i, run, :] = jnp.where(lane == 2 * step + inner, lse[rows], lse_scr[i, run, :])
-
-    @pl.when(step == HEADS // 2 - 1)
-    def _():
-        for i in range(2 * X_SIZE):
-            outs[i // X_SIZE][i % X_SIZE, :, HEADS * D_VAL :] = packed(lse_scr[i])
+            for half in range(2):
+                added, peak = sums[inner][half], peaks[inner][half]
+                some = added[:, D_VAL:] > 0.0
+                total = jnp.where(some, added[:, D_VAL:], 1.0)
+                result = (added[:, :D_VAL] / total).astype(jnp.bfloat16)
+                lse = jnp.where(some, peak + jnp.log2(total), NEGATIVE)
+                for i in range(2 * X_SIZE):
+                    rows = slice(i * RUN, (i + 1) * RUN)
+                    outs[i // X_SIZE][i % X_SIZE, runs[half], pl.ds(head_at, 128)] = result[rows]
+                    held = lse_scr[i, runs[half], :]
+                    lse_scr[i, runs[half], :] = jnp.where(lane == 2 * step + inner, lse[rows], held)
+        return carry
+
+    lax.fori_loop(0, HEADS // 2, pair_of_heads, 0)
+    for i in range(2 * X_SIZE):
+        outs[i // X_SIZE][i % X_SIZE, :, HEADS * D_VAL :] = packed(lse_scr[i])
 
 
 def attend(near, far, chunks, own):
-    whole = lambda shape: pl.BlockSpec(shape, lambda i: (0,) * len(shape))
-    by_head = lambda a: pl.BlockSpec((2, a.shape[1], 256), lambda i: (0, 0, i))
     ks, vs, tails = zip(*chunks)
     out = jax.ShapeDtypeStruct((X_SIZE, TOK, OUT_ROW), jnp.bfloat16)
     return pl.pallas_call(
         functools.partial(attend_kernel, len(chunks), own),
-        grid=(HEADS // 2,),
-        in_specs=[whole(near.shape), whole(far.shape)]
-        + [by_head(a) for a in ks + vs]
-        + [whole(a.shape) for a in tails],
-        out_specs=[whole(out.shape)] * 2,
+        in_specs=[VMEM] * (2 + 3 * len(chunks)),
+        out_specs=[VMEM] * 2,
         out_shape=[out, out],
         scratch_shapes=[pltpu.VMEM((2 * X_SIZE, TOK, 128), jnp.float32)],
         compiler_params=pltpu.CompilerParams(vmem_limit_bytes=22 << 20),

time: 89.3 us -> 87.5 us (0.980)
  Pallas kernels: 31.8 us -> 26.4 us
  waiting for transfers between devices: 19.1 us -> 22.7 us
    pallas_call x3, Pallas kernels: 18.7 us -> 13.2 us  [attend(): pl.pallas_call(functools.partial(attend_kernel, len(chunks), own), in_spe...]
    ppermute x8, waiting for transfers between devices: 1.31 us -> 4.88 us  [body(): along = lambda block, by: lax.ppermute(block, 'z', shift(Z_SIZE, by))]
  transfers between devices with their start and end apart: 21 -> 21, of which waited for: 9 -> 11; matrix products, arithmetic and copies ran while one was open for 1% -> 1% of each run, Pallas kernels for 28% -> 22%
where the time goes in v3:
time: 87.5 us; the launch traced here: 87.4 us
  starting transfers between devices  35.8 us (41%)
  Pallas kernels  26.4 us (30%)
  waiting for transfers between devices  22.7 us (26%)
  local copies, waits for them, and re-layouts  1.27 us (1%)
  other arithmetic  1.11 us (1%)
    ppermute x8, starting transfers between devices, body(): along = lambda block, by: lax.ppermute(block, 'z', shift(Z_SIZE, by))  13.8 us
    pallas_call x3, Pallas kernels, attend(): pl.pallas_call(functools.partial(attend_kernel, len(chunks), own), in_spe...  13.2 us
    ppermute x6, waiting for transfers between devices, body(): across = lambda block, by: lax.ppermute(block, ACROSS, shift(X_SIZE, by))  11.8 us
    ppermute x6, starting transfers between devices, body(): across = lambda block, by: lax.ppermute(block, ACROSS, shift(X_SIZE, by))  10.2 us
    ppermute x4, starting transfers between devices, body(): swap = lambda block: lax.ppermute(block, 'core', [(0, 1), (1, 0)])  7.44 us
    pallas_call x5, Pallas kernels, expand(): pl.pallas_call(functools.partial(expand_kernel, len(blocks)), in_specs=[V...  5.92 us
    ppermute x8, waiting for transfers between devices, body(): along = lambda block, by: lax.ppermute(block, 'z', shift(Z_SIZE, by))  4.88 us
    ppermute x3, starting transfers between devices, body(): lax.ppermute(key_rows, 'y', shift(Y_SIZE, by))  4.38 us
  transfers between devices with their start and end apart: 21, of which 11 were waited for; matrix products, arithmetic and copies ran while one was open for 1% of the time, Pallas kernels for 22%

profile of v3, /device:TPU:1, one launch (start us, length us, event | category | flops | bytes accessed | tf_op | source)
XLA Modules:
  0.0 87.4 jit_solution(16299653977940974448)
XLA Ops:
  0.0 0.0 copy-start
  0.0 2.7 %rows.1 = (bf16[64,640]{1,0:T(8,128)(2,1)}, bf16[64,1664]{1,0:T(8,128)(2,1)}) custom-call(s32[64]{0:T(128)} %pos_ref.3, f32[512,2,128]{2,1,0:T(2,128)} %constant.4.clone.low_ref.high_ref, f32[512,2,128]{2,1,0:T(2,128)} %constant.4.clone.low_ref.high_ref, f32[2,32,128]{2,1,0:T(8,128)} %constant.5.clone.step_ref, bf16[64,1024]{1,0:T(8,128)(2,1)} %qn_ref.1, ...), custom_call_target="tpu_custom_call" | custom-call | tf_op jit(solution)/shard_map/rows/pallas_call | solution.py:280
  2.7 2.0 %collective-permute-start.3 = (bf16[64,1664]{1,0:T(8,128)(2,1)}, bf16[64,1664]{1,0:T(8,128)(2,1)S(1)}, u32[]{:S(2)}, u32[]{:S(2)}) collective-permute-start(bf16[64,1664]{1,0:T(8,128)(2,1)} %get-tuple-element.75), channel_id=1, source_target_pairs={{0,1},{1,128},{128,129},{129,0},{2,3},{3,130},{130,131},{131,2},{4... | collective-permute-start | bytes 638984 | tf_op jit(solution)/shard_map/ppermute | solution.py:304
  4.7 2.9 %collective-permute-start.2 = (bf16[64,640]{1,0:T(8,128)(2,1)}, bf16[64,640]{1,0:T(8,128)(2,1)S(1)}, u32[]{:S(2)}, u32[]{:S(2)}) collective-permute-start(bf16[64,640]{1,0:T(8,128)(2,1)} %get-tuple-element.66), channel_id=1, source_target_pairs={{0,32},{16,48},{32,0},{48,16},{1,33},{17,49},{33,1},{49,17},{2,34}... | collective-permute-start | bytes 245768 | tf_op jit(solution)/shard_map/ppermute | solution.py:307
  7.6 0.8 collective-permute-start.1
  8.4 0.7 collective-permute-start
  9.1 0.6 collective-permute-done.2
  9.7 2.3 %collective-permute-done.1 = bf16[64,640]{1,0:T(8,128)(2,1)S(1)} collective-permute-done((bf16[64,640]{1,0:T(8,128)(2,1)}, bf16[64,640]{1,0:T(8,128)(2,1)S(1)}, u32[]{:S(2)}, u32[]{:S(2)}) %collective-permute-start.1) | collective-permute-done | bytes 81952 | tf_op jit(solution)/shard_map/ppermute | solution.py:307
  12.0 1.1 %collective-permute-done = bf16[64,640]{1,0:T(8,128)(2,1)S(1)} collective-permute-done((bf16[64,640]{1,0:T(8,128)(2,1)}, bf16[64,640]{1,0:T(8,128)(2,1)S(1)}, u32[]{:S(2)}, u32[]{:S(2)}) %collective-permute-start) | collective-permute-done | bytes 81952 | tf_op jit(solution)/shard_map/ppermute | solution.py:307
  13.1 0.0 copy-start.4
  13.1 1.0 %pad_maximum_fusion.1.refs_0_ = bf16[4,64,640]{2,1,0:T(8,128)(2,1)S(1)} fusion(bf16[1,64,640]{2,1,0:T(8,128)(2,1)S(1)} %bitcast.20, bf16[1,64,640]{2,1,0:T(8,128)(2,1)S(1)} %bitcast.21, bf16[1,64,640]{2,1,0:T(8,128)(2,1)S(1)} %bitcast.22, bf16[1,64,640]{2,1,0:T(8,128)(2,1)} %bitcast.19), kind=kLoop, calls=%fused_computation.1 | loop fusion | flops 491520 | bytes 655360 | tf_op jit(solution)/shard_map/stack | solution.py:308
  14.1 0.0 collective-permute-done.3
  14.1 5.7 %collective-permute-start.5 = (bf16[4,64,640]{2,1,0:T(8,128)(2,1)S(1)}, bf16[4,64,640]{2,1,0:T(8,128)(2,1)S(1)}, u32[]{:S(2)}, u32[]{:S(2)}) collective-permute-start(bf16[4,64,640]{2,1,0:T(8,128)(2,1)S(1)} %pad_maximum_fusion.1.refs_0_), channel_id=1, source_target_pairs={{0,14},{2,0},{4,2},{6,4},{8,6},{10,8},{12,10},{14,12},{1,15},{3,1}... | collective-permute-start | bytes 983048 | tf_op jit(solution)/shard_map/ppermute | solution.py:305
  19.8 0.0 collective-permute-start.4
  19.8 0.0 copy-done.4
  19.8 2.5 %collective-permute-start.6 = (bf16[64,1664]{1,0:T(8,128)(2,1)S(1)}, bf16[64,1664]{1,0:T(8,128)(2,1)S(1)}, u32[]{:S(2)}, u32[]{:S(2)}) collective-permute-start(bf16[64,1664]{1,0:T(8,128)(2,1)S(1)} %copy-done.4), channel_id=1, source_target_pairs={{0,128},{1,129},{128,0},{129,1},{2,130},{3,131},{130,2},{131,3},{4... | collective-permute-start | bytes 638984 | tf_op jit(solution)/shard_map/ppermute | solution.py:304
  22.2 0.0 copy-done
  22.2 0.0 copy-start.1
  22.2 1.2 %copy-done.1 = bf16[8,512,128]{2,1,0:T(8,128)(2,1)S(1)} copy-done((bf16[8,512,128]{2,1,0:T(8,128)(2,1)S(1)}, bf16[8,512,128]{2,1,0:T(8,128)(2,1)}, u32[]{:S(2)}) %copy-start.1) | copy-done | bytes 1048600
  23.4 1.1 %expand.5 = (bf16[2,128,1024]{2,1,0:T(8,128)(2,1)S(1)}, bf16[2,128,1024]{2,1,0:T(8,128)(2,1)S(1)}, bf16[2,128,128]{2,1,0:T(8,128)(2,1)S(1)}) custom-call(bf16[4,64,640]{2,1,0:T(8,128)(2,1)S(1)} %pad_maximum_fusion.1.refs_0_, bf16[1024,512]{1,0:T(8,128)(2,1)S(1)} %bitcast.10, bf16[8,512,128]{2,1,0:T(8,128)(2,1)S(1)} %copy-done.1), custom_call_target="tpu_custom_call" | custom-call | flops 536870912 | bytes 3633152 | tf_op jit(solution)/shard_map/expand/pallas_call | solution.py:107
  24.5 1.4 %collective-permute-done.6 = bf16[64,1664]{1,0:T(8,128)(2,1)S(1)} collective-permute-done((bf16[64,1664]{1,0:T(8,128)(2,1)S(1)}, bf16[64,1664]{1,0:T(8,128)(2,1)S(1)}, u32[]{:S(2)}, u32[]{:S(2)}) %collective-permute-start.6) | collective-permute-done | bytes 213024 | tf_op jit(solution)/shard_map/ppermute | solution.py:304
  26.0 0.0 collective-permute-done.5.refs_1_
  26.0 1.3 %collective-permute-done.4.refs_0_ = bf16[4,64,640]{2,1,0:T(8,128)(2,1)S(1)} collective-permute-done((bf16[4,64,640]{2,1,0:T(8,128)(2,1)S(1)}, bf16[4,64,640]{2,1,0:T(8,128)(2,1)S(1)}, u32[]{:S(2)}, u32[]{:S(2)}) %collective-permute-start.4) | collective-permute-done | bytes 327712 | tf_op jit(solution)/shard_map/ppermute | solution.py:305
  27.2 0.0 collective-permute-start.7
  27.2 2.7 %collective-permute-start.8 = (bf16[4,64,640]{2,1,0:T(8,128)(2,1)S(1)}, bf16[4,64,640]{2,1,0:T(8,128)(2,1)S(1)}, u32[]{:S(2)}, u32[]{:S(2)}) collective-permute-start(bf16[4,64,640]{2,1,0:T(8,128)(2,1)S(1)} %collective-permute-done.5.refs_1_), channel_id=1, source_target_pairs={{0,14},{2,0},{4,2},{6,4},{8,6},{10,8},{12,10},{14,12},{1,15},{3,1}... | collective-permute-start | bytes 983048 | tf_op jit(solution)/shard_map/ppermute | solution.py:305
  29.9 1.5 %collective-permute-start.9 = (bf16[64,1664]{1,0:T(8,128)(2,1)S(1)}, bf16[64,1664]{1,0:T(8,128)(2,1)S(1)}, u32[]{:S(2)}, u32[]{:S(2)}) collective-permute-start(bf16[64,1664]{1,0:T(8,128)(2,1)S(1)} %copy-done.4), channel_id=1, source_target_pairs={{0,129},{1,0},{128,1},{129,128},{2,131},{3,2},{130,3},{131,130},{4... | collective-permute-start | bytes 638984 | tf_op jit(solution)/shard_map/ppermute | solution.py:304
  31.4 1.3 %expand.6 = (bf16[2,256,1024]{2,1,0:T(8,128)(2,1)S(1)}, bf16[2,256,1024]{2,1,0:T(8,128)(2,1)S(1)}, bf16[2,256,128]{2,1,0:T(8,128)(2,1)S(1)}) custom-call(bf16[4,64,640]{2,1,0:T(8,128)(2,1)S(1)} %collective-permute-done.4.refs_0_, bf16[4,64,640]{2,1,0:T(8,128)(2,1)S(1)} %collective-permute-done.5.refs_1_, bf16[1024,512]{1,0:T(8,128)(2,1)S(1)} %bitcast.11, ...), custom_call_target="tpu_custom_call" | custom-call | flops 1073741824 | bytes 5169152 | tf_op jit(solution)/shard_map/expand/pallas_call | solution.py:107
  32.6 0.0 copy-start.2
  32.7 2.2 %collective-permute-done.9 = bf16[64,1664]{1,0:T(8,128)(2,1)S(1)} collective-permute-done((bf16[64,1664]{1,0:T(8,128)(2,1)S(1)}, bf16[64,1664]{1,0:T(8,128)(2,1)S(1)}, u32[]{:S(2)}, u32[]{:S(2)}) %collective-permute-start.9) | collective-permute-done | bytes 213024 | tf_op jit(solution)/shard_map/ppermute | solution.py:304
  34.9 0.0 collective-permute-done.7.refs_0_
  34.9 0.0 collective-permute-done.8.refs_1_
  34.9 0.1 pad_maximum_fusion.refs_0_
  35.0 5.4 %collective-permute-start.12 = (bf16[4,64,1664]{2,1,0:T(8,128)(2,1)S(1)}, bf16[4,64,1664]{2,1,0:T(8,128)(2,1)S(1)}, u32[]{:S(2)}, u32[]{:S(2)}) collective-permute-start(bf16[4,64,1664]{2,1,0:T(8,128)(2,1)S(1)} %pad_maximum_fusion.refs_0_), channel_id=1, source_target_pairs={{0,64},{64,0},{1,65},{65,1},{2,66},{66,2},{3,67},{67,3},{4,68},{68... | collective-permute-start | bytes 2555912 | tf_op jit(solution)/shard_map/ppermute | solution.py:303
  40.4 0.0 collective-permute-start.10
  40.4 2.7 %collective-permute-start.11 = (bf16[4,64,640]{2,1,0:T(8,128)(2,1)S(1)}, bf16[4,64,640]{2,1,0:T(8,128)(2,1)S(1)}, u32[]{:S(2)}, u32[]{:S(2)}) collective-permute-start(bf16[4,64,640]{2,1,0:T(8,128)(2,1)S(1)} %collective-permute-done.8.refs_1_), channel_id=1, source_target_pairs={{0,14},{2,0},{4,2},{6,4},{8,6},{10,8},{12,10},{14,12},{1,15},{3,1}... | collective-permute-start | bytes 983048 | tf_op jit(solution)/shard_map/ppermute | solution.py:305
  43.1 0.0 copy-done.2
  43.1 1.3 %expand.7 = (bf16[2,256,1024]{2,1,0:T(8,128)(2,1)S(1)}, bf16[2,256,1024]{2,1,0:T(8,128)(2,1)S(1)}, bf16[2,256,128]{2,1,0:T(8,128)(2,1)S(1)}) custom-call(bf16[4,64,640]{2,1,0:T(8,128)(2,1)S(1)} %collective-permute-done.7.refs_0_, bf16[4,64,640]{2,1,0:T(8,128)(2,1)S(1)} %collective-permute-done.8.refs_1_, bf16[1024,512]{1,0:T(8,128)(2,1)S(1)} %bitcast.12, ...), custom_call_target="tpu_custom_call" | custom-call | flops 1073741824 | bytes 5169152 | tf_op jit(solution)/shard_map/expand/pallas_call | solution.py:107
  44.4 0.0 collective-permute-done.12.refs_1_
  44.4 4.9 %attend.3 = (bf16[4,64,1152]{2,1,0:T(8,128)(2,1)S(1)}, bf16[4,64,1152]{2,1,0:T(8,128)(2,1)S(1)}) custom-call(bf16[4,64,1664]{2,1,0:T(8,128)(2,1)S(1)} %pad_maximum_fusion.refs_0_, bf16[4,64,1664]{2,1,0:T(8,128)(2,1)S(1)} %collective-permute-done.12.refs_1_, bf16[2,128,1024]{2,1,0:T(8,128)(2,1)S(1)} %get-tuple-element.90.refs_2_, ...), custom_call_target="tpu_custom_call" | custom-call | flops 3840000000 | bytes 8388608 | tf_op jit(solution)/shard_map/attend/pallas_call | solution.py:222
  49.3 1.6 %collective-permute-done.10.refs_0_ = bf16[4,64,640]{2,1,0:T(8,128)(2,1)S(1)} collective-permute-done((bf16[4,64,640]{2,1,0:T(8,128)(2,1)S(1)}, bf16[4,64,640]{2,1,0:T(8,128)(2,1)S(1)}, u32[]{:S(2)}, u32[]{:S(2)}) %collective-permute-start.10) | collective-permute-done | bytes 327712 | tf_op jit(solution)/shard_map/ppermute | solution.py:305
  50.9 0.0 collective-permute-done.11.refs_1_
  50.9 0.9 collective-permute-start.15
  51.8 2.7 %collective-permute-start.14 = (bf16[2,64,640]{2,1,0:T(8,128)(2,1)S(1)}, bf16[2,64,640]{2,1,0:T(8,128)(2,1)S(1)}, u32[]{:S(2)}, u32[]{:S(2)}) collective-permute-start(bf16[2,64,640]{2,1,0:T(8,128)(2,1)S(1)} %slice.7), channel_id=1, source_target_pairs={{0,14},{2,0},{4,2},{6,4},{8,6},{10,8},{12,10},{14,12},{1,15},{3,1}... | collective-permute-start | bytes 491528 | tf_op jit(solution)/shard_map/ppermute | solution.py:305
  54.6 0.0 collective-permute-start.13
  54.6 3.5 %attend.4 = (bf16[4,64,1152]{2,1,0:T(8,128)(2,1)S(1)}, bf16[4,64,1152]{2,1,0:T(8,128)(2,1)S(1)}) custom-call(bf16[4,64,1664]{2,1,0:T(8,128)(2,1)S(1)} %pad_maximum_fusion.refs_0_, bf16[4,64,1664]{2,1,0:T(8,128)(2,1)S(1)} %collective-permute-done.12.refs_1_, bf16[2,256,1024]{2,1,0:T(8,128)(2,1)S(1)} %get-tuple-element.105.refs_2_, ...), custom_call_target="tpu_custom_call" | custom-call | flops 2560000000 | bytes 8388608 | tf_op jit(solution)/shard_map/attend/pallas_call | solution.py:222
  58.0 1.3 %expand.8 = (bf16[2,256,1024]{2,1,0:T(8,128)(2,1)S(1)}, bf16[2,256,1024]{2,1,0:T(8,128)(2,1)S(1)}, bf16[2,256,128]{2,1,0:T(8,128)(2,1)S(1)}) custom-call(bf16[4,64,640]{2,1,0:T(8,128)(2,1)S(1)} %collective-permute-done.10.refs_0_, bf16[4,64,640]{2,1,0:T(8,128)(2,1)S(1)} %collective-permute-done.11.refs_1_, bf16[1024,512]{1,0:T(8,128)(2,1)S(1)} %bitcast.13, ...), custom_call_target="tpu_custom_call" | custom-call | flops 1073741824 | bytes 5169152 | tf_op jit(solution)/shard_map/expand/pallas_call | solution.py:107
  59.3 0.0 collective-permute-done.14.refs_1_
  59.3 2.0 %collective-permute-done.13.refs_0_ = bf16[2,64,640]{2,1,0:T(8,128)(2,1)S(1)} collective-permute-done((bf16[2,64,640]{2,1,0:T(8,128)(2,1)S(1)}, bf16[2,64,640]{2,1,0:T(8,128)(2,1)S(1)}, u32[]{:S(2)}, u32[]{:S(2)}) %collective-permute-start.13) | collective-permute-done | bytes 163872 | tf_op jit(solution)/shard_map/ppermute | solution.py:305
  61.3 0.0 collective-permute-done.15.refs_3_
  61.3 1.1 %collective-permute-start.16 = (bf16[4,64,1152]{2,1,0:T(8,128)(2,1)S(1)}, bf16[4,64,1152]{2,1,0:T(8,128)(2,1)S(1)}, u32[]{:S(2)}, u32[]{:S(2)}) collective-permute-start(bf16[4,64,1152]{2,1,0:T(8,128)(2,1)S(1)} %get-tuple-element.122), channel_id=1, source_target_pairs={{0,64},{64,0},{1,65},{65,1},{2,66},{66,2},{3,67},{67,3},{4,68},{68... | collective-permute-start | bytes 1769480 | tf_op jit(solution)/shard_map/ppermute | solution.py:303
  62.4 1.1 %expand.9 = (bf16[2,128,1024]{2,1,0:T(8,128)(2,1)S(1)}, bf16[2,128,1024]{2,1,0:T(8,128)(2,1)S(1)}, bf16[2,128,128]{2,1,0:T(8,128)(2,1)S(1)}) custom-call(bf16[2,64,640]{2,1,0:T(8,128)(2,1)S(1)} %collective-permute-done.13.refs_0_, bf16[2,64,640]{2,1,0:T(8,128)(2,1)S(1)} %collective-permute-done.14.refs_1_, bf16[1024,512]{1,0:T(8,128)(2,1)S(1)} %bitcast.14, ...), custom_call_target="tpu_custom_call" | custom-call | flops 536870912 | bytes 3633152 | tf_op jit(solution)/shard_map/expand/pallas_call | solution.py:107
  63.5 4.9 %attend.5 = (bf16[4,64,1152]{2,1,0:T(8,128)(2,1)S(1)}, bf16[4,64,1152]{2,1,0:T(8,128)(2,1)S(1)}) custom-call(bf16[4,64,1664]{2,1,0:T(8,128)(2,1)S(1)} %pad_maximum_fusion.refs_0_, bf16[4,64,1664]{2,1,0:T(8,128)(2,1)S(1)} %collective-permute-done.12.refs_1_, bf16[2,256,1024]{2,1,0:T(8,128)(2,1)S(1)} %get-tuple-element.112.refs_2_, ...), custom_call_target="tpu_custom_call" | custom-call | flops 3840000000 | bytes 8388608 | tf_op jit(solution)/shard_map/attend/pallas_call | solution.py:222
  68.4 0.1 collective-permute-start.17
  68.5 0.0 collective-permute-done.16.refs_4_
  68.5 2.0 %collective-permute-done.17.refs_5_ = bf16[4,64,1152]{2,1,0:T(8,128)(2,1)S(1)} collective-permute-done((bf16[4,64,1152]{2,1,0:T(8,128)(2,1)S(1)}, bf16[4,64,1152]{2,1,0:T(8,128)(2,1)S(1)}, u32[]{:S(2)}, u32[]{:S(2)}) %collective-permute-start.17) | collective-permute-done | bytes 589856 | tf_op jit(solution)/shard_map/ppermute | solution.py:303
  70.5 2.5 %merge.1 = (bf16[64,1152]{1,0:T(8,128)(2,1)S(1)}, bf16[64,1152]{1,0:T(8,128)(2,1)S(1)}, bf16[64,1152]{1,0:T(8,128)(2,1)S(1)}) custom-call(bf16[4,64,1152]{2,1,0:T(8,128)(2,1)S(1)} %get-tuple-element.110.refs_0_, bf16[4,64,1152]{2,1,0:T(8,128)(2,1)S(1)} %get-tuple-element.111.refs_1_, bf16[4,64,1152]{2,1,0:T(8,128)(2,1)S(1)} %get-tuple-element.120.refs_2_, ...), custom_call_target="tpu_custom_call" | custom-call | tf_op jit(solution)/shard_map/merge/pallas_call | solution.py:346
  73.0 3.0 %collective-permute-start.18 = (bf16[64,1152]{1,0:T(8,128)(2,1)S(1)}, bf16[64,1152]{1,0:T(8,128)(2,1)S(1)}, u32[]{:S(2)}, u32[]{:S(2)}) collective-permute-start(bf16[64,1152]{1,0:T(8,128)(2,1)S(1)} %get-tuple-element.124), channel_id=1, source_target_pairs={{0,129},{1,0},{128,1},{129,128},{2,131},{3,2},{130,3},{131,130},{4... | collective-permute-start | bytes 442376 | tf_op jit(solution)/shard_map/ppermute | solution.py:304
  75.9 0.0 collective-permute-start.19
  75.9 1.3 %collective-permute-start.20 = (bf16[64,1152]{1,0:T(8,128)(2,1)S(1)}, bf16[64,1152]{1,0:T(8,128)(2,1)S(1)}, u32[]{:S(2)}, u32[]{:S(2)}) collective-permute-start(bf16[64,1152]{1,0:T(8,128)(2,1)S(1)} %get-tuple-element.126), channel_id=1, source_target_pairs={{0,128},{1,129},{128,0},{129,1},{2,130},{3,131},{130,2},{131,3},{4... | collective-permute-start | bytes 442376 | tf_op jit(solution)/shard_map/ppermute | solution.py:304
  77.2 1.8 %collective-permute-done.18.refs_6_ = bf16[64,1152]{1,0:T(8,128)(2,1)S(1)} collective-permute-done((bf16[64,1152]{1,0:T(8,128)(2,1)S(1)}, bf16[64,1152]{1,0:T(8,128)(2,1)S(1)}, u32[]{:S(2)}, u32[]{:S(2)}) %collective-permute-start.18) | collective-permute-done | bytes 147488 | tf_op jit(solution)/shard_map/ppermute | solution.py:304
  79.0 6.3 %collective-permute-done.19.refs_7_ = bf16[64,1152]{1,0:T(8,128)(2,1)S(1)} collective-permute-done((bf16[64,1152]{1,0:T(8,128)(2,1)S(1)}, bf16[64,1152]{1,0:T(8,128)(2,1)S(1)}, u32[]{:S(2)}, u32[]{:S(2)}) %collective-permute-start.19) | collective-permute-done | bytes 147488 | tf_op jit(solution)/shard_map/ppermute | solution.py:304
  85.3 0.0 collective-permute-done.20.refs_8_
  85.3 0.0 copy-done.3
  85.3 2.1 %combine.1 = bf16[64,1024]{1,0:T(8,128)(2,1)} custom-call(s32[64]{0:T(128)S(1)} %copy-done.3, bf16[4,64,1152]{2,1,0:T(8,128)(2,1)S(1)} %get-tuple-element.110.refs_0_, bf16[4,64,1152]{2,1,0:T(8,128)(2,1)S(1)} %get-tuple-element.111.refs_1_, bf16[4,64,1152]{2,1,0:T(8,128)(2,1)S(1)} %get-tuple-element.120.refs_2_, ...), custom_call_target="tpu_custom_call" | custom-call | tf_op jit(solution)/shard_map/combine/pallas_call | solution.py:355
  (3 shorter events, 0.0 us)
Async XLA Ops:
  0.0 22.2 %copy-start = (bf16[8,128,512]{2,1,0:T(8,128)(2,1)S(1)}, bf16[8,128,512]{2,1,0:T(8,128)(2,1)}, u32[]{:S(2)}) copy-start(bf16[8,128,512]{2,1,0:T(8,128)(2,1)} %param.14) | copy-start | bytes 3145732
  2.7 11.4 %collective-permute-start.3 = (bf16[64,1664]{1,0:T(8,128)(2,1)}, bf16[64,1664]{1,0:T(8,128)(2,1)S(1)}, u32[]{:S(2)}, u32[]{:S(2)}) collective-permute-start(bf16[64,1664]{1,0:T(8,128)(2,1)} %get-tuple-element.75), channel_id=1, source_target_pairs={{0,1},{1,128},{128,129},{129,0},{2,3},{3,130},{130,131},{131,2},{4... | collective-permute-start | bytes 638984 | tf_op jit(solution)/shard_map/ppermute | solution.py:304
  4.7 5.0 %collective-permute-start.2 = (bf16[64,640]{1,0:T(8,128)(2,1)}, bf16[64,640]{1,0:T(8,128)(2,1)S(1)}, u32[]{:S(2)}, u32[]{:S(2)}) collective-permute-start(bf16[64,640]{1,0:T(8,128)(2,1)} %get-tuple-element.66), channel_id=1, source_target_pairs={{0,32},{16,48},{32,0},{48,16},{1,33},{17,49},{33,1},{49,17},{2,34}... | collective-permute-start | bytes 245768 | tf_op jit(solution)/shard_map/ppermute | solution.py:307
  7.6 4.4 %collective-permute-start.1 = (bf16[64,640]{1,0:T(8,128)(2,1)}, bf16[64,640]{1,0:T(8,128)(2,1)S(1)}, u32[]{:S(2)}, u32[]{:S(2)}) collective-permute-start(bf16[64,640]{1,0:T(8,128)(2,1)} %get-tuple-element.66), channel_id=1, source_target_pairs={{0,48},{16,0},{32,16},{48,32},{1,49},{17,1},{33,17},{49,33},{2,50}... | collective-permute-start | bytes 245768 | tf_op jit(solution)/shard_map/ppermute | solution.py:307
  8.4 4.7 %collective-permute-start = (bf16[64,640]{1,0:T(8,128)(2,1)}, bf16[64,640]{1,0:T(8,128)(2,1)S(1)}, u32[]{:S(2)}, u32[]{:S(2)}) collective-permute-start(bf16[64,640]{1,0:T(8,128)(2,1)} %get-tuple-element.66), channel_id=1, source_target_pairs={{0,16},{16,32},{32,48},{48,0},{1,17},{17,33},{33,49},{49,1},{2,18}... | collective-permute-start | bytes 245768 | tf_op jit(solution)/shard_map/ppermute | solution.py:307
  13.1 6.7 %copy-start.4 = (bf16[64,1664]{1,0:T(8,128)(2,1)S(1)}, bf16[64,1664]{1,0:T(8,128)(2,1)}, u32[]{:S(2)}) copy-start(bf16[64,1664]{1,0:T(8,128)(2,1)} %get-tuple-element.75) | copy-start | bytes 638980
  14.1 11.9 %collective-permute-start.5 = (bf16[4,64,640]{2,1,0:T(8,128)(2,1)S(1)}, bf16[4,64,640]{2,1,0:T(8,128)(2,1)S(1)}, u32[]{:S(2)}, u32[]{:S(2)}) collective-permute-start(bf16[4,64,640]{2,1,0:T(8,128)(2,1)S(1)} %pad_maximum_fusion.1.refs_0_), channel_id=1, source_target_pairs={{0,14},{2,0},{4,2},{6,4},{8,6},{10,8},{12,10},{14,12},{1,15},{3,1}... | collective-permute-start | bytes 983048 | tf_op jit(solution)/shard_map/ppermute | solution.py:305
  19.8 7.5 %collective-permute-start.4 = (bf16[4,64,640]{2,1,0:T(8,128)(2,1)S(1)}, bf16[4,64,640]{2,1,0:T(8,128)(2,1)S(1)}, u32[]{:S(2)}, u32[]{:S(2)}) collective-permute-start(bf16[4,64,640]{2,1,0:T(8,128)(2,1)S(1)} %pad_maximum_fusion.1.refs_0_), channel_id=1, source_target_pairs={{0,2},{2,4},{4,6},{6,8},{8,10},{10,12},{12,14},{14,0},{1,3},{3,5},... | collective-permute-start | bytes 983048 | tf_op jit(solution)/shard_map/ppermute | solution.py:305
  19.8 6.2 %collective-permute-start.6 = (bf16[64,1664]{1,0:T(8,128)(2,1)S(1)}, bf16[64,1664]{1,0:T(8,128)(2,1)S(1)}, u32[]{:S(2)}, u32[]{:S(2)}) collective-permute-start(bf16[64,1664]{1,0:T(8,128)(2,1)S(1)} %copy-done.4), channel_id=1, source_target_pairs={{0,128},{1,129},{128,0},{129,1},{2,130},{3,131},{130,2},{131,3},{4... | collective-permute-start | bytes 638984 | tf_op jit(solution)/shard_map/ppermute | solution.py:304
  22.2 1.2 %copy-start.1 = (bf16[8,512,128]{2,1,0:T(8,128)(2,1)S(1)}, bf16[8,512,128]{2,1,0:T(8,128)(2,1)}, u32[]{:S(2)}) copy-start(bf16[8,512,128]{2,1,0:T(8,128)(2,1)} %refs_3_.7) | copy-start | bytes 3145732
  27.2 7.7 %collective-permute-start.7 = (bf16[4,64,640]{2,1,0:T(8,128)(2,1)S(1)}, bf16[4,64,640]{2,1,0:T(8,128)(2,1)S(1)}, u32[]{:S(2)}, u32[]{:S(2)}) collective-permute-start(bf16[4,64,640]{2,1,0:T(8,128)(2,1)S(1)} %collective-permute-done.4.refs_0_), channel_id=1, source_target_pairs={{0,2},{2,4},{4,6},{6,8},{8,10},{10,12},{12,14},{14,0},{1,3},{3,5},... | collective-permute-start | bytes 983048 | tf_op jit(solution)/shard_map/ppermute | solution.py:305
  27.2 7.7 %collective-permute-start.8 = (bf16[4,64,640]{2,1,0:T(8,128)(2,1)S(1)}, bf16[4,64,640]{2,1,0:T(8,128)(2,1)S(1)}, u32[]{:S(2)}, u32[]{:S(2)}) collective-permute-start(bf16[4,64,640]{2,1,0:T(8,128)(2,1)S(1)} %collective-permute-done.5.refs_1_), channel_id=1, source_target_pairs={{0,14},{2,0},{4,2},{6,4},{8,6},{10,8},{12,10},{14,12},{1,15},{3,1}... | collective-permute-start | bytes 983048 | tf_op jit(solution)/shard_map/ppermute | solution.py:305
  29.9 5.0 %collective-permute-start.9 = (bf16[64,1664]{1,0:T(8,128)(2,1)S(1)}, bf16[64,1664]{1,0:T(8,128)(2,1)S(1)}, u32[]{:S(2)}, u32[]{:S(2)}) collective-permute-start(bf16[64,1664]{1,0:T(8,128)(2,1)S(1)} %copy-done.4), channel_id=1, source_target_pairs={{0,129},{1,0},{128,1},{129,128},{2,131},{3,2},{130,3},{131,130},{4... | collective-permute-start | bytes 638984 | tf_op jit(solution)/shard_map/ppermute | solution.py:304
  32.6 10.5 %copy-start.2 = (bf16[8,512,128]{2,1,0:T(8,128)(2,1)S(1)}, bf16[8,512,128]{2,1,0:T(8,128)(2,1)}, u32[]{:S(2)}) copy-start(bf16[8,512,128]{2,1,0:T(8,128)(2,1)} %refs_3_.7) | copy-start | bytes 3145732
  35.0 9.3 %collective-permute-start.12 = (bf16[4,64,1664]{2,1,0:T(8,128)(2,1)S(1)}, bf16[4,64,1664]{2,1,0:T(8,128)(2,1)S(1)}, u32[]{:S(2)}, u32[]{:S(2)}) collective-permute-start(bf16[4,64,1664]{2,1,0:T(8,128)(2,1)S(1)} %pad_maximum_fusion.refs_0_), channel_id=1, source_target_pairs={{0,64},{64,0},{1,65},{65,1},{2,66},{66,2},{3,67},{67,3},{4,68},{68... | collective-permute-start | bytes 2555912 | tf_op jit(solution)/shard_map/ppermute | solution.py:303
  40.4 10.5 %collective-permute-start.10 = (bf16[4,64,640]{2,1,0:T(8,128)(2,1)S(1)}, bf16[4,64,640]{2,1,0:T(8,128)(2,1)S(1)}, u32[]{:S(2)}, u32[]{:S(2)}) collective-permute-start(bf16[4,64,640]{2,1,0:T(8,128)(2,1)S(1)} %collective-permute-done.7.refs_0_), channel_id=1, source_target_pairs={{0,2},{2,4},{4,6},{6,8},{8,10},{10,12},{12,14},{14,0},{1,3},{3,5},... | collective-permute-start | bytes 983048 | tf_op jit(solution)/shard_map/ppermute | solution.py:305
  40.4 10.5 %collective-permute-start.11 = (bf16[4,64,640]{2,1,0:T(8,128)(2,1)S(1)}, bf16[4,64,640]{2,1,0:T(8,128)(2,1)S(1)}, u32[]{:S(2)}, u32[]{:S(2)}) collective-permute-start(bf16[4,64,640]{2,1,0:T(8,128)(2,1)S(1)} %collective-permute-done.8.refs_1_), channel_id=1, source_target_pairs={{0,14},{2,0},{4,2},{6,4},{8,6},{10,8},{12,10},{14,12},{1,15},{3,1}... | collective-permute-start | bytes 983048 | tf_op jit(solution)/shard_map/ppermute | solution.py:305
  50.9 10.4 %collective-permute-start.15 = (bf16[4,64,1152]{2,1,0:T(8,128)(2,1)S(1)}, bf16[4,64,1152]{2,1,0:T(8,128)(2,1)S(1)}, u32[]{:S(2)}, u32[]{:S(2)}) collective-permute-start(bf16[4,64,1152]{2,1,0:T(8,128)(2,1)S(1)} %get-tuple-element.104), channel_id=1, source_target_pairs={{0,64},{64,0},{1,65},{65,1},{2,66},{66,2},{3,67},{67,3},{4,68},{68... | collective-permute-start | bytes 1769480 | tf_op jit(solution)/shard_map/ppermute | solution.py:303
  51.8 7.5 %collective-permute-start.14 = (bf16[2,64,640]{2,1,0:T(8,128)(2,1)S(1)}, bf16[2,64,640]{2,1,0:T(8,128)(2,1)S(1)}, u32[]{:S(2)}, u32[]{:S(2)}) collective-permute-start(bf16[2,64,640]{2,1,0:T(8,128)(2,1)S(1)} %slice.7), channel_id=1, source_target_pairs={{0,14},{2,0},{4,2},{6,4},{8,6},{10,8},{12,10},{14,12},{1,15},{3,1}... | collective-permute-start | bytes 491528 | tf_op jit(solution)/shard_map/ppermute | solution.py:305
  54.6 6.7 %collective-permute-start.13 = (bf16[2,64,640]{2,1,0:T(8,128)(2,1)S(1)}, bf16[2,64,640]{2,1,0:T(8,128)(2,1)S(1)}, u32[]{:S(2)}, u32[]{:S(2)}) collective-permute-start(bf16[2,64,640]{2,1,0:T(8,128)(2,1)S(1)} %slice.6), channel_id=1, source_target_pairs={{0,2},{2,4},{4,6},{6,8},{8,10},{10,12},{12,14},{14,0},{1,3},{3,5},... | collective-permute-start | bytes 491528 | tf_op jit(solution)/shard_map/ppermute | solution.py:305
  61.3 7.2 %collective-permute-start.16 = (bf16[4,64,1152]{2,1,0:T(8,128)(2,1)S(1)}, bf16[4,64,1152]{2,1,0:T(8,128)(2,1)S(1)}, u32[]{:S(2)}, u32[]{:S(2)}) collective-permute-start(bf16[4,64,1152]{2,1,0:T(8,128)(2,1)S(1)} %get-tuple-element.122), channel_id=1, source_target_pairs={{0,64},{64,0},{1,65},{65,1},{2,66},{66,2},{3,67},{67,3},{4,68},{68... | collective-permute-start | bytes 1769480 | tf_op jit(solution)/shard_map/ppermute | solution.py:303
  68.4 2.1 %collective-permute-start.17 = (bf16[4,64,1152]{2,1,0:T(8,128)(2,1)S(1)}, bf16[4,64,1152]{2,1,0:T(8,128)(2,1)S(1)}, u32[]{:S(2)}, u32[]{:S(2)}) collective-permute-start(bf16[4,64,1152]{2,1,0:T(8,128)(2,1)S(1)} %get-tuple-element.123), channel_id=1, source_target_pairs={{0,64},{64,0},{1,65},{65,1},{2,66},{66,2},{3,67},{67,3},{4,68},{68... | collective-permute-start | bytes 1769480 | tf_op jit(solution)/shard_map/ppermute | solution.py:303
  73.0 6.1 %collective-permute-start.18 = (bf16[64,1152]{1,0:T(8,128)(2,1)S(1)}, bf16[64,1152]{1,0:T(8,128)(2,1)S(1)}, u32[]{:S(2)}, u32[]{:S(2)}) collective-permute-start(bf16[64,1152]{1,0:T(8,128)(2,1)S(1)} %get-tuple-element.124), channel_id=1, source_target_pairs={{0,129},{1,0},{128,1},{129,128},{2,131},{3,2},{130,3},{131,130},{4... | collective-permute-start | bytes 442376 | tf_op jit(solution)/shard_map/ppermute | solution.py:304
  75.9 9.4 %copy-start.3 = (s32[64]{0:T(128)S(1)}, s32[64]{0:T(128)}, u32[]{:S(2)}) copy-start(s32[64]{0:T(128)} %pos_ref.3) | copy-start | bytes 772
  75.9 9.4 %collective-permute-start.19 = (bf16[64,1152]{1,0:T(8,128)(2,1)S(1)}, bf16[64,1152]{1,0:T(8,128)(2,1)S(1)}, u32[]{:S(2)}, u32[]{:S(2)}) collective-permute-start(bf16[64,1152]{1,0:T(8,128)(2,1)S(1)} %get-tuple-element.125), channel_id=1, source_target_pairs={{0,1},{1,128},{128,129},{129,0},{2,3},{3,130},{130,131},{131,2},{4... | collective-permute-start | bytes 442376 | tf_op jit(solution)/shard_map/ppermute | solution.py:304
  75.9 9.4 %collective-permute-start.20 = (bf16[64,1152]{1,0:T(8,128)(2,1)S(1)}, bf16[64,1152]{1,0:T(8,128)(2,1)S(1)}, u32[]{:S(2)}, u32[]{:S(2)}) collective-permute-start(bf16[64,1152]{1,0:T(8,128)(2,1)S(1)} %get-tuple-element.126), channel_id=1, source_target_pairs={{0,128},{1,129},{128,0},{129,1},{2,130},{3,131},{130,2},{131,3},{4... | collective-permute-start | bytes 442376 | tf_op jit(solution)/shard_map/ppermute | solution.py:304

commit v4 on v3

--- a/solution.py
+++ b/solution.py
@@ -239,8 +239,8 @@
     return functools.reduce(jnp.add, terms)
 
 
-def merge_kernel(n_parts, *refs):
-    for i, out_ref in enumerate(refs[n_parts:], 1):
+def merge_kernel(n_parts, which, *refs):
+    for i, out_ref in zip(which, refs[n_parts:]):
         parts = [ref.at[i] for ref in refs[:n_parts]]
         stats = [unpacked(p[:, HEADS * D_VAL :]) for p in parts]
         best = functools.reduce(jnp.maximum, stats)
@@ -251,6 +251,17 @@
         shares = [s / whole for s in shares]
         for h in range(HEADS):
             out_ref[:, h * D_VAL : (h + 1) * D_VAL] = mix(parts, shares, slice(0, TOK), h).astype(jnp.bfloat16)
+
+
+def merge(parts, which):
+    return pl.pallas_call(
+        functools.partial(merge_kernel, len(parts), which),
+        in_specs=[VMEM] * len(parts),
+        out_specs=[VMEM] * len(which),
+        out_shape=[jax.ShapeDtypeStruct((TOK, OUT_ROW), jnp.bfloat16)] * len(which),
+        compiler_params=pltpu.CompilerParams(vmem_limit_bytes=8 << 20),
+        name="merge",
+    )(*parts)
 
 
 def combine_kernel(n_local, pos_ref, *refs):
@@ -331,27 +342,19 @@
     blocks = [up, down]
     half = Y_SIZE // 2
     up, down = along(up[:half], 1), along(down[half:], -1)
-    crossed = [swap(partials[0][1])]
-    third = [expand(blocks, w_uk, w_uv)]
+    second.append(expand(blocks, w_uk, w_uv))
     partials.append(attend(near, far, second, False))
-    up, down, third, partials, crossed = lax.optimization_barrier((up, down, third, partials, crossed))
-
-    third.append(expand([up, down], w_uk, w_uv))
-    crossed.append(swap(partials[1][1]))
-    partials.append(attend(near, far, third, False))
+    up, down, partials = lax.optimization_barrier((up, down, partials))
+
+    crossed = [swap(p[1]) for p in partials]
+    partials.append(attend(near, far, [expand([up, down], w_uk, w_uv)], False))
     crossed.append(swap(partials[2][1]))
 
     local = [p[0] for p in partials] + crossed
-    part = jax.ShapeDtypeStruct((TOK, OUT_ROW), jnp.bfloat16)
-    merged = pl.pallas_call(
-        functools.partial(merge_kernel, len(local)),
-        in_specs=[VMEM] * len(local),
-        out_specs=[VMEM] * 3,
-        out_shape=[part] * 3,
-        compiler_params=pltpu.CompilerParams(vmem_limit_bytes=8 << 20),
-        name="merge",
-    )(*local)
-    back = [across(m, by) for m, by in zip(merged, (-1, 1, 2))]
+    opposite, = merge(local, [3])
+    local, opposite = lax.optimization_barrier((local, opposite))
+    right, left = merge(local, [1, 2])
+    back = [across(m, by) for m, by in ((opposite, 2), (right, -1), (left, 1))]
     return pl.pallas_call(
         functools.partial(combine_kernel, len(local)),
         in_specs=[SMEM] + [VMEM] * (len(local) + 3),

time: 87.5 us -> 82.8 us (0.946)
  waiting for transfers between devices: 22.7 us -> 17.9 us
    ppermute x6, waiting for transfers between devices: 11.8 us -> 9.01 us  [body(): across = lambda block, by: lax.ppermute(block, ACROSS, shift(X_SIZE, by))]
    ppermute x8, waiting for transfers between devices: 4.88 us -> 3.22 us  [body(): along = lambda block, by: lax.ppermute(block, 'z', shift(Z_SIZE, by))]
    ppermute x4, starting transfers between devices: 7.44 us -> 8.59 us  [body(): swap = lambda block: lax.ppermute(block, 'core', [(0, 1), (1, 0)])]
    pallas_call x1 -> x2, Pallas kernels: 2.48 us -> 2.21 us  [merge(): pl.pallas_call(functools.partial(merge_kernel, len(parts), which), in_spe...]
  transfers between devices with their start and end apart: 21 -> 21, of which waited for: 11 -> 12; matrix products, arithmetic and copies ran while one was open for 1% -> 1% of each run, Pallas kernels for 22% -> 23%
where the time goes in v4:
time: 82.8 us; the launch traced here: 82.6 us
  starting transfers between devices  36.5 us (44%)
  Pallas kernels  25.8 us (31%)
  waiting for transfers between devices  17.9 us (22%)
  local copies, waits for them, and re-layouts  1.28 us (2%)
  other arithmetic  1.11 us (1%)
    ppermute x8, starting transfers between devices, body(): along = lambda block, by: lax.ppermute(block, 'z', shift(Z_SIZE, by))  13.5 us
    pallas_call x3, Pallas kernels, attend(): pl.pallas_call(functools.partial(attend_kernel, len(chunks), own), in_spe...  12.9 us
    ppermute x6, starting transfers between devices, body(): across = lambda block, by: lax.ppermute(block, ACROSS, shift(X_SIZE, by))  10 us
    ppermute x6, waiting for transfers between devices, body(): across = lambda block, by: lax.ppermute(block, ACROSS, shift(X_SIZE, by))  9.01 us
    ppermute x4, starting transfers between devices, body(): swap = lambda block: lax.ppermute(block, 'core', [(0, 1), (1, 0)])  8.59 us
    pallas_call x5, Pallas kernels, expand(): pl.pallas_call(functools.partial(expand_kernel, len(blocks)), in_specs=[V...  5.92 us
    ppermute x3, starting transfers between devices, body(): lax.ppermute(key_rows, 'y', shift(Y_SIZE, by))  4.38 us
    ppermute x3, waiting for transfers between devices, body(): lax.ppermute(key_rows, 'y', shift(Y_SIZE, by))  4.02 us
  transfers between devices with their start and end apart: 21, of which 12 were waited for; matrix products, arithmetic and copies ran while one was open for 1% of the time, Pallas kernels for 23%

profile of v4, /device:TPU:1, one launch (start us, length us, event | category | flops | bytes accessed | tf_op | source)
XLA Modules:
  0.0 82.6 jit_solution(1071732634565435155)
XLA Ops:
  0.0 0.0 copy-start
  0.0 2.7 %rows.1 = (bf16[64,640]{1,0:T(8,128)(2,1)}, bf16[64,1664]{1,0:T(8,128)(2,1)}) custom-call(s32[64]{0:T(128)} %pos_ref.3, f32[512,2,128]{2,1,0:T(2,128)} %constant.4.clone.low_ref.high_ref, f32[512,2,128]{2,1,0:T(2,128)} %constant.4.clone.low_ref.high_ref, f32[2,32,128]{2,1,0:T(8,128)} %constant.5.clone.step_ref, bf16[64,1024]{1,0:T(8,128)(2,1)} %qn_ref.1, ...), custom_call_target="tpu_custom_call" | custom-call | tf_op jit(solution)/shard_map/rows/pallas_call | solution.py:291
  2.7 2.0 %collective-permute-start.3 = (bf16[64,1664]{1,0:T(8,128)(2,1)}, bf16[64,1664]{1,0:T(8,128)(2,1)S(1)}, u32[]{:S(2)}, u32[]{:S(2)}) collective-permute-start(bf16[64,1664]{1,0:T(8,128)(2,1)} %get-tuple-element.78), channel_id=1, source_target_pairs={{0,1},{1,128},{128,129},{129,0},{2,3},{3,130},{130,131},{131,2},{4... | collective-permute-start | bytes 638984 | tf_op jit(solution)/shard_map/ppermute | solution.py:315
  4.7 2.9 %collective-permute-start.2 = (bf16[64,640]{1,0:T(8,128)(2,1)}, bf16[64,640]{1,0:T(8,128)(2,1)S(1)}, u32[]{:S(2)}, u32[]{:S(2)}) collective-permute-start(bf16[64,640]{1,0:T(8,128)(2,1)} %get-tuple-element.69), channel_id=1, source_target_pairs={{0,32},{16,48},{32,0},{48,16},{1,33},{17,49},{33,1},{49,17},{2,34}... | collective-permute-start | bytes 245768 | tf_op jit(solution)/shard_map/ppermute | solution.py:318
  7.6 0.8 collective-permute-start.1
  8.4 0.7 collective-permute-start
  9.1 0.6 collective-permute-done.2
  9.7 2.3 %collective-permute-done.1 = bf16[64,640]{1,0:T(8,128)(2,1)S(1)} collective-permute-done((bf16[64,640]{1,0:T(8,128)(2,1)}, bf16[64,640]{1,0:T(8,128)(2,1)S(1)}, u32[]{:S(2)}, u32[]{:S(2)}) %collective-permute-start.1) | collective-permute-done | bytes 81952 | tf_op jit(solution)/shard_map/ppermute | solution.py:318
  12.0 1.1 %collective-permute-done = bf16[64,640]{1,0:T(8,128)(2,1)S(1)} collective-permute-done((bf16[64,640]{1,0:T(8,128)(2,1)}, bf16[64,640]{1,0:T(8,128)(2,1)S(1)}, u32[]{:S(2)}, u32[]{:S(2)}) %collective-permute-start) | collective-permute-done | bytes 81952 | tf_op jit(solution)/shard_map/ppermute | solution.py:318
  13.1 1.0 %pad_maximum_fusion.1.refs_0_ = bf16[4,64,640]{2,1,0:T(8,128)(2,1)S(1)} fusion(bf16[1,64,640]{2,1,0:T(8,128)(2,1)S(1)} %bitcast.20, bf16[1,64,640]{2,1,0:T(8,128)(2,1)S(1)} %bitcast.21, bf16[1,64,640]{2,1,0:T(8,128)(2,1)S(1)} %bitcast.22, bf16[1,64,640]{2,1,0:T(8,128)(2,1)} %bitcast.19), kind=kLoop, calls=%fused_computation.1 | loop fusion | flops 491520 | bytes 655360 | tf_op jit(solution)/shard_map/stack | solution.py:319
  14.1 0.0 collective-permute-done.3
  14.1 5.7 %collective-permute-start.5 = (bf16[4,64,640]{2,1,0:T(8,128)(2,1)S(1)}, bf16[4,64,640]{2,1,0:T(8,128)(2,1)S(1)}, u32[]{:S(2)}, u32[]{:S(2)}) collective-permute-start(bf16[4,64,640]{2,1,0:T(8,128)(2,1)S(1)} %pad_maximum_fusion.1.refs_0_), channel_id=1, source_target_pairs={{0,14},{2,0},{4,2},{6,4},{8,6},{10,8},{12,10},{14,12},{1,15},{3,1}... | collective-permute-start | bytes 983048 | tf_op jit(solution)/shard_map/ppermute | solution.py:316
  19.8 0.0 collective-permute-start.4
  19.8 0.0 copy-done.4
  19.8 2.5 %collective-permute-start.6 = (bf16[64,1664]{1,0:T(8,128)(2,1)S(1)}, bf16[64,1664]{1,0:T(8,128)(2,1)S(1)}, u32[]{:S(2)}, u32[]{:S(2)}) collective-permute-start(bf16[64,1664]{1,0:T(8,128)(2,1)S(1)} %copy-done.4), channel_id=1, source_target_pairs={{0,128},{1,129},{128,0},{129,1},{2,130},{3,131},{130,2},{131,3},{4... | collective-permute-start | bytes 638984 | tf_op jit(solution)/shard_map/ppermute | solution.py:315
  22.2 0.0 copy-done
  22.2 1.2 %copy-done.1 = bf16[8,512,128]{2,1,0:T(8,128)(2,1)S(1)} copy-done((bf16[8,512,128]{2,1,0:T(8,128)(2,1)S(1)}, bf16[8,512,128]{2,1,0:T(8,128)(2,1)}, u32[]{:S(2)}) %copy-start.1) | copy-done | bytes 1048600
  23.4 1.1 %expand.5 = (bf16[2,128,1024]{2,1,0:T(8,128)(2,1)S(1)}, bf16[2,128,1024]{2,1,0:T(8,128)(2,1)S(1)}, bf16[2,128,128]{2,1,0:T(8,128)(2,1)S(1)}) custom-call(bf16[4,64,640]{2,1,0:T(8,128)(2,1)S(1)} %pad_maximum_fusion.1.refs_0_, bf16[1024,512]{1,0:T(8,128)(2,1)S(1)} %bitcast.10, bf16[8,512,128]{2,1,0:T(8,128)(2,1)S(1)} %copy-done.1), custom_call_target="tpu_custom_call" | custom-call | flops 536870912 | bytes 3633152 | tf_op jit(solution)/shard_map/expand/pallas_call | solution.py:107
  24.5 1.4 %collective-permute-done.6 = bf16[64,1664]{1,0:T(8,128)(2,1)S(1)} collective-permute-done((bf16[64,1664]{1,0:T(8,128)(2,1)S(1)}, bf16[64,1664]{1,0:T(8,128)(2,1)S(1)}, u32[]{:S(2)}, u32[]{:S(2)}) %collective-permute-start.6) | collective-permute-done | bytes 213024 | tf_op jit(solution)/shard_map/ppermute | solution.py:315
  26.0 0.0 collective-permute-done.5.refs_1_
  26.0 1.3 %collective-permute-done.4.refs_0_ = bf16[4,64,640]{2,1,0:T(8,128)(2,1)S(1)} collective-permute-done((bf16[4,64,640]{2,1,0:T(8,128)(2,1)S(1)}, bf16[4,64,640]{2,1,0:T(8,128)(2,1)S(1)}, u32[]{:S(2)}, u32[]{:S(2)}) %collective-permute-start.4) | collective-permute-done | bytes 327712 | tf_op jit(solution)/shard_map/ppermute | solution.py:316
  27.2 0.0 collective-permute-start.7
  27.2 2.7 %collective-permute-start.8 = (bf16[4,64,640]{2,1,0:T(8,128)(2,1)S(1)}, bf16[4,64,640]{2,1,0:T(8,128)(2,1)S(1)}, u32[]{:S(2)}, u32[]{:S(2)}) collective-permute-start(bf16[4,64,640]{2,1,0:T(8,128)(2,1)S(1)} %collective-permute-done.5.refs_1_), channel_id=1, source_target_pairs={{0,14},{2,0},{4,2},{6,4},{8,6},{10,8},{12,10},{14,12},{1,15},{3,1}... | collective-permute-start | bytes 983048 | tf_op jit(solution)/shard_map/ppermute | solution.py:316
  29.9 1.5 %collective-permute-start.9 = (bf16[64,1664]{1,0:T(8,128)(2,1)S(1)}, bf16[64,1664]{1,0:T(8,128)(2,1)S(1)}, u32[]{:S(2)}, u32[]{:S(2)}) collective-permute-start(bf16[64,1664]{1,0:T(8,128)(2,1)S(1)} %copy-done.4), channel_id=1, source_target_pairs={{0,129},{1,0},{128,1},{129,128},{2,131},{3,2},{130,3},{131,130},{4... | collective-permute-start | bytes 638984 | tf_op jit(solution)/shard_map/ppermute | solution.py:315
  31.4 1.3 %expand.6 = (bf16[2,256,1024]{2,1,0:T(8,128)(2,1)S(1)}, bf16[2,256,1024]{2,1,0:T(8,128)(2,1)S(1)}, bf16[2,256,128]{2,1,0:T(8,128)(2,1)S(1)}) custom-call(bf16[4,64,640]{2,1,0:T(8,128)(2,1)S(1)} %collective-permute-done.4.refs_0_, bf16[4,64,640]{2,1,0:T(8,128)(2,1)S(1)} %collective-permute-done.5.refs_1_, bf16[1024,512]{1,0:T(8,128)(2,1)S(1)} %bitcast.11, ...), custom_call_target="tpu_custom_call" | custom-call | flops 1073741824 | bytes 5169152 | tf_op jit(solution)/shard_map/expand/pallas_call | solution.py:107
  32.6 0.0 copy-start.2
  32.7 2.2 %collective-permute-done.9 = bf16[64,1664]{1,0:T(8,128)(2,1)S(1)} collective-permute-done((bf16[64,1664]{1,0:T(8,128)(2,1)S(1)}, bf16[64,1664]{1,0:T(8,128)(2,1)S(1)}, u32[]{:S(2)}, u32[]{:S(2)}) %collective-permute-start.9) | collective-permute-done | bytes 213024 | tf_op jit(solution)/shard_map/ppermute | solution.py:315
  34.9 0.0 collective-permute-done.7.refs_0_
  34.9 0.0 collective-permute-done.8.refs_1_
  34.9 0.1 pad_maximum_fusion.refs_0_
  35.0 5.4 %collective-permute-start.12 = (bf16[4,64,1664]{2,1,0:T(8,128)(2,1)S(1)}, bf16[4,64,1664]{2,1,0:T(8,128)(2,1)S(1)}, u32[]{:S(2)}, u32[]{:S(2)}) collective-permute-start(bf16[4,64,1664]{2,1,0:T(8,128)(2,1)S(1)} %pad_maximum_fusion.refs_0_), channel_id=1, source_target_pairs={{0,64},{64,0},{1,65},{65,1},{2,66},{66,2},{3,67},{67,3},{4,68},{68... | collective-permute-start | bytes 2555912 | tf_op jit(solution)/shard_map/ppermute | solution.py:314
  40.4 0.0 collective-permute-start.10
  40.4 2.7 %collective-permute-start.11 = (bf16[4,64,640]{2,1,0:T(8,128)(2,1)S(1)}, bf16[4,64,640]{2,1,0:T(8,128)(2,1)S(1)}, u32[]{:S(2)}, u32[]{:S(2)}) collective-permute-start(bf16[4,64,640]{2,1,0:T(8,128)(2,1)S(1)} %collective-permute-done.8.refs_1_), channel_id=1, source_target_pairs={{0,14},{2,0},{4,2},{6,4},{8,6},{10,8},{12,10},{14,12},{1,15},{3,1}... | collective-permute-start | bytes 983048 | tf_op jit(solution)/shard_map/ppermute | solution.py:316
  43.1 0.0 copy-done.2
  43.1 1.3 %expand.7 = (bf16[2,256,1024]{2,1,0:T(8,128)(2,1)S(1)}, bf16[2,256,1024]{2,1,0:T(8,128)(2,1)S(1)}, bf16[2,256,128]{2,1,0:T(8,128)(2,1)S(1)}) custom-call(bf16[4,64,640]{2,1,0:T(8,128)(2,1)S(1)} %collective-permute-done.7.refs_0_, bf16[4,64,640]{2,1,0:T(8,128)(2,1)S(1)} %collective-permute-done.8.refs_1_, bf16[1024,512]{1,0:T(8,128)(2,1)S(1)} %bitcast.12, ...), custom_call_target="tpu_custom_call" | custom-call | flops 1073741824 | bytes 5169152 | tf_op jit(solution)/shard_map/expand/pallas_call | solution.py:107
  44.4 0.0 collective-permute-done.12.refs_1_
  44.4 4.9 %attend.3 = (bf16[4,64,1152]{2,1,0:T(8,128)(2,1)S(1)}, bf16[4,64,1152]{2,1,0:T(8,128)(2,1)S(1)}) custom-call(bf16[4,64,1664]{2,1,0:T(8,128)(2,1)S(1)} %pad_maximum_fusion.refs_0_, bf16[4,64,1664]{2,1,0:T(8,128)(2,1)S(1)} %collective-permute-done.12.refs_1_, bf16[2,128,1024]{2,1,0:T(8,128)(2,1)S(1)} %get-tuple-element.93.refs_2_, ...), custom_call_target="tpu_custom_call" | custom-call | flops 3840000000 | bytes 8388608 | tf_op jit(solution)/shard_map/attend/pallas_call | solution.py:222
  49.3 1.6 %collective-permute-done.10.refs_0_ = bf16[4,64,640]{2,1,0:T(8,128)(2,1)S(1)} collective-permute-done((bf16[4,64,640]{2,1,0:T(8,128)(2,1)S(1)}, bf16[4,64,640]{2,1,0:T(8,128)(2,1)S(1)}, u32[]{:S(2)}, u32[]{:S(2)}) %collective-permute-start.10) | collective-permute-done | bytes 327712 | tf_op jit(solution)/shard_map/ppermute | solution.py:316
  50.9 0.0 collective-permute-done.11.refs_1_
  50.9 1.3 %expand.8 = (bf16[2,256,1024]{2,1,0:T(8,128)(2,1)S(1)}, bf16[2,256,1024]{2,1,0:T(8,128)(2,1)S(1)}, bf16[2,256,128]{2,1,0:T(8,128)(2,1)S(1)}) custom-call(bf16[4,64,640]{2,1,0:T(8,128)(2,1)S(1)} %collective-permute-done.10.refs_0_, bf16[4,64,640]{2,1,0:T(8,128)(2,1)S(1)} %collective-permute-done.11.refs_1_, bf16[1024,512]{1,0:T(8,128)(2,1)S(1)} %bitcast.13, ...), custom_call_target="tpu_custom_call" | custom-call | flops 1073741824 | bytes 5169152 | tf_op jit(solution)/shard_map/expand/pallas_call | solution.py:107
  52.2 2.4 %collective-permute-start.14 = (bf16[2,64,640]{2,1,0:T(8,128)(2,1)S(1)}, bf16[2,64,640]{2,1,0:T(8,128)(2,1)S(1)}, u32[]{:S(2)}, u32[]{:S(2)}) collective-permute-start(bf16[2,64,640]{2,1,0:T(8,128)(2,1)S(1)} %slice.7), channel_id=1, source_target_pairs={{0,14},{2,0},{4,2},{6,4},{8,6},{10,8},{12,10},{14,12},{1,15},{3,1}... | collective-permute-start | bytes 491528 | tf_op jit(solution)/shard_map/ppermute | solution.py:316
  54.6 0.0 collective-permute-start.13
  54.6 5.0 %attend.4 = (bf16[4,64,1152]{2,1,0:T(8,128)(2,1)S(1)}, bf16[4,64,1152]{2,1,0:T(8,128)(2,1)S(1)}) custom-call(bf16[4,64,1664]{2,1,0:T(8,128)(2,1)S(1)} %pad_maximum_fusion.refs_0_, bf16[4,64,1664]{2,1,0:T(8,128)(2,1)S(1)} %collective-permute-done.12.refs_1_, bf16[2,256,1024]{2,1,0:T(8,128)(2,1)S(1)} %get-tuple-element.105.refs_2_, ...), custom_call_target="tpu_custom_call" | custom-call | flops 5120000000 | bytes 8388608 | tf_op jit(solution)/shard_map/attend/pallas_call | solution.py:222
  59.7 0.0 collective-permute-done.14.refs_1_
  59.7 0.3 collective-permute-done.13.refs_0_
  60.0 2.6 %collective-permute-start.15 = (bf16[4,64,1152]{2,1,0:T(8,128)(2,1)S(1)}, bf16[4,64,1152]{2,1,0:T(8,128)(2,1)S(1)}, u32[]{:S(2)}, u32[]{:S(2)}) collective-permute-start(bf16[4,64,1152]{2,1,0:T(8,128)(2,1)S(1)} %get-tuple-element.121), channel_id=1, source_target_pairs={{0,64},{64,0},{1,65},{65,1},{2,66},{66,2},{3,67},{67,3},{4,68},{68... | collective-permute-start | bytes 1769480 | tf_op jit(solution)/shard_map/ppermute | solution.py:314
  62.6 0.0 collective-permute-start.16
  62.6 1.1 %expand.9 = (bf16[2,128,1024]{2,1,0:T(8,128)(2,1)S(1)}, bf16[2,128,1024]{2,1,0:T(8,128)(2,1)S(1)}, bf16[2,128,128]{2,1,0:T(8,128)(2,1)S(1)}) custom-call(bf16[2,64,640]{2,1,0:T(8,128)(2,1)S(1)} %collective-permute-done.13.refs_0_, bf16[2,64,640]{2,1,0:T(8,128)(2,1)S(1)} %collective-permute-done.14.refs_1_, bf16[1024,512]{1,0:T(8,128)(2,1)S(1)} %bitcast.14, ...), custom_call_target="tpu_custom_call" | custom-call | flops 536870912 | bytes 3633152 | tf_op jit(solution)/shard_map/expand/pallas_call | solution.py:107
  63.7 3.0 %attend.5 = (bf16[4,64,1152]{2,1,0:T(8,128)(2,1)S(1)}, bf16[4,64,1152]{2,1,0:T(8,128)(2,1)S(1)}) custom-call(bf16[4,64,1664]{2,1,0:T(8,128)(2,1)S(1)} %pad_maximum_fusion.refs_0_, bf16[4,64,1664]{2,1,0:T(8,128)(2,1)S(1)} %collective-permute-done.12.refs_1_, bf16[2,128,1024]{2,1,0:T(8,128)(2,1)S(1)} %get-tuple-element.117.refs_2_, ...), custom_call_target="tpu_custom_call" | custom-call | flops 1280000000 | bytes 8388608 | tf_op jit(solution)/shard_map/attend/pallas_call | solution.py:222
  66.7 0.6 collective-permute-start.17
  67.3 0.0 collective-permute-done.15.refs_3_
  67.3 0.0 collective-permute-done.16.refs_4_
  67.3 1.6 %collective-permute-done.17.refs_5_ = bf16[4,64,1152]{2,1,0:T(8,128)(2,1)S(1)} collective-permute-done((bf16[4,64,1152]{2,1,0:T(8,128)(2,1)S(1)}, bf16[4,64,1152]{2,1,0:T(8,128)(2,1)S(1)}, u32[]{:S(2)}, u32[]{:S(2)}) %collective-permute-start.17) | collective-permute-done | bytes 589856 | tf_op jit(solution)/shard_map/ppermute | solution.py:314
  68.9 0.7 merge.2
  69.6 2.5 %collective-permute-start.18 = (bf16[64,1152]{1,0:T(8,128)(2,1)S(1)}, bf16[64,1152]{1,0:T(8,128)(2,1)S(1)}, u32[]{:S(2)}, u32[]{:S(2)}) collective-permute-start(bf16[64,1152]{1,0:T(8,128)(2,1)S(1)} %merge.2), channel_id=1, source_target_pairs={{0,128},{1,129},{128,0},{129,1},{2,130},{3,131},{130,2},{131,3},{4... | collective-permute-start | bytes 442376 | tf_op jit(solution)/shard_map/ppermute | solution.py:315
  72.1 1.6 %merge.3 = (bf16[64,1152]{1,0:T(8,128)(2,1)S(1)}, bf16[64,1152]{1,0:T(8,128)(2,1)S(1)}) custom-call(bf16[4,64,1152]{2,1,0:T(8,128)(2,1)S(1)} %get-tuple-element.124.refs_0_, bf16[4,64,1152]{2,1,0:T(8,128)(2,1)S(1)} %get-tuple-element.125.refs_1_, bf16[4,64,1152]{2,1,0:T(8,128)(2,1)S(1)} %get-tuple-element.126.refs_2_, ...), custom_call_target="tpu_custom_call" | custom-call | tf_op jit(solution)/shard_map/merge/pallas_call | solution.py:257
  73.7 0.0 copy-start.3
  73.7 1.2 %collective-permute-start.19 = (bf16[64,1152]{1,0:T(8,128)(2,1)S(1)}, bf16[64,1152]{1,0:T(8,128)(2,1)S(1)}, u32[]{:S(2)}, u32[]{:S(2)}) collective-permute-start(bf16[64,1152]{1,0:T(8,128)(2,1)S(1)} %get-tuple-element.131), channel_id=1, source_target_pairs={{0,129},{1,0},{128,1},{129,128},{2,131},{3,2},{130,3},{131,130},{4... | collective-permute-start | bytes 442376 | tf_op jit(solution)/shard_map/ppermute | solution.py:315
  74.9 0.3 collective-permute-start.20
  75.2 1.0 %collective-permute-done.18.refs_6_ = bf16[64,1152]{1,0:T(8,128)(2,1)S(1)} collective-permute-done((bf16[64,1152]{1,0:T(8,128)(2,1)S(1)}, bf16[64,1152]{1,0:T(8,128)(2,1)S(1)}, u32[]{:S(2)}, u32[]{:S(2)}) %collective-permute-start.18) | collective-permute-done | bytes 147488 | tf_op jit(solution)/shard_map/ppermute | solution.py:315
  76.2 3.4 %collective-permute-done.19.refs_7_ = bf16[64,1152]{1,0:T(8,128)(2,1)S(1)} collective-permute-done((bf16[64,1152]{1,0:T(8,128)(2,1)S(1)}, bf16[64,1152]{1,0:T(8,128)(2,1)S(1)}, u32[]{:S(2)}, u32[]{:S(2)}) %collective-permute-start.19) | collective-permute-done | bytes 147488 | tf_op jit(solution)/shard_map/ppermute | solution.py:315
  79.7 0.9 %collective-permute-done.20.refs_8_ = bf16[64,1152]{1,0:T(8,128)(2,1)S(1)} collective-permute-done((bf16[64,1152]{1,0:T(8,128)(2,1)S(1)}, bf16[64,1152]{1,0:T(8,128)(2,1)S(1)}, u32[]{:S(2)}, u32[]{:S(2)}) %collective-permute-start.20) | collective-permute-done | bytes 147488 | tf_op jit(solution)/shard_map/ppermute | solution.py:315
  80.5 0.0 copy-done.3
  80.5 2.1 %combine.1 = bf16[64,1024]{1,0:T(8,128)(2,1)} custom-call(s32[64]{0:T(128)S(1)} %copy-done.3, bf16[4,64,1152]{2,1,0:T(8,128)(2,1)S(1)} %get-tuple-element.124.refs_0_, bf16[4,64,1152]{2,1,0:T(8,128)(2,1)S(1)} %get-tuple-element.125.refs_1_, bf16[4,64,1152]{2,1,0:T(8,128)(2,1)S(1)} %get-tuple-element.126.refs_2_, ...), custom_call_target="tpu_custom_call" | custom-call | tf_op jit(solution)/shard_map/combine/pallas_call | solution.py:358
  (4 shorter events, 0.0 us)
Async XLA Ops:
  0.0 22.2 %copy-start = (bf16[8,128,512]{2,1,0:T(8,128)(2,1)S(1)}, bf16[8,128,512]{2,1,0:T(8,128)(2,1)}, u32[]{:S(2)}) copy-start(bf16[8,128,512]{2,1,0:T(8,128)(2,1)} %param.14) | copy-start | bytes 3145732
  2.7 11.4 %collective-permute-start.3 = (bf16[64,1664]{1,0:T(8,128)(2,1)}, bf16[64,1664]{1,0:T(8,128)(2,1)S(1)}, u32[]{:S(2)}, u32[]{:S(2)}) collective-permute-start(bf16[64,1664]{1,0:T(8,128)(2,1)} %get-tuple-element.78), channel_id=1, source_target_pairs={{0,1},{1,128},{128,129},{129,0},{2,3},{3,130},{130,131},{131,2},{4... | collective-permute-start | bytes 638984 | tf_op jit(solution)/shard_map/ppermute | solution.py:315
  4.7 5.0 %collective-permute-start.2 = (bf16[64,640]{1,0:T(8,128)(2,1)}, bf16[64,640]{1,0:T(8,128)(2,1)S(1)}, u32[]{:S(2)}, u32[]{:S(2)}) collective-permute-start(bf16[64,640]{1,0:T(8,128)(2,1)} %get-tuple-element.69), channel_id=1, source_target_pairs={{0,32},{16,48},{32,0},{48,16},{1,33},{17,49},{33,1},{49,17},{2,34}... | collective-permute-start | bytes 245768 | tf_op jit(solution)/shard_map/ppermute | solution.py:318
  7.6 4.4 %collective-permute-start.1 = (bf16[64,640]{1,0:T(8,128)(2,1)}, bf16[64,640]{1,0:T(8,128)(2,1)S(1)}, u32[]{:S(2)}, u32[]{:S(2)}) collective-permute-start(bf16[64,640]{1,0:T(8,128)(2,1)} %get-tuple-element.69), channel_id=1, source_target_pairs={{0,48},{16,0},{32,16},{48,32},{1,49},{17,1},{33,17},{49,33},{2,50}... | collective-permute-start | bytes 245768 | tf_op jit(solution)/shard_map/ppermute | solution.py:318
  8.4 4.7 %collective-permute-start = (bf16[64,640]{1,0:T(8,128)(2,1)}, bf16[64,640]{1,0:T(8,128)(2,1)S(1)}, u32[]{:S(2)}, u32[]{:S(2)}) collective-permute-start(bf16[64,640]{1,0:T(8,128)(2,1)} %get-tuple-element.69), channel_id=1, source_target_pairs={{0,16},{16,32},{32,48},{48,0},{1,17},{17,33},{33,49},{49,1},{2,18}... | collective-permute-start | bytes 245768 | tf_op jit(solution)/shard_map/ppermute | solution.py:318
  13.1 6.7 %copy-start.4 = (bf16[64,1664]{1,0:T(8,128)(2,1)S(1)}, bf16[64,1664]{1,0:T(8,128)(2,1)}, u32[]{:S(2)}) copy-start(bf16[64,1664]{1,0:T(8,128)(2,1)} %get-tuple-element.78) | copy-start | bytes 638980
  14.1 11.9 %collective-permute-start.5 = (bf16[4,64,640]{2,1,0:T(8,128)(2,1)S(1)}, bf16[4,64,640]{2,1,0:T(8,128)(2,1)S(1)}, u32[]{:S(2)}, u32[]{:S(2)}) collective-permute-start(bf16[4,64,640]{2,1,0:T(8,128)(2,1)S(1)} %pad_maximum_fusion.1.refs_0_), channel_id=1, source_target_pairs={{0,14},{2,0},{4,2},{6,4},{8,6},{10,8},{12,10},{14,12},{1,15},{3,1}... | collective-permute-start | bytes 983048 | tf_op jit(solution)/shard_map/ppermute | solution.py:316
  19.8 7.5 %collective-permute-start.4 = (bf16[4,64,640]{2,1,0:T(8,128)(2,1)S(1)}, bf16[4,64,640]{2,1,0:T(8,128)(2,1)S(1)}, u32[]{:S(2)}, u32[]{:S(2)}) collective-permute-start(bf16[4,64,640]{2,1,0:T(8,128)(2,1)S(1)} %pad_maximum_fusion.1.refs_0_), channel_id=1, source_target_pairs={{0,2},{2,4},{4,6},{6,8},{8,10},{10,12},{12,14},{14,0},{1,3},{3,5},... | collective-permute-start | bytes 983048 | tf_op jit(solution)/shard_map/ppermute | solution.py:316
  19.8 6.2 %collective-permute-start.6 = (bf16[64,1664]{1,0:T(8,128)(2,1)S(1)}, bf16[64,1664]{1,0:T(8,128)(2,1)S(1)}, u32[]{:S(2)}, u32[]{:S(2)}) collective-permute-start(bf16[64,1664]{1,0:T(8,128)(2,1)S(1)} %copy-done.4), channel_id=1, source_target_pairs={{0,128},{1,129},{128,0},{129,1},{2,130},{3,131},{130,2},{131,3},{4... | collective-permute-start | bytes 638984 | tf_op jit(solution)/shard_map/ppermute | solution.py:315
  22.2 1.2 %copy-start.1 = (bf16[8,512,128]{2,1,0:T(8,128)(2,1)S(1)}, bf16[8,512,128]{2,1,0:T(8,128)(2,1)}, u32[]{:S(2)}) copy-start(bf16[8,512,128]{2,1,0:T(8,128)(2,1)} %refs_3_.7) | copy-start | bytes 3145732
  27.2 7.7 %collective-permute-start.7 = (bf16[4,64,640]{2,1,0:T(8,128)(2,1)S(1)}, bf16[4,64,640]{2,1,0:T(8,128)(2,1)S(1)}, u32[]{:S(2)}, u32[]{:S(2)}) collective-permute-start(bf16[4,64,640]{2,1,0:T(8,128)(2,1)S(1)} %collective-permute-done.4.refs_0_), channel_id=1, source_target_pairs={{0,2},{2,4},{4,6},{6,8},{8,10},{10,12},{12,14},{14,0},{1,3},{3,5},... | collective-permute-start | bytes 983048 | tf_op jit(solution)/shard_map/ppermute | solution.py:316
  27.2 7.7 %collective-permute-start.8 = (bf16[4,64,640]{2,1,0:T(8,128)(2,1)S(1)}, bf16[4,64,640]{2,1,0:T(8,128)(2,1)S(1)}, u32[]{:S(2)}, u32[]{:S(2)}) collective-permute-start(bf16[4,64,640]{2,1,0:T(8,128)(2,1)S(1)} %collective-permute-done.5.refs_1_), channel_id=1, source_target_pairs={{0,14},{2,0},{4,2},{6,4},{8,6},{10,8},{12,10},{14,12},{1,15},{3,1}... | collective-permute-start | bytes 983048 | tf_op jit(solution)/shard_map/ppermute | solution.py:316
  29.9 5.0 %collective-permute-start.9 = (bf16[64,1664]{1,0:T(8,128)(2,1)S(1)}, bf16[64,1664]{1,0:T(8,128)(2,1)S(1)}, u32[]{:S(2)}, u32[]{:S(2)}) collective-permute-start(bf16[64,1664]{1,0:T(8,128)(2,1)S(1)} %copy-done.4), channel_id=1, source_target_pairs={{0,129},{1,0},{128,1},{129,128},{2,131},{3,2},{130,3},{131,130},{4... | collective-permute-start | bytes 638984 | tf_op jit(solution)/shard_map/ppermute | solution.py:315
  32.6 10.5 %copy-start.2 = (bf16[8,512,128]{2,1,0:T(8,128)(2,1)S(1)}, bf16[8,512,128]{2,1,0:T(8,128)(2,1)}, u32[]{:S(2)}) copy-start(bf16[8,512,128]{2,1,0:T(8,128)(2,1)} %refs_3_.7) | copy-start | bytes 3145732
  35.0 9.3 %collective-permute-start.12 = (bf16[4,64,1664]{2,1,0:T(8,128)(2,1)S(1)}, bf16[4,64,1664]{2,1,0:T(8,128)(2,1)S(1)}, u32[]{:S(2)}, u32[]{:S(2)}) collective-permute-start(bf16[4,64,1664]{2,1,0:T(8,128)(2,1)S(1)} %pad_maximum_fusion.refs_0_), channel_id=1, source_target_pairs={{0,64},{64,0},{1,65},{65,1},{2,66},{66,2},{3,67},{67,3},{4,68},{68... | collective-permute-start | bytes 2555912 | tf_op jit(solution)/shard_map/ppermute | solution.py:314
  40.4 10.5 %collective-permute-start.10 = (bf16[4,64,640]{2,1,0:T(8,128)(2,1)S(1)}, bf16[4,64,640]{2,1,0:T(8,128)(2,1)S(1)}, u32[]{:S(2)}, u32[]{:S(2)}) collective-permute-start(bf16[4,64,640]{2,1,0:T(8,128)(2,1)S(1)} %collective-permute-done.7.refs_0_), channel_id=1, source_target_pairs={{0,2},{2,4},{4,6},{6,8},{8,10},{10,12},{12,14},{14,0},{1,3},{3,5},... | collective-permute-start | bytes 983048 | tf_op jit(solution)/shard_map/ppermute | solution.py:316
  40.4 10.5 %collective-permute-start.11 = (bf16[4,64,640]{2,1,0:T(8,128)(2,1)S(1)}, bf16[4,64,640]{2,1,0:T(8,128)(2,1)S(1)}, u32[]{:S(2)}, u32[]{:S(2)}) collective-permute-start(bf16[4,64,640]{2,1,0:T(8,128)(2,1)S(1)} %collective-permute-done.8.refs_1_), channel_id=1, source_target_pairs={{0,14},{2,0},{4,2},{6,4},{8,6},{10,8},{12,10},{14,12},{1,15},{3,1}... | collective-permute-start | bytes 983048 | tf_op jit(solution)/shard_map/ppermute | solution.py:316
  52.2 7.5 %collective-permute-start.14 = (bf16[2,64,640]{2,1,0:T(8,128)(2,1)S(1)}, bf16[2,64,640]{2,1,0:T(8,128)(2,1)S(1)}, u32[]{:S(2)}, u32[]{:S(2)}) collective-permute-start(bf16[2,64,640]{2,1,0:T(8,128)(2,1)S(1)} %slice.7), channel_id=1, source_target_pairs={{0,14},{2,0},{4,2},{6,4},{8,6},{10,8},{12,10},{14,12},{1,15},{3,1}... | collective-permute-start | bytes 491528 | tf_op jit(solution)/shard_map/ppermute | solution.py:316
  54.6 5.4 %collective-permute-start.13 = (bf16[2,64,640]{2,1,0:T(8,128)(2,1)S(1)}, bf16[2,64,640]{2,1,0:T(8,128)(2,1)S(1)}, u32[]{:S(2)}, u32[]{:S(2)}) collective-permute-start(bf16[2,64,640]{2,1,0:T(8,128)(2,1)S(1)} %slice.6), channel_id=1, source_target_pairs={{0,2},{2,4},{4,6},{6,8},{8,10},{10,12},{12,14},{14,0},{1,3},{3,5},... | collective-permute-start | bytes 491528 | tf_op jit(solution)/shard_map/ppermute | solution.py:316
  60.0 7.3 %collective-permute-start.15 = (bf16[4,64,1152]{2,1,0:T(8,128)(2,1)S(1)}, bf16[4,64,1152]{2,1,0:T(8,128)(2,1)S(1)}, u32[]{:S(2)}, u32[]{:S(2)}) collective-permute-start(bf16[4,64,1152]{2,1,0:T(8,128)(2,1)S(1)} %get-tuple-element.121), channel_id=1, source_target_pairs={{0,64},{64,0},{1,65},{65,1},{2,66},{66,2},{3,67},{67,3},{4,68},{68... | collective-permute-start | bytes 1769480 | tf_op jit(solution)/shard_map/ppermute | solution.py:314
  62.6 4.6 %collective-permute-start.16 = (bf16[4,64,1152]{2,1,0:T(8,128)(2,1)S(1)}, bf16[4,64,1152]{2,1,0:T(8,128)(2,1)S(1)}, u32[]{:S(2)}, u32[]{:S(2)}) collective-permute-start(bf16[4,64,1152]{2,1,0:T(8,128)(2,1)S(1)} %get-tuple-element.122), channel_id=1, source_target_pairs={{0,64},{64,0},{1,65},{65,1},{2,66},{66,2},{3,67},{67,3},{4,68},{68... | collective-permute-start | bytes 1769480 | tf_op jit(solution)/shard_map/ppermute | solution.py:314
  66.7 2.2 %collective-permute-start.17 = (bf16[4,64,1152]{2,1,0:T(8,128)(2,1)S(1)}, bf16[4,64,1152]{2,1,0:T(8,128)(2,1)S(1)}, u32[]{:S(2)}, u32[]{:S(2)}) collective-permute-start(bf16[4,64,1152]{2,1,0:T(8,128)(2,1)S(1)} %get-tuple-element.123), channel_id=1, source_target_pairs={{0,64},{64,0},{1,65},{65,1},{2,66},{66,2},{3,67},{67,3},{4,68},{68... | collective-permute-start | bytes 1769480 | tf_op jit(solution)/shard_map/ppermute | solution.py:314
  69.6 6.7 %collective-permute-start.18 = (bf16[64,1152]{1,0:T(8,128)(2,1)S(1)}, bf16[64,1152]{1,0:T(8,128)(2,1)S(1)}, u32[]{:S(2)}, u32[]{:S(2)}) collective-permute-start(bf16[64,1152]{1,0:T(8,128)(2,1)S(1)} %merge.2), channel_id=1, source_target_pairs={{0,128},{1,129},{128,0},{129,1},{2,130},{3,131},{130,2},{131,3},{4... | collective-permute-start | bytes 442376 | tf_op jit(solution)/shard_map/ppermute | solution.py:315
  73.7 6.9 %copy-start.3 = (s32[64]{0:T(128)S(1)}, s32[64]{0:T(128)}, u32[]{:S(2)}) copy-start(s32[64]{0:T(128)} %pos_ref.3) | copy-start | bytes 772
  73.7 6.0 %collective-permute-start.19 = (bf16[64,1152]{1,0:T(8,128)(2,1)S(1)}, bf16[64,1152]{1,0:T(8,128)(2,1)S(1)}, u32[]{:S(2)}, u32[]{:S(2)}) collective-permute-start(bf16[64,1152]{1,0:T(8,128)(2,1)S(1)} %get-tuple-element.131), channel_id=1, source_target_pairs={{0,129},{1,0},{128,1},{129,128},{2,131},{3,2},{130,3},{131,130},{4... | collective-permute-start | bytes 442376 | tf_op jit(solution)/shard_map/ppermute | solution.py:315
  74.9 5.6 %collective-permute-start.20 = (bf16[64,1152]{1,0:T(8,128)(2,1)S(1)}, bf16[64,1152]{1,0:T(8,128)(2,1)S(1)}, u32[]{:S(2)}, u32[]{:S(2)}) collective-permute-start(bf16[64,1152]{1,0:T(8,128)(2,1)S(1)} %get-tuple-element.132), channel_id=1, source_target_pairs={{0,1},{1,128},{128,129},{129,0},{2,3},{3,130},{130,131},{131,2},{4... | collective-permute-start | bytes 442376 | tf_op jit(solution)/shard_map/ppermute | solution.py:315

commit v5 on v4

--- a/solution.py
+++ b/solution.py
@@ -339,9 +339,9 @@
     partials = [attend(near, far, first, True)]
     up, down, second, partials = lax.optimization_barrier((up, down, second, partials))
 
-    blocks = [up, down]
     half = Y_SIZE // 2
-    up, down = along(up[:half], 1), along(down[half:], -1)
+    blocks, ends = lax.optimization_barrier(([up, down], [up[:half], down[half:]]))
+    up, down = along(ends[0], 1), along(ends[1], -1)
     second.append(expand(blocks, w_uk, w_uv))
     partials.append(attend(near, far, second, False))
     up, down, partials = lax.optimization_barrier((up, down, partials))

time: 82.8 us -> 81.7 us (0.987)
    ppermute x4, starting transfers between devices: 8.59 us -> 7.48 us  [body(): swap = lambda block: lax.ppermute(block, 'core', [(0, 1), (1, 0)])]
  transfers between devices with their start and end apart: 21 -> 21, of which waited for: 12 -> 11; matrix products, arithmetic and copies ran while one was open for 1% -> 1% of each run, Pallas kernels for 23% -> 25%
where the time goes in v5:
time: 81.7 us; the launch traced here: 81.5 us
  starting transfers between devices  35.7 us (44%)
  Pallas kernels  25.8 us (32%)
  waiting for transfers between devices  17.6 us (22%)
  local copies, waits for them, and re-layouts  1.28 us (2%)
  other arithmetic  1.11 us (1%)
    ppermute x8, starting transfers between devices, body(): along = lambda block, by: lax.ppermute(block, 'z', shift(Z_SIZE, by))  13.8 us
    pallas_call x3, Pallas kernels, attend(): pl.pallas_call(functools.partial(attend_kernel, len(chunks), own), in_spe...  12.9 us
    ppermute x6, starting transfers between devices, body(): across = lambda block, by: lax.ppermute(block, ACROSS, shift(X_SIZE, by))  10 us
    ppermute x6, waiting for transfers between devices, body(): across = lambda block, by: lax.ppermute(block, ACROSS, shift(X_SIZE, by))  9.01 us
    ppermute x4, starting transfers between devices, body(): swap = lambda block: lax.ppermute(block, 'core', [(0, 1), (1, 0)])  7.48 us
    pallas_call x5, Pallas kernels, expand(): pl.pallas_call(functools.partial(expand_kernel, len(blocks)), in_specs=[V...  5.92 us
    ppermute x3, starting transfers between devices, body(): lax.ppermute(key_rows, 'y', shift(Y_SIZE, by))  4.38 us
    ppermute x3, waiting for transfers between devices, body(): lax.ppermute(key_rows, 'y', shift(Y_SIZE, by))  4.02 us
  transfers between devices with their start and end apart: 21, of which 11 were waited for; matrix products, arithmetic and copies ran while one was open for 1% of the time, Pallas kernels for 25%

profile of v5, /device:TPU:1, one launch (start us, length us, event | category | flops | bytes accessed | tf_op | source)
XLA Modules:
  0.0 81.5 jit_solution(7817571590437620865)
XLA Ops:
  0.0 0.0 copy-start
  0.0 2.7 %rows.1 = (bf16[64,640]{1,0:T(8,128)(2,1)}, bf16[64,1664]{1,0:T(8,128)(2,1)}) custom-call(s32[64]{0:T(128)} %pos_ref.3, f32[512,2,128]{2,1,0:T(2,128)} %constant.4.clone.low_ref.high_ref, f32[512,2,128]{2,1,0:T(2,128)} %constant.4.clone.low_ref.high_ref, f32[2,32,128]{2,1,0:T(8,128)} %constant.5.clone.step_ref, bf16[64,1024]{1,0:T(8,128)(2,1)} %qn_ref.1, ...), custom_call_target="tpu_custom_call" | custom-call | tf_op jit(solution)/shard_map/rows/pallas_call | solution.py:291
  2.7 2.0 %collective-permute-start.3 = (bf16[64,1664]{1,0:T(8,128)(2,1)}, bf16[64,1664]{1,0:T(8,128)(2,1)S(1)}, u32[]{:S(2)}, u32[]{:S(2)}) collective-permute-start(bf16[64,1664]{1,0:T(8,128)(2,1)} %get-tuple-element.82), channel_id=1, source_target_pairs={{0,1},{1,128},{128,129},{129,0},{2,3},{3,130},{130,131},{131,2},{4... | collective-permute-start | bytes 638984 | tf_op jit(solution)/shard_map/ppermute | solution.py:315
  4.7 2.9 %collective-permute-start.2 = (bf16[64,640]{1,0:T(8,128)(2,1)}, bf16[64,640]{1,0:T(8,128)(2,1)S(1)}, u32[]{:S(2)}, u32[]{:S(2)}) collective-permute-start(bf16[64,640]{1,0:T(8,128)(2,1)} %get-tuple-element.73), channel_id=1, source_target_pairs={{0,32},{16,48},{32,0},{48,16},{1,33},{17,49},{33,1},{49,17},{2,34}... | collective-permute-start | bytes 245768 | tf_op jit(solution)/shard_map/ppermute | solution.py:318
  7.6 0.8 collective-permute-start.1
  8.4 0.7 collective-permute-start
  9.1 0.6 collective-permute-done.2
  9.7 2.3 %collective-permute-done.1 = bf16[64,640]{1,0:T(8,128)(2,1)S(1)} collective-permute-done((bf16[64,640]{1,0:T(8,128)(2,1)}, bf16[64,640]{1,0:T(8,128)(2,1)S(1)}, u32[]{:S(2)}, u32[]{:S(2)}) %collective-permute-start.1) | collective-permute-done | bytes 81952 | tf_op jit(solution)/shard_map/ppermute | solution.py:318
  12.0 1.1 %collective-permute-done = bf16[64,640]{1,0:T(8,128)(2,1)S(1)} collective-permute-done((bf16[64,640]{1,0:T(8,128)(2,1)}, bf16[64,640]{1,0:T(8,128)(2,1)S(1)}, u32[]{:S(2)}, u32[]{:S(2)}) %collective-permute-start) | collective-permute-done | bytes 81952 | tf_op jit(solution)/shard_map/ppermute | solution.py:318
  13.1 1.0 %pad_maximum_fusion.1.refs_0_ = bf16[4,64,640]{2,1,0:T(8,128)(2,1)S(1)} fusion(bf16[1,64,640]{2,1,0:T(8,128)(2,1)S(1)} %bitcast.20, bf16[1,64,640]{2,1,0:T(8,128)(2,1)S(1)} %bitcast.21, bf16[1,64,640]{2,1,0:T(8,128)(2,1)S(1)} %bitcast.22, bf16[1,64,640]{2,1,0:T(8,128)(2,1)} %bitcast.19), kind=kLoop, calls=%fused_computation.1 | loop fusion | flops 491520 | bytes 655360 | tf_op jit(solution)/shard_map/stack | solution.py:319
  14.1 0.0 collective-permute-done.3
  14.1 5.7 %collective-permute-start.5 = (bf16[4,64,640]{2,1,0:T(8,128)(2,1)S(1)}, bf16[4,64,640]{2,1,0:T(8,128)(2,1)S(1)}, u32[]{:S(2)}, u32[]{:S(2)}) collective-permute-start(bf16[4,64,640]{2,1,0:T(8,128)(2,1)S(1)} %pad_maximum_fusion.1.refs_0_), channel_id=1, source_target_pairs={{0,14},{2,0},{4,2},{6,4},{8,6},{10,8},{12,10},{14,12},{1,15},{3,1}... | collective-permute-start | bytes 983048 | tf_op jit(solution)/shard_map/ppermute | solution.py:316
  19.8 0.0 collective-permute-start.4
  19.8 0.0 copy-done.4
  19.8 2.5 %collective-permute-start.6 = (bf16[64,1664]{1,0:T(8,128)(2,1)S(1)}, bf16[64,1664]{1,0:T(8,128)(2,1)S(1)}, u32[]{:S(2)}, u32[]{:S(2)}) collective-permute-start(bf16[64,1664]{1,0:T(8,128)(2,1)S(1)} %copy-done.4), channel_id=1, source_target_pairs={{0,128},{1,129},{128,0},{129,1},{2,130},{3,131},{130,2},{131,3},{4... | collective-permute-start | bytes 638984 | tf_op jit(solution)/shard_map/ppermute | solution.py:315
  22.2 0.0 copy-done
  22.2 1.2 %copy-done.1 = bf16[8,512,128]{2,1,0:T(8,128)(2,1)S(1)} copy-done((bf16[8,512,128]{2,1,0:T(8,128)(2,1)S(1)}, bf16[8,512,128]{2,1,0:T(8,128)(2,1)}, u32[]{:S(2)}) %copy-start.1) | copy-done | bytes 1048600
  23.4 1.1 %expand.5 = (bf16[2,128,1024]{2,1,0:T(8,128)(2,1)S(1)}, bf16[2,128,1024]{2,1,0:T(8,128)(2,1)S(1)}, bf16[2,128,128]{2,1,0:T(8,128)(2,1)S(1)}) custom-call(bf16[4,64,640]{2,1,0:T(8,128)(2,1)S(1)} %pad_maximum_fusion.1.refs_0_, bf16[1024,512]{1,0:T(8,128)(2,1)S(1)} %bitcast.10, bf16[8,512,128]{2,1,0:T(8,128)(2,1)S(1)} %copy-done.1), custom_call_target="tpu_custom_call" | custom-call | flops 536870912 | bytes 3633152 | tf_op jit(solution)/shard_map/expand/pallas_call | solution.py:107
  24.5 1.4 %collective-permute-done.6 = bf16[64,1664]{1,0:T(8,128)(2,1)S(1)} collective-permute-done((bf16[64,1664]{1,0:T(8,128)(2,1)S(1)}, bf16[64,1664]{1,0:T(8,128)(2,1)S(1)}, u32[]{:S(2)}, u32[]{:S(2)}) %collective-permute-start.6) | collective-permute-done | bytes 213024 | tf_op jit(solution)/shard_map/ppermute | solution.py:315
  26.0 0.0 collective-permute-done.5.refs_1_
  26.0 1.3 %collective-permute-done.4.refs_0_ = bf16[4,64,640]{2,1,0:T(8,128)(2,1)S(1)} collective-permute-done((bf16[4,64,640]{2,1,0:T(8,128)(2,1)S(1)}, bf16[4,64,640]{2,1,0:T(8,128)(2,1)S(1)}, u32[]{:S(2)}, u32[]{:S(2)}) %collective-permute-start.4) | collective-permute-done | bytes 327712 | tf_op jit(solution)/shard_map/ppermute | solution.py:316
  27.2 0.0 collective-permute-start.7
  27.2 2.7 %collective-permute-start.8 = (bf16[4,64,640]{2,1,0:T(8,128)(2,1)S(1)}, bf16[4,64,640]{2,1,0:T(8,128)(2,1)S(1)}, u32[]{:S(2)}, u32[]{:S(2)}) collective-permute-start(bf16[4,64,640]{2,1,0:T(8,128)(2,1)S(1)} %collective-permute-done.5.refs_1_), channel_id=1, source_target_pairs={{0,14},{2,0},{4,2},{6,4},{8,6},{10,8},{12,10},{14,12},{1,15},{3,1}... | collective-permute-start | bytes 983048 | tf_op jit(solution)/shard_map/ppermute | solution.py:316
  29.9 1.5 %collective-permute-start.9 = (bf16[64,1664]{1,0:T(8,128)(2,1)S(1)}, bf16[64,1664]{1,0:T(8,128)(2,1)S(1)}, u32[]{:S(2)}, u32[]{:S(2)}) collective-permute-start(bf16[64,1664]{1,0:T(8,128)(2,1)S(1)} %copy-done.4), channel_id=1, source_target_pairs={{0,129},{1,0},{128,1},{129,128},{2,131},{3,2},{130,3},{131,130},{4... | collective-permute-start | bytes 638984 | tf_op jit(solution)/shard_map/ppermute | solution.py:315
  31.4 1.3 %expand.6 = (bf16[2,256,1024]{2,1,0:T(8,128)(2,1)S(1)}, bf16[2,256,1024]{2,1,0:T(8,128)(2,1)S(1)}, bf16[2,256,128]{2,1,0:T(8,128)(2,1)S(1)}) custom-call(bf16[4,64,640]{2,1,0:T(8,128)(2,1)S(1)} %collective-permute-done.4.refs_0_, bf16[4,64,640]{2,1,0:T(8,128)(2,1)S(1)} %collective-permute-done.5.refs_1_, bf16[1024,512]{1,0:T(8,128)(2,1)S(1)} %bitcast.11, ...), custom_call_target="tpu_custom_call" | custom-call | flops 1073741824 | bytes 5169152 | tf_op jit(solution)/shard_map/expand/pallas_call | solution.py:107
  32.6 0.0 copy-start.2
  32.7 2.2 %collective-permute-done.9 = bf16[64,1664]{1,0:T(8,128)(2,1)S(1)} collective-permute-done((bf16[64,1664]{1,0:T(8,128)(2,1)S(1)}, bf16[64,1664]{1,0:T(8,128)(2,1)S(1)}, u32[]{:S(2)}, u32[]{:S(2)}) %collective-permute-start.9) | collective-permute-done | bytes 213024 | tf_op jit(solution)/shard_map/ppermute | solution.py:315
  34.9 0.0 collective-permute-done.7.refs_0_
  34.9 0.0 collective-permute-done.8.refs_1_
  34.9 0.1 pad_maximum_fusion.refs_0_
  35.0 5.4 %collective-permute-start.12 = (bf16[4,64,1664]{2,1,0:T(8,128)(2,1)S(1)}, bf16[4,64,1664]{2,1,0:T(8,128)(2,1)S(1)}, u32[]{:S(2)}, u32[]{:S(2)}) collective-permute-start(bf16[4,64,1664]{2,1,0:T(8,128)(2,1)S(1)} %pad_maximum_fusion.refs_0_), channel_id=1, source_target_pairs={{0,64},{64,0},{1,65},{65,1},{2,66},{66,2},{3,67},{67,3},{4,68},{68... | collective-permute-start | bytes 2555912 | tf_op jit(solution)/shard_map/ppermute | solution.py:314
  40.4 0.0 collective-permute-start.10
  40.4 2.7 %collective-permute-start.11 = (bf16[4,64,640]{2,1,0:T(8,128)(2,1)S(1)}, bf16[4,64,640]{2,1,0:T(8,128)(2,1)S(1)}, u32[]{:S(2)}, u32[]{:S(2)}) collective-permute-start(bf16[4,64,640]{2,1,0:T(8,128)(2,1)S(1)} %collective-permute-done.8.refs_1_), channel_id=1, source_target_pairs={{0,14},{2,0},{4,2},{6,4},{8,6},{10,8},{12,10},{14,12},{1,15},{3,1}... | collective-permute-start | bytes 983048 | tf_op jit(solution)/shard_map/ppermute | solution.py:316
  43.1 0.0 copy-done.2
  43.1 1.3 %expand.7 = (bf16[2,256,1024]{2,1,0:T(8,128)(2,1)S(1)}, bf16[2,256,1024]{2,1,0:T(8,128)(2,1)S(1)}, bf16[2,256,128]{2,1,0:T(8,128)(2,1)S(1)}) custom-call(bf16[4,64,640]{2,1,0:T(8,128)(2,1)S(1)} %collective-permute-done.7.refs_0_, bf16[4,64,640]{2,1,0:T(8,128)(2,1)S(1)} %collective-permute-done.8.refs_1_, bf16[1024,512]{1,0:T(8,128)(2,1)S(1)} %bitcast.12, ...), custom_call_target="tpu_custom_call" | custom-call | flops 1073741824 | bytes 5169152 | tf_op jit(solution)/shard_map/expand/pallas_call | solution.py:107
  44.4 0.0 collective-permute-done.12.refs_1_
  44.4 4.9 %attend.3 = (bf16[4,64,1152]{2,1,0:T(8,128)(2,1)S(1)}, bf16[4,64,1152]{2,1,0:T(8,128)(2,1)S(1)}) custom-call(bf16[4,64,1664]{2,1,0:T(8,128)(2,1)S(1)} %pad_maximum_fusion.refs_0_, bf16[4,64,1664]{2,1,0:T(8,128)(2,1)S(1)} %collective-permute-done.12.refs_1_, bf16[2,128,1024]{2,1,0:T(8,128)(2,1)S(1)} %get-tuple-element.97.refs_2_, ...), custom_call_target="tpu_custom_call" | custom-call | flops 3840000000 | bytes 8388608 | tf_op jit(solution)/shard_map/attend/pallas_call | solution.py:222
  49.3 1.6 %collective-permute-done.10.refs_0_ = bf16[4,64,640]{2,1,0:T(8,128)(2,1)S(1)} collective-permute-done((bf16[4,64,640]{2,1,0:T(8,128)(2,1)S(1)}, bf16[4,64,640]{2,1,0:T(8,128)(2,1)S(1)}, u32[]{:S(2)}, u32[]{:S(2)}) %collective-permute-start.10) | collective-permute-done | bytes 327712 | tf_op jit(solution)/shard_map/ppermute | solution.py:316
  50.9 0.0 collective-permute-done.11.refs_1_
  50.9 0.1 collective-permute-start.13
  51.0 2.7 %collective-permute-start.14 = (bf16[2,64,640]{2,1,0:T(8,128)(2,1)S(1)}, bf16[2,64,640]{2,1,0:T(8,128)(2,1)S(1)}, u32[]{:S(2)}, u32[]{:S(2)}) collective-permute-start(bf16[2,64,640]{2,1,0:T(8,128)(2,1)S(1)} %slice.7), channel_id=1, source_target_pairs={{0,14},{2,0},{4,2},{6,4},{8,6},{10,8},{12,10},{14,12},{1,15},{3,1}... | collective-permute-start | bytes 491528 | tf_op jit(solution)/shard_map/ppermute | solution.py:316
  53.7 1.3 %expand.8 = (bf16[2,256,1024]{2,1,0:T(8,128)(2,1)S(1)}, bf16[2,256,1024]{2,1,0:T(8,128)(2,1)S(1)}, bf16[2,256,128]{2,1,0:T(8,128)(2,1)S(1)}) custom-call(bf16[4,64,640]{2,1,0:T(8,128)(2,1)S(1)} %collective-permute-done.10.refs_0_, bf16[4,64,640]{2,1,0:T(8,128)(2,1)S(1)} %collective-permute-done.11.refs_1_, bf16[1024,512]{1,0:T(8,128)(2,1)S(1)} %bitcast.13, ...), custom_call_target="tpu_custom_call" | custom-call | flops 1073741824 | bytes 5169152 | tf_op jit(solution)/shard_map/expand/pallas_call | solution.py:107
  55.0 5.0 %attend.4 = (bf16[4,64,1152]{2,1,0:T(8,128)(2,1)S(1)}, bf16[4,64,1152]{2,1,0:T(8,128)(2,1)S(1)}) custom-call(bf16[4,64,1664]{2,1,0:T(8,128)(2,1)S(1)} %pad_maximum_fusion.refs_0_, bf16[4,64,1664]{2,1,0:T(8,128)(2,1)S(1)} %collective-permute-done.12.refs_1_, bf16[2,256,1024]{2,1,0:T(8,128)(2,1)S(1)} %get-tuple-element.111.refs_2_, ...), custom_call_target="tpu_custom_call" | custom-call | flops 5120000000 | bytes 8388608 | tf_op jit(solution)/shard_map/attend/pallas_call | solution.py:222
  60.0 0.0 collective-permute-done.13.refs_0_
  60.0 0.0 collective-permute-done.14.refs_1_
  60.0 1.5 %collective-permute-start.15 = (bf16[4,64,1152]{2,1,0:T(8,128)(2,1)S(1)}, bf16[4,64,1152]{2,1,0:T(8,128)(2,1)S(1)}, u32[]{:S(2)}, u32[]{:S(2)}) collective-permute-start(bf16[4,64,1152]{2,1,0:T(8,128)(2,1)S(1)} %get-tuple-element.129), channel_id=1, source_target_pairs={{0,64},{64,0},{1,65},{65,1},{2,66},{66,2},{3,67},{67,3},{4,68},{68... | collective-permute-start | bytes 1769480 | tf_op jit(solution)/shard_map/ppermute | solution.py:314
  61.5 0.1 collective-permute-start.16
  61.6 1.1 %expand.9 = (bf16[2,128,1024]{2,1,0:T(8,128)(2,1)S(1)}, bf16[2,128,1024]{2,1,0:T(8,128)(2,1)S(1)}, bf16[2,128,128]{2,1,0:T(8,128)(2,1)S(1)}) custom-call(bf16[2,64,640]{2,1,0:T(8,128)(2,1)S(1)} %collective-permute-done.13.refs_0_, bf16[2,64,640]{2,1,0:T(8,128)(2,1)S(1)} %collective-permute-done.14.refs_1_, bf16[1024,512]{1,0:T(8,128)(2,1)S(1)} %bitcast.14, ...), custom_call_target="tpu_custom_call" | custom-call | flops 536870912 | bytes 3633152 | tf_op jit(solution)/shard_map/expand/pallas_call | solution.py:107
  62.7 3.0 %attend.5 = (bf16[4,64,1152]{2,1,0:T(8,128)(2,1)S(1)}, bf16[4,64,1152]{2,1,0:T(8,128)(2,1)S(1)}) custom-call(bf16[4,64,1664]{2,1,0:T(8,128)(2,1)S(1)} %pad_maximum_fusion.refs_0_, bf16[4,64,1664]{2,1,0:T(8,128)(2,1)S(1)} %collective-permute-done.12.refs_1_, bf16[2,128,1024]{2,1,0:T(8,128)(2,1)S(1)} %get-tuple-element.125.refs_2_, ...), custom_call_target="tpu_custom_call" | custom-call | flops 1280000000 | bytes 8388608 | tf_op jit(solution)/shard_map/attend/pallas_call | solution.py:222
  65.7 0.5 collective-permute-start.17
  66.2 0.0 collective-permute-done.15.refs_3_
  66.2 0.0 collective-permute-done.16.refs_4_
  66.2 1.6 %collective-permute-done.17.refs_5_ = bf16[4,64,1152]{2,1,0:T(8,128)(2,1)S(1)} collective-permute-done((bf16[4,64,1152]{2,1,0:T(8,128)(2,1)S(1)}, bf16[4,64,1152]{2,1,0:T(8,128)(2,1)S(1)}, u32[]{:S(2)}, u32[]{:S(2)}) %collective-permute-start.17) | collective-permute-done | bytes 589856 | tf_op jit(solution)/shard_map/ppermute | solution.py:314
  67.8 0.7 merge.2
  68.5 2.5 %collective-permute-start.18 = (bf16[64,1152]{1,0:T(8,128)(2,1)S(1)}, bf16[64,1152]{1,0:T(8,128)(2,1)S(1)}, u32[]{:S(2)}, u32[]{:S(2)}) collective-permute-start(bf16[64,1152]{1,0:T(8,128)(2,1)S(1)} %merge.2), channel_id=1, source_target_pairs={{0,128},{1,129},{128,0},{129,1},{2,130},{3,131},{130,2},{131,3},{4... | collective-permute-start | bytes 442376 | tf_op jit(solution)/shard_map/ppermute | solution.py:315
  71.0 1.6 %merge.3 = (bf16[64,1152]{1,0:T(8,128)(2,1)S(1)}, bf16[64,1152]{1,0:T(8,128)(2,1)S(1)}) custom-call(bf16[4,64,1152]{2,1,0:T(8,128)(2,1)S(1)} %get-tuple-element.132.refs_0_, bf16[4,64,1152]{2,1,0:T(8,128)(2,1)S(1)} %get-tuple-element.133.refs_1_, bf16[4,64,1152]{2,1,0:T(8,128)(2,1)S(1)} %get-tuple-element.134.refs_2_, ...), custom_call_target="tpu_custom_call" | custom-call | tf_op jit(solution)/shard_map/merge/pallas_call | solution.py:257
  72.6 0.0 copy-start.3
  72.6 1.2 %collective-permute-start.19 = (bf16[64,1152]{1,0:T(8,128)(2,1)S(1)}, bf16[64,1152]{1,0:T(8,128)(2,1)S(1)}, u32[]{:S(2)}, u32[]{:S(2)}) collective-permute-start(bf16[64,1152]{1,0:T(8,128)(2,1)S(1)} %get-tuple-element.139), channel_id=1, source_target_pairs={{0,129},{1,0},{128,1},{129,128},{2,131},{3,2},{130,3},{131,130},{4... | collective-permute-start | bytes 442376 | tf_op jit(solution)/shard_map/ppermute | solution.py:315
  73.8 0.3 collective-permute-start.20
  74.1 1.0 %collective-permute-done.18.refs_6_ = bf16[64,1152]{1,0:T(8,128)(2,1)S(1)} collective-permute-done((bf16[64,1152]{1,0:T(8,128)(2,1)S(1)}, bf16[64,1152]{1,0:T(8,128)(2,1)S(1)}, u32[]{:S(2)}, u32[]{:S(2)}) %collective-permute-start.18) | collective-permute-done | bytes 147488 | tf_op jit(solution)/shard_map/ppermute | solution.py:315
  75.1 3.4 %collective-permute-done.19.refs_7_ = bf16[64,1152]{1,0:T(8,128)(2,1)S(1)} collective-permute-done((bf16[64,1152]{1,0:T(8,128)(2,1)S(1)}, bf16[64,1152]{1,0:T(8,128)(2,1)S(1)}, u32[]{:S(2)}, u32[]{:S(2)}) %collective-permute-start.19) | collective-permute-done | bytes 147488 | tf_op jit(solution)/shard_map/ppermute | solution.py:315
  78.6 0.9 %collective-permute-done.20.refs_8_ = bf16[64,1152]{1,0:T(8,128)(2,1)S(1)} collective-permute-done((bf16[64,1152]{1,0:T(8,128)(2,1)S(1)}, bf16[64,1152]{1,0:T(8,128)(2,1)S(1)}, u32[]{:S(2)}, u32[]{:S(2)}) %collective-permute-start.20) | collective-permute-done | bytes 147488 | tf_op jit(solution)/shard_map/ppermute | solution.py:315
  79.5 0.0 copy-done.3
  79.5 2.1 %combine.1 = bf16[64,1024]{1,0:T(8,128)(2,1)} custom-call(s32[64]{0:T(128)S(1)} %copy-done.3, bf16[4,64,1152]{2,1,0:T(8,128)(2,1)S(1)} %get-tuple-element.132.refs_0_, bf16[4,64,1152]{2,1,0:T(8,128)(2,1)S(1)} %get-tuple-element.133.refs_1_, bf16[4,64,1152]{2,1,0:T(8,128)(2,1)S(1)} %get-tuple-element.134.refs_2_, ...), custom_call_target="tpu_custom_call" | custom-call | tf_op jit(solution)/shard_map/combine/pallas_call | solution.py:358
  (4 shorter events, 0.0 us)
Async XLA Ops:
  0.0 22.2 %copy-start = (bf16[8,128,512]{2,1,0:T(8,128)(2,1)S(1)}, bf16[8,128,512]{2,1,0:T(8,128)(2,1)}, u32[]{:S(2)}) copy-start(bf16[8,128,512]{2,1,0:T(8,128)(2,1)} %param.14) | copy-start | bytes 3145732
  2.7 11.4 %collective-permute-start.3 = (bf16[64,1664]{1,0:T(8,128)(2,1)}, bf16[64,1664]{1,0:T(8,128)(2,1)S(1)}, u32[]{:S(2)}, u32[]{:S(2)}) collective-permute-start(bf16[64,1664]{1,0:T(8,128)(2,1)} %get-tuple-element.82), channel_id=1, source_target_pairs={{0,1},{1,128},{128,129},{129,0},{2,3},{3,130},{130,131},{131,2},{4... | collective-permute-start | bytes 638984 | tf_op jit(solution)/shard_map/ppermute | solution.py:315
  4.7 5.0 %collective-permute-start.2 = (bf16[64,640]{1,0:T(8,128)(2,1)}, bf16[64,640]{1,0:T(8,128)(2,1)S(1)}, u32[]{:S(2)}, u32[]{:S(2)}) collective-permute-start(bf16[64,640]{1,0:T(8,128)(2,1)} %get-tuple-element.73), channel_id=1, source_target_pairs={{0,32},{16,48},{32,0},{48,16},{1,33},{17,49},{33,1},{49,17},{2,34}... | collective-permute-start | bytes 245768 | tf_op jit(solution)/shard_map/ppermute | solution.py:318
  7.6 4.4 %collective-permute-start.1 = (bf16[64,640]{1,0:T(8,128)(2,1)}, bf16[64,640]{1,0:T(8,128)(2,1)S(1)}, u32[]{:S(2)}, u32[]{:S(2)}) collective-permute-start(bf16[64,640]{1,0:T(8,128)(2,1)} %get-tuple-element.73), channel_id=1, source_target_pairs={{0,48},{16,0},{32,16},{48,32},{1,49},{17,1},{33,17},{49,33},{2,50}... | collective-permute-start | bytes 245768 | tf_op jit(solution)/shard_map/ppermute | solution.py:318
  8.4 4.7 %collective-permute-start = (bf16[64,640]{1,0:T(8,128)(2,1)}, bf16[64,640]{1,0:T(8,128)(2,1)S(1)}, u32[]{:S(2)}, u32[]{:S(2)}) collective-permute-start(bf16[64,640]{1,0:T(8,128)(2,1)} %get-tuple-element.73), channel_id=1, source_target_pairs={{0,16},{16,32},{32,48},{48,0},{1,17},{17,33},{33,49},{49,1},{2,18}... | collective-permute-start | bytes 245768 | tf_op jit(solution)/shard_map/ppermute | solution.py:318
  13.1 6.7 %copy-start.4 = (bf16[64,1664]{1,0:T(8,128)(2,1)S(1)}, bf16[64,1664]{1,0:T(8,128)(2,1)}, u32[]{:S(2)}) copy-start(bf16[64,1664]{1,0:T(8,128)(2,1)} %get-tuple-element.82) | copy-start | bytes 638980
  14.1 11.9 %collective-permute-start.5 = (bf16[4,64,640]{2,1,0:T(8,128)(2,1)S(1)}, bf16[4,64,640]{2,1,0:T(8,128)(2,1)S(1)}, u32[]{:S(2)}, u32[]{:S(2)}) collective-permute-start(bf16[4,64,640]{2,1,0:T(8,128)(2,1)S(1)} %pad_maximum_fusion.1.refs_0_), channel_id=1, source_target_pairs={{0,14},{2,0},{4,2},{6,4},{8,6},{10,8},{12,10},{14,12},{1,15},{3,1}... | collective-permute-start | bytes 983048 | tf_op jit(solution)/shard_map/ppermute | solution.py:316
  19.8 7.5 %collective-permute-start.4 = (bf16[4,64,640]{2,1,0:T(8,128)(2,1)S(1)}, bf16[4,64,640]{2,1,0:T(8,128)(2,1)S(1)}, u32[]{:S(2)}, u32[]{:S(2)}) collective-permute-start(bf16[4,64,640]{2,1,0:T(8,128)(2,1)S(1)} %pad_maximum_fusion.1.refs_0_), channel_id=1, source_target_pairs={{0,2},{2,4},{4,6},{6,8},{8,10},{10,12},{12,14},{14,0},{1,3},{3,5},... | collective-permute-start | bytes 983048 | tf_op jit(solution)/shard_map/ppermute | solution.py:316
  19.8 6.2 %collective-permute-start.6 = (bf16[64,1664]{1,0:T(8,128)(2,1)S(1)}, bf16[64,1664]{1,0:T(8,128)(2,1)S(1)}, u32[]{:S(2)}, u32[]{:S(2)}) collective-permute-start(bf16[64,1664]{1,0:T(8,128)(2,1)S(1)} %copy-done.4), channel_id=1, source_target_pairs={{0,128},{1,129},{128,0},{129,1},{2,130},{3,131},{130,2},{131,3},{4... | collective-permute-start | bytes 638984 | tf_op jit(solution)/shard_map/ppermute | solution.py:315
  22.2 1.2 %copy-start.1 = (bf16[8,512,128]{2,1,0:T(8,128)(2,1)S(1)}, bf16[8,512,128]{2,1,0:T(8,128)(2,1)}, u32[]{:S(2)}) copy-start(bf16[8,512,128]{2,1,0:T(8,128)(2,1)} %refs_3_.7) | copy-start | bytes 3145732
  27.2 7.7 %collective-permute-start.7 = (bf16[4,64,640]{2,1,0:T(8,128)(2,1)S(1)}, bf16[4,64,640]{2,1,0:T(8,128)(2,1)S(1)}, u32[]{:S(2)}, u32[]{:S(2)}) collective-permute-start(bf16[4,64,640]{2,1,0:T(8,128)(2,1)S(1)} %collective-permute-done.4.refs_0_), channel_id=1, source_target_pairs={{0,2},{2,4},{4,6},{6,8},{8,10},{10,12},{12,14},{14,0},{1,3},{3,5},... | collective-permute-start | bytes 983048 | tf_op jit(solution)/shard_map/ppermute | solution.py:316
  27.2 7.7 %collective-permute-start.8 = (bf16[4,64,640]{2,1,0:T(8,128)(2,1)S(1)}, bf16[4,64,640]{2,1,0:T(8,128)(2,1)S(1)}, u32[]{:S(2)}, u32[]{:S(2)}) collective-permute-start(bf16[4,64,640]{2,1,0:T(8,128)(2,1)S(1)} %collective-permute-done.5.refs_1_), channel_id=1, source_target_pairs={{0,14},{2,0},{4,2},{6,4},{8,6},{10,8},{12,10},{14,12},{1,15},{3,1}... | collective-permute-start | bytes 983048 | tf_op jit(solution)/shard_map/ppermute | solution.py:316
  29.9 5.0 %collective-permute-start.9 = (bf16[64,1664]{1,0:T(8,128)(2,1)S(1)}, bf16[64,1664]{1,0:T(8,128)(2,1)S(1)}, u32[]{:S(2)}, u32[]{:S(2)}) collective-permute-start(bf16[64,1664]{1,0:T(8,128)(2,1)S(1)} %copy-done.4), channel_id=1, source_target_pairs={{0,129},{1,0},{128,1},{129,128},{2,131},{3,2},{130,3},{131,130},{4... | collective-permute-start | bytes 638984 | tf_op jit(solution)/shard_map/ppermute | solution.py:315
  32.6 10.5 %copy-start.2 = (bf16[8,512,128]{2,1,0:T(8,128)(2,1)S(1)}, bf16[8,512,128]{2,1,0:T(8,128)(2,1)}, u32[]{:S(2)}) copy-start(bf16[8,512,128]{2,1,0:T(8,128)(2,1)} %refs_3_.7) | copy-start | bytes 3145732
  35.0 9.3 %collective-permute-start.12 = (bf16[4,64,1664]{2,1,0:T(8,128)(2,1)S(1)}, bf16[4,64,1664]{2,1,0:T(8,128)(2,1)S(1)}, u32[]{:S(2)}, u32[]{:S(2)}) collective-permute-start(bf16[4,64,1664]{2,1,0:T(8,128)(2,1)S(1)} %pad_maximum_fusion.refs_0_), channel_id=1, source_target_pairs={{0,64},{64,0},{1,65},{65,1},{2,66},{66,2},{3,67},{67,3},{4,68},{68... | collective-permute-start | bytes 2555912 | tf_op jit(solution)/shard_map/ppermute | solution.py:314
  40.4 10.5 %collective-permute-start.10 = (bf16[4,64,640]{2,1,0:T(8,128)(2,1)S(1)}, bf16[4,64,640]{2,1,0:T(8,128)(2,1)S(1)}, u32[]{:S(2)}, u32[]{:S(2)}) collective-permute-start(bf16[4,64,640]{2,1,0:T(8,128)(2,1)S(1)} %collective-permute-done.7.refs_0_), channel_id=1, source_target_pairs={{0,2},{2,4},{4,6},{6,8},{8,10},{10,12},{12,14},{14,0},{1,3},{3,5},... | collective-permute-start | bytes 983048 | tf_op jit(solution)/shard_map/ppermute | solution.py:316
  40.4 10.5 %collective-permute-start.11 = (bf16[4,64,640]{2,1,0:T(8,128)(2,1)S(1)}, bf16[4,64,640]{2,1,0:T(8,128)(2,1)S(1)}, u32[]{:S(2)}, u32[]{:S(2)}) collective-permute-start(bf16[4,64,640]{2,1,0:T(8,128)(2,1)S(1)} %collective-permute-done.8.refs_1_), channel_id=1, source_target_pairs={{0,14},{2,0},{4,2},{6,4},{8,6},{10,8},{12,10},{14,12},{1,15},{3,1}... | collective-permute-start | bytes 983048 | tf_op jit(solution)/shard_map/ppermute | solution.py:316
  50.9 9.1 %collective-permute-start.13 = (bf16[2,64,640]{2,1,0:T(8,128)(2,1)S(1)}, bf16[2,64,640]{2,1,0:T(8,128)(2,1)S(1)}, u32[]{:S(2)}, u32[]{:S(2)}) collective-permute-start(bf16[2,64,640]{2,1,0:T(8,128)(2,1)S(1)} %slice.6), channel_id=1, source_target_pairs={{0,2},{2,4},{4,6},{6,8},{8,10},{10,12},{12,14},{14,0},{1,3},{3,5},... | collective-permute-start | bytes 491528 | tf_op jit(solution)/shard_map/ppermute | solution.py:316
  51.0 9.0 %collective-permute-start.14 = (bf16[2,64,640]{2,1,0:T(8,128)(2,1)S(1)}, bf16[2,64,640]{2,1,0:T(8,128)(2,1)S(1)}, u32[]{:S(2)}, u32[]{:S(2)}) collective-permute-start(bf16[2,64,640]{2,1,0:T(8,128)(2,1)S(1)} %slice.7), channel_id=1, source_target_pairs={{0,14},{2,0},{4,2},{6,4},{8,6},{10,8},{12,10},{14,12},{1,15},{3,1}... | collective-permute-start | bytes 491528 | tf_op jit(solution)/shard_map/ppermute | solution.py:316
  60.0 6.2 %collective-permute-start.15 = (bf16[4,64,1152]{2,1,0:T(8,128)(2,1)S(1)}, bf16[4,64,1152]{2,1,0:T(8,128)(2,1)S(1)}, u32[]{:S(2)}, u32[]{:S(2)}) collective-permute-start(bf16[4,64,1152]{2,1,0:T(8,128)(2,1)S(1)} %get-tuple-element.129), channel_id=1, source_target_pairs={{0,64},{64,0},{1,65},{65,1},{2,66},{66,2},{3,67},{67,3},{4,68},{68... | collective-permute-start | bytes 1769480 | tf_op jit(solution)/shard_map/ppermute | solution.py:314
  61.5 4.6 %collective-permute-start.16 = (bf16[4,64,1152]{2,1,0:T(8,128)(2,1)S(1)}, bf16[4,64,1152]{2,1,0:T(8,128)(2,1)S(1)}, u32[]{:S(2)}, u32[]{:S(2)}) collective-permute-start(bf16[4,64,1152]{2,1,0:T(8,128)(2,1)S(1)} %get-tuple-element.130), channel_id=1, source_target_pairs={{0,64},{64,0},{1,65},{65,1},{2,66},{66,2},{3,67},{67,3},{4,68},{68... | collective-permute-start | bytes 1769480 | tf_op jit(solution)/shard_map/ppermute | solution.py:314
  65.7 2.1 %collective-permute-start.17 = (bf16[4,64,1152]{2,1,0:T(8,128)(2,1)S(1)}, bf16[4,64,1152]{2,1,0:T(8,128)(2,1)S(1)}, u32[]{:S(2)}, u32[]{:S(2)}) collective-permute-start(bf16[4,64,1152]{2,1,0:T(8,128)(2,1)S(1)} %get-tuple-element.131), channel_id=1, source_target_pairs={{0,64},{64,0},{1,65},{65,1},{2,66},{66,2},{3,67},{67,3},{4,68},{68... | collective-permute-start | bytes 1769480 | tf_op jit(solution)/shard_map/ppermute | solution.py:314
  68.5 6.7 %collective-permute-start.18 = (bf16[64,1152]{1,0:T(8,128)(2,1)S(1)}, bf16[64,1152]{1,0:T(8,128)(2,1)S(1)}, u32[]{:S(2)}, u32[]{:S(2)}) collective-permute-start(bf16[64,1152]{1,0:T(8,128)(2,1)S(1)} %merge.2), channel_id=1, source_target_pairs={{0,128},{1,129},{128,0},{129,1},{2,130},{3,131},{130,2},{131,3},{4... | collective-permute-start | bytes 442376 | tf_op jit(solution)/shard_map/ppermute | solution.py:315
  72.6 6.9 %copy-start.3 = (s32[64]{0:T(128)S(1)}, s32[64]{0:T(128)}, u32[]{:S(2)}) copy-start(s32[64]{0:T(128)} %pos_ref.3) | copy-start | bytes 772
  72.6 6.0 %collective-permute-start.19 = (bf16[64,1152]{1,0:T(8,128)(2,1)S(1)}, bf16[64,1152]{1,0:T(8,128)(2,1)S(1)}, u32[]{:S(2)}, u32[]{:S(2)}) collective-permute-start(bf16[64,1152]{1,0:T(8,128)(2,1)S(1)} %get-tuple-element.139), channel_id=1, source_target_pairs={{0,129},{1,0},{128,1},{129,128},{2,131},{3,2},{130,3},{131,130},{4... | collective-permute-start | bytes 442376 | tf_op jit(solution)/shard_map/ppermute | solution.py:315
  73.8 5.6 %collective-permute-start.20 = (bf16[64,1152]{1,0:T(8,128)(2,1)S(1)}, bf16[64,1152]{1,0:T(8,128)(2,1)S(1)}, u32[]{:S(2)}, u32[]{:S(2)}) collective-permute-start(bf16[64,1152]{1,0:T(8,128)(2,1)S(1)} %get-tuple-element.140), channel_id=1, source_target_pairs={{0,1},{1,128},{128,129},{129,0},{2,3},{3,130},{130,131},{131,2},{4... | collective-permute-start | bytes 442376 | tf_op jit(solution)/shard_map/ppermute | solution.py:315
